TPU v7x, 256 devices: a whole 4x4x8 slice. The times are simulated.
256 devices in a mesh: dp: 2 (over core), blk: 16 (over z, x_hi), head: 8 (over x_lo, y).
Axes of the slice: x: 4 (x_hi: 2, x_lo: 2; x = x_hi * 2 + x_lo), y: 4, z: 8, core: 2. Of those that a mesh axis runs over, the one named last changes fastest.
Arguments:
- queries: bfloat16 [16384, 5120], P(('dp', 'blk'), 'head'), parts along dimension 0, may hold values from -20 to 20, as said below
- keys: bfloat16 [16384, 5120], P(('dp', 'blk'), 'head'), parts along dimension 0, may hold values from -20 to 20
- values: bfloat16 [16384, 5120], P(('dp', 'blk'), 'head'), parts along dimension 0, may hold values from -6 to 6
- block_list: int32 [128, 16], P(('dp', 'blk')), parts along dimension 0, may hold values from 0 to 63, as said below
- block_count: int32 [128], P(('dp', 'blk')), parts along dimension 0, may hold values from 4 to 16, as said below
- out_weight: bfloat16 [5120, 5120], P('head'), may hold values from -0.25 to 0.25
Outputs:
- projected: bfloat16 [16384, 5120], P(('dp', 'blk', 'head')), parts along dimension 0
There are 2 independent parts, one for each index of `dp`. A program takes and returns all parts, laid end to end along the dimension named above; an argument that names none is the same for every part. Nothing has to cross between parts.
Inputs may be any that keep to these rules, and one draw needn't show every extreme that they name: `block_list`: each row names 16 different key blocks of the same clip; its first entry is the query block itself; only the first block_count entries of a row are used. `block_count`: some query block uses all 16 entries in every draw. `queries`: query entries lie in the stated range.
All inputs are finite; a program needn't handle non-finite values.
Results may differ from a plain program's by a relative error of at most 0.02.
Values may be sent and summed in bfloat16 or wider, within the bound.
No kernel may reach another device: no remote copies, remote signals or barrier semaphores. Data moves between devices by JAX's collectives and lax.ppermute only.
A program may use at most 128 MiB of HBM per device.

v0:
```python
import math

import jax
import jax.numpy as jnp
from jax import lax
from jax.sharding import PartitionSpec as P

HD = 128
BS = 128
KB = 16


def on_device(queries, keys, values, block_list, block_count, out_weight):
    tok_rows, feature_width = queries.shape
    head_count = feature_width // HD
    query_blocks = tok_rows // BS
    block_total = tok_rows * lax.axis_size("blk") // BS
    score_scale = 1.0 / math.sqrt(HD)
    query_heads = queries.reshape(tok_rows, head_count, HD)
    block_range = jnp.arange(block_total, dtype=jnp.int32)
    listed = jnp.arange(KB, dtype=jnp.int32)[None, :] < block_count[:, None]
    matches = listed[:, :, None] & (block_list[:, :, None] == block_range[None, None, :])
    allowed = jnp.sum(jnp.where(matches, 1.0, 0.0), axis=1).astype(jnp.float32)

    def attend(state_in, key_piece, value_piece, row_start):
        running, totals, summed = state_in
        row_count = key_piece.shape[0]
        piece_blocks = (row_start + jnp.arange(row_count, dtype=jnp.int32)) // BS
        onehot = jnp.where(piece_blocks[:, None] == block_range[None, :], 1.0, 0.0).astype(
            jnp.float32
        )
        columns = jnp.einsum("bn,pn->bp", allowed, onehot)
        visible = jnp.broadcast_to(
            columns[:, None, :] > 0.5, (query_blocks, BS, row_count)
        ).reshape(tok_rows, row_count)
        scores = (
            jnp.einsum(
                "qhd,khd->hqk",
                query_heads,
                key_piece.reshape(row_count, head_count, HD),
                preferred_element_type=jnp.float32,
            )
            * score_scale
        )
        scores = jnp.where(visible[None], scores, -jnp.inf)
        highest = jnp.maximum(running, jnp.max(scores, axis=-1))
        weights = jnp.where(visible[None], jnp.exp(scores - highest[:, :, None]), 0.0)
        rescale = jnp.exp(running - highest)
        totals = totals * rescale + jnp.sum(weights, axis=-1)
        update = jnp.einsum(
            "hqk,khd->qhd",
            weights.astype(jnp.bfloat16),
            value_piece.reshape(row_count, head_count, HD),
            preferred_element_type=jnp.float32,
        )
        summed = summed * jnp.transpose(rescale)[:, :, None] + update
        return (highest, totals, summed)

    initial = (
        jnp.full((head_count, tok_rows), -1e30, jnp.float32),
        jnp.zeros((head_count, tok_rows), jnp.float32),
        jnp.zeros((tok_rows, head_count, HD), jnp.float32),
    )
    key_piece = lax.all_gather(keys, "blk", axis=0, tiled=True)
    value_piece = lax.all_gather(values, "blk", axis=0, tiled=True)
    row_count = key_piece.shape[0]
    sub_rows = 512
    key_split = key_piece.reshape(row_count // sub_rows, sub_rows, feature_width)
    value_split = value_piece.reshape(row_count // sub_rows, sub_rows, feature_width)
    offsets = sub_rows * jnp.arange(row_count // sub_rows, dtype=jnp.int32)

    def advance(inner_state, packed):
        key_sub, value_sub, offset_now = packed
        return (attend(inner_state, key_sub, value_sub, offset_now), None)

    finished, unused = lax.scan(advance, initial, (key_split, value_split, offsets))
    running, totals, summed = finished
    attended = (
        (summed / jnp.transpose(totals)[:, :, None])
        .astype(jnp.bfloat16)
        .reshape(tok_rows, feature_width)
    )
    return lax.psum_scatter(
        jnp.dot(attended, out_weight, preferred_element_type=jnp.float32).astype(jnp.bfloat16),
        "head",
        scatter_dimension=0,
        tiled=True,
    )


def solution(mesh):
    placed = (
        P(("dp", "blk"), "head"),
        P(("dp", "blk"), "head"),
        P(("dp", "blk"), "head"),
        P(("dp", "blk"), None),
        P(("dp", "blk")),
        P("head", None),
    )
    return jax.shard_map(
        on_device,
        mesh=mesh,
        in_specs=placed,
        out_specs=P(("dp", "blk", "head"), None),
        check_vma=False,
    )
```

profile of v0, /device:TPU:122, one launch (start us, length us, event | category | flops | bytes accessed | tf_op | source)
XLA Modules:
  0.0 655.3 jit_solution(10925951334080078393)
XLA Ops:
  11.3 155.7 %all-gather.3.cloned.1.call-done = bf16[8192,640]{1,0:T(8,128)(2,1)} async-done(((bf16[512,640]{1,0:T(8,128)(2,1)}), bf16[8192,640]{1,0:T(8,128)(2,1)}) %all-gather.3.cloned.1.call-update) | async-done | bytes 10485776 | tf_op jit(solution)/shard_map/all_gather | solution.py:64
  166.9 156.2 %all-gather.5.cloned.1.call-done = bf16[8192,640]{1,0:T(8,128)(2,1)} async-done(((bf16[512,640]{1,0:T(8,128)(2,1)}), bf16[8192,640]{1,0:T(8,128)(2,1)}) %all-gather.5.cloned.1.call-update) | async-done | bytes 10485776 | tf_op jit(solution)/shard_map/all_gather | solution.py:65
  323.2 254.1 %while.17 = (s32[]{:T(128)}, f32[5,512]{1,0:T(8,128)S(1)}, f32[5,512]{1,0:T(8,128)S(1)}, f32[512,5,128]{0,2,1:T(8,128)}, s32[16]{0:T(128)S(1)}, /*index=5*/bf16[...) while((s32[]{:T(128)}, f32[5,512]{1,0:T(8,128)S(1)}, ...), condition=%wide.region_4.5_spmd.clone, body=%wide.region_1.4_spmd.clone.sunk | while | flops 689464320 | bytes 43037372 | solution.py:76
  324.8 1.6 broadcast_in_dim.150
  328.3 3.4 fusion.55
  332.0 5.3 fusion.59
  340.4 1.6 broadcast_in_dim.150
  343.8 3.4 fusion.55
  347.5 5.7 fusion.59
  356.3 1.6 broadcast_in_dim.150
  359.7 3.5 fusion.55
  363.4 5.7 fusion.59
  372.2 1.6 broadcast_in_dim.150
  375.6 3.4 fusion.55
  379.3 5.7 fusion.59
  388.1 1.6 broadcast_in_dim.150
  391.5 3.5 fusion.55
  395.2 5.7 fusion.59
  404.0 1.6 broadcast_in_dim.150
  407.4 3.4 fusion.55
  411.1 5.7 fusion.59
  419.9 1.6 broadcast_in_dim.150
  423.3 3.5 fusion.55
  427.1 5.7 fusion.59
  435.8 1.6 broadcast_in_dim.150
  439.2 3.4 fusion.55
  443.0 5.7 fusion.59
  451.7 1.6 broadcast_in_dim.150
  455.1 3.5 fusion.55
  458.9 5.7 fusion.59
  471.0 3.4 fusion.55
  474.8 5.7 fusion.59
  483.5 1.6 broadcast_in_dim.150
  486.9 3.5 fusion.55
  490.7 5.7 fusion.59
  502.9 3.4 fusion.55
  506.6 5.7 fusion.59
  518.8 3.5 fusion.55
  522.5 5.7 fusion.59
  531.2 1.6 broadcast_in_dim.150
  534.7 3.4 fusion.55
  538.4 5.7 fusion.59
  550.6 3.5 fusion.55
  554.3 5.7 fusion.59
  566.5 3.4 fusion.55
  570.2 5.7 fusion.59
  578.8 8.9 %convolution_convert_fusion = bf16[512,5120]{1,0:T(8,128)(2,1)} fusion(bf16[512,640]{0,1:T(8,128)(2,1)S(1)} %bitcast.84, bf16[640,5120]{1,0:T(8,128)(2,1)} %param.13), kind=kOutput, calls=%fused_computation.40 | convolution fusion | flops 3358064640 | bytes 12451840 | tf_op jit(solution)/shard_map/dot_general | solution.py:84
  587.7 61.1 %reduce-scatter.2.cloned.1.call-done = bf16[64,5120]{1,0:T(8,128)(2,1)} async-done(((bf16[512,5120]{1,0:T(8,128)(2,1)}), bf16[64,5120]{1,0:T(8,128)(2,1)}) %reduce-scatter.2.cloned.1.call-update) | async-done | bytes 655376 | tf_op jit(solution)/shard_map/reduce_scatter | solution.py:83
  (292 shorter events, 94.7 us)
Async XLA Ops:
  6.5 160.4 %all-gather.3.cloned.1.call-start = ((), (), s32[]{:S(2)}) async-start(), calls=%async_computation.1 | async-start | bytes 11141120 | tf_op jit(solution)/shard_map/all_gather | solution.py:64
  7.3 315.9 %all-gather.5.cloned.1.call-start = ((), (), s32[]{:S(2)}) async-start(), calls=%async_computation.2 | async-start | bytes 11141120 | tf_op jit(solution)/shard_map/all_gather | solution.py:65
  8.0 640.8 %reduce-scatter.2.cloned.1.call-start = ((), (), s32[]{:S(2)}) async-start(), calls=%async_computation.3 | async-start | bytes 5898240 | tf_op jit(solution)/shard_map/reduce_scatter | solution.py:83
  331.7 5.6 slice-start
  332.0 5.4 slice-start.1
  347.2 6.0 slice-start
  347.5 5.7 slice-start.1
  363.1 6.0 slice-start
  363.4 5.7 slice-start.1
  379.0 6.0 slice-start
  379.3 5.7 slice-start.1
  395.0 6.0 slice-start
  395.2 5.7 slice-start.1
  410.9 6.0 slice-start
  411.1 5.7 slice-start.1
  426.8 6.0 slice-start
  427.0 5.7 slice-start.1
  442.7 6.0 slice-start
  442.9 5.7 slice-start.1
  458.6 6.0 slice-start
  458.9 5.7 slice-start.1
  474.5 6.0 slice-start
  474.8 5.7 slice-start.1
  490.4 6.0 slice-start
  490.7 5.7 slice-start.1
  506.3 6.0 slice-start
  506.6 5.7 slice-start.1
  522.2 6.0 slice-start
  522.5 5.7 slice-start.1
  538.1 6.0 slice-start
  538.4 5.7 slice-start.1
  554.0 6.0 slice-start
  554.3 5.7 slice-start.1
  569.9 6.0 slice-start
  570.2 5.7 slice-start.1
Sparse Core Ops, SparseCore 0:
  9.9 156.9 all-gather.2
  169.5 153.6 all-gather.4
  587.8 60.9 reduce-scatter.1
where the time goes:
time: 661 us; the launch traced here: 655 us
  waiting for transfers between devices  374 us (57%)
  matrix products  159 us (24%)
  local copies, waits for them, and re-layouts  72.9 us (11%)
  other arithmetic  33.8 us (5%)
  between operations  13.2 us (2%)
    all_gather x1, waiting for transfers between devices, on_device(): value_piece = lax.all_gather(values, 'blk', axis=0, tiled=True)  156 us
    all_gather x1, waiting for transfers between devices, on_device(): key_piece = lax.all_gather(keys, 'blk', axis=0, tiled=True)  156 us
    dot_general x16, matrix products, attend(): jnp.einsum('hqk,khd->qhd', weights.astype(jnp.bfloat16), value_piece.resh...  91.3 us
    reduce_scatter x1, waiting for transfers between devices, on_device(): lax.psum_scatter(jnp.dot(attended, out_weight, preferred_element_type=jnp...  61.1 us
    dot_general x16, matrix products, attend(): jnp.einsum('qhd,khd->hqk', query_heads, key_piece.reshape(row_count, head...  55.1 us
    dynamic_slice x64, local copies, waits for them, and re-layouts, on_device(): lax.scan(advance, initial, (key_split, value_split, offsets))  40.1 us
    broadcast_in_dim x16, local copies, waits for them, and re-layouts, attend(): jnp.broadcast_to(columns[:, None, :] > 0.5, (query_blocks, BS, row_count))  25.6 us
    reduce_sum x16, other arithmetic, attend(): totals = totals * rescale + jnp.sum(weights, axis=-1)  20.3 us
  transfers between devices with their start and end apart: 3, of which 3 were waited for; matrix products, arithmetic and copies ran while one was open for 0% of the time, Pallas kernels for 0%

commit v1 on v0

v1 whole, which is shorter than its diff:
```python
import math

import jax
import jax.numpy as jnp
from jax import lax
from jax.experimental import pallas as pl
from jax.experimental.pallas import tpu as pltpu
from jax.sharding import PartitionSpec as P

HD = 128
BS = 128
KB = 16
TAB = 16
GROUP = 4
NZ = 8
NX = 2
NY = 4
LEVELS = ((0, 2, 3, 5, 6), (1, 3, 4, 6, 7))
SERVED = tuple(tuple(lv.index(z) if z in lv else -1 for z in range(NZ)) for lv in LEVELS)
BOTH = ("blk", "head")


def flat(z, xh, head):
    return (z * NX + xh) * 2 * NY + head


def pairs(shift):
    out = []
    for head in range(2 * NY):
        for z in range(NZ):
            to = (z + shift) % NZ
            if SERVED[head // NY][to] >= 0:
                for xh in range(NX):
                    out.append((flat(z, xh, head), flat(to, xh, head)))
    return out


def swap_pairs():
    out = []
    for head in range(2 * NY):
        for z in LEVELS[head // NY]:
            for xh in range(NX):
                out.append((flat(z, xh, head), flat(z, 1 - xh, head)))
    return out


def attend_kernel(lists, counts, *refs):
    own = refs[:NZ]
    other = refs[NZ : 2 * NZ]
    out = refs[2 * NZ]
    kbuf, vbuf, qbuf, sbuf, sems = refs[2 * NZ + 1 :]
    rows = out.shape[0] // NZ
    factor = math.log2(math.e) / math.sqrt(HD)

    copies = []
    for s in range(NZ):
        for src, dst, i in (
            (own[s].at[pl.ds(0 * rows, rows)], kbuf.at[pl.ds(s * rows, rows)], 0),
            (own[s].at[pl.ds(1 * rows, rows)], vbuf.at[pl.ds(s * rows, rows)], 1),
            (own[s].at[pl.ds(2 * rows, rows)], qbuf.at[pl.ds(s * rows, rows)], 2),
            (other[s].at[pl.ds(0 * rows, rows)], kbuf.at[pl.ds((NZ + s) * rows, rows)], 3),
            (other[s].at[pl.ds(1 * rows, rows)], vbuf.at[pl.ds((NZ + s) * rows, rows)], 4),
        ):
            copies.append(pltpu.make_async_copy(src, dst, sems.at[s, i]))
    for c in copies:
        c.start()
    for c in copies:
        c.wait()

    def gather(buf, qb, g):
        parts = []
        for j in range(GROUP):
            at = pl.multiple_of(lists[qb * KB + g * GROUP + j] * BS, BS)
            parts.append(buf[pl.ds(at, BS), :])
        return jnp.concatenate(parts, axis=0)

    def branch(qb, n, groups):
        q = qbuf[pl.ds(pl.multiple_of(qb * BS, BS), BS), :]
        high = None
        for g in range(groups):
            s = lax.dot_general(
                q, gather(kbuf, qb, g), (((1,), (1,)), ((), ())), preferred_element_type=jnp.float32
            )
            if g == groups - 1:
                lane = lax.broadcasted_iota(jnp.int32, s.shape, 1)
                s = jnp.where(lane < (n - g * GROUP) * BS, s, -1e30)
            sbuf[:, g * GROUP * BS : (g + 1) * GROUP * BS] = s
            for j in range(GROUP):
                t = s[:, j * BS : (j + 1) * BS]
                high = t if high is None else jnp.maximum(high, t)
        m = jnp.max(high, axis=-1, keepdims=True)
        acc = None
        tot = None
        for g in range(groups):
            p = jnp.exp2((sbuf[:, g * GROUP * BS : (g + 1) * GROUP * BS] - m) * factor)
            for j in range(GROUP):
                t = p[:, j * BS : (j + 1) * BS]
                tot = t if tot is None else tot + t
            part = jnp.dot(
                p.astype(jnp.bfloat16), gather(vbuf, qb, g), preferred_element_type=jnp.float32
            )
            acc = part if acc is None else acc + part
        total = jnp.sum(tot, axis=-1, keepdims=True)
        out[pl.ds(pl.multiple_of(qb * BS, BS), BS), :] = (acc / total).astype(out.dtype)

    def step(qb, carry):
        n = counts[qb]
        for groups in range(1, KB // GROUP + 1):

            @pl.when((n > (groups - 1) * GROUP) & (n <= groups * GROUP))
            def _():
                branch(qb, n, groups)

        return carry

    lax.fori_loop(0, out.shape[0] // BS, step, 0)


def attend(lists, counts, own, other, rows):
    any_spec = pl.BlockSpec(memory_space=pl.ANY)
    smem = pl.BlockSpec(memory_space=pltpu.SMEM)
    return pl.pallas_call(
        attend_kernel,
        out_shape=jax.ShapeDtypeStruct((NZ * rows, HD), jnp.bfloat16),
        in_specs=[smem, smem] + [any_spec] * (2 * NZ),
        out_specs=pl.BlockSpec(memory_space=pltpu.VMEM),
        scratch_shapes=[
            pltpu.VMEM((2 * NZ * rows, HD), jnp.bfloat16),
            pltpu.VMEM((2 * NZ * rows, HD), jnp.bfloat16),
            pltpu.VMEM((NZ * rows, HD), jnp.bfloat16),
            pltpu.VMEM((BS, KB * BS), jnp.float32),
            pltpu.SemaphoreType.DMA((NZ, 5)),
        ],
        compiler_params=pltpu.CompilerParams(vmem_limit_bytes=24 << 20),
        cost_estimate=pl.CostEstimate(
            flops=32 * 8 * 4 * BS * BS * HD, bytes_accessed=6 << 20, transcendentals=32 * 8 * BS * BS
        ),
        name="attend",
    )(lists, counts, *own, *other)


def on_device(queries, keys, values, block_list, block_count, out_weight):
    rows, width = queries.shape
    heads = width // HD
    blk, head = lax.axis_index("blk"), lax.axis_index("head")
    z, xh, x_lo = blk // NX, blk % NX, head // NY
    served = jnp.asarray(SERVED, jnp.int32)[x_lo]
    levels = jnp.asarray(LEVELS, jnp.int32)[x_lo]

    table = jnp.concatenate([block_list, block_count[:, None]], axis=1).astype(jnp.bfloat16)
    table = jnp.pad(table, ((0, TAB - table.shape[0]), (0, HD - table.shape[1])))

    def payload(shift):
        at = jnp.maximum(served[(z + shift) % NZ], 0) * HD
        return jnp.concatenate(
            [lax.dynamic_slice_in_dim(a, at, HD, 1) for a in (keys, values, queries)] + [table]
        )

    own = [None] * NZ
    other = [None] * NZ
    swap = swap_pairs()
    for s in (0, 4, 3, 5, 2, 6, 1, 7):
        sent = payload(s)
        own[s] = sent if s == 0 else lax.ppermute(sent, BOTH, pairs(s))
    for s in (0, 4, 3, 5, 2, 6, 1, 7):
        other[s] = lax.ppermute(own[s][: 2 * rows], BOTH, swap)

    per = rows // BS
    table = jnp.stack([o[3 * rows : 3 * rows + per, : KB + 1] for o in own]).astype(jnp.int32)
    kblk = table[..., :KB] // per
    slot = (z - kblk // NX) % NZ + jnp.where(kblk % NX == xh, 0, NZ)
    lists = (slot * per + table[..., :KB] % per).reshape(-1)
    counts = jnp.where(served[z] >= 0, table[..., KB].reshape(-1), 0)

    mixed = attend(lists, counts, own, other, rows)
    back = []
    for s in range(NZ):
        piece = mixed[s * rows : (s + 1) * rows]
        if s:
            piece = lax.ppermute(piece, BOTH, [(b, a) for a, b in pairs(s)])
        back.append(piece)
    back = jnp.stack(back)
    attended = jnp.concatenate(
        [lax.dynamic_index_in_dim(back, (levels[h] - z) % NZ, 0, False) for h in range(heads)], axis=1
    )
    return lax.psum_scatter(
        jnp.dot(attended, out_weight, preferred_element_type=jnp.float32).astype(jnp.bfloat16),
        "head",
        scatter_dimension=0,
        tiled=True,
    )


def solution(mesh):
    placed = (
        P(("dp", "blk"), "head"),
        P(("dp", "blk"), "head"),
        P(("dp", "blk"), "head"),
        P(("dp", "blk"), None),
        P(("dp", "blk")),
        P("head", None),
    )
    return jax.shard_map(
        on_device,
        mesh=mesh,
        in_specs=placed,
        out_specs=P(("dp", "blk", "head"), None),
        check_vma=False,
    )
```

time: 661 us -> 282 us (0.43)
  the two profiles are of different devices: /device:TPU:122 before, /device:TPU:1 now
where the time goes in v1:
time: 282 us; the launch traced here: 281 us
  waiting for transfers between devices  139 us (49%)
  starting transfers between devices  66.4 us (24%)
  Pallas kernels  25.9 us (9%)
  between operations  22.9 us (8%)
  local copies, waits for them, and re-layouts  13.5 us (5%)
  matrix products  8.91 us (3%)
  other arithmetic  4.05 us (1%)
    reduce_scatter x1, waiting for transfers between devices, on_device(): lax.psum_scatter(jnp.dot(attended, out_weight, preferred_element_type=jnp...  69.3 us
    ppermute x7, waiting for transfers between devices, on_device(): own[s] = sent if s == 0 else lax.ppermute(sent, BOTH, pairs(s))  45.8 us
    ppermute x8, starting transfers between devices, on_device(): other[s] = lax.ppermute(own[s][:2 * rows], BOTH, swap)  27.9 us
    pallas_call x1, Pallas kernels, attend(): pl.pallas_call(attend_kernel, out_shape=jax.ShapeDtypeStruct((NZ * rows,...  25.9 us
    ppermute x7, starting transfers between devices, on_device(): own[s] = sent if s == 0 else lax.ppermute(sent, BOTH, pairs(s))  20.1 us
    ppermute x7, starting transfers between devices, on_device(): piece = lax.ppermute(piece, BOTH, [(b, a) for a, b in pairs(s)])  18.4 us
    ppermute x8, waiting for transfers between devices, on_device(): other[s] = lax.ppermute(own[s][:2 * rows], BOTH, swap)  15.9 us
    dot_general x1, matrix products, on_device(): jnp.dot(attended, out_weight, preferred_element_type=jnp.float32)  8.91 us
  transfers between devices with their start and end apart: 23, of which 7 were waited for; matrix products, arithmetic and copies ran while one was open for 2% of the time, Pallas kernels for 0%

profile of v1, /device:TPU:1, one launch (start us, length us, event | category | flops | bytes accessed | tf_op | source)
XLA Modules:
  0.0 280.7 jit_solution(4651338255492431501)
XLA Ops:
  6.5 1.7 fusion.17
  13.3 0.7 convert_bitcast_fusion
  14.0 0.7 convert.11
  14.7 1.4 constant_dynamic-slice_fusion.3
  16.1 1.9 constant_dynamic-slice_fusion.1
  18.1 1.0 pad_maximum_fusion
  19.1 5.7 %collective-permute-start.1 = (bf16[1552,128]{1,0:T(8,128)(2,1)}, bf16[1552,128]{1,0:T(8,128)(2,1)S(1)}, u32[]{:S(2)}, u32[]{:S(2)}) collective-permute-start(bf16[1552,128]{1,0:T(8,128)(2,1)} %get-tuple-element.37), channel_id=1, source_target_pairs={{0,32},{8,40},{16,48},{24,56},{48,80},{56,88},{64,96},{72,104},{96... | collective-permute-start | bytes 1191944 | tf_op jit(solution)/shard_map/ppermute | solution.py:164
  24.8 1.2 pad_maximum_fusion.1
  25.9 1.3 collective-permute-start
  27.2 6.6 %collective-permute-start.2 = (bf16[1552,128]{1,0:T(8,128)(2,1)}, bf16[1552,128]{1,0:T(8,128)(2,1)S(1)}, u32[]{:S(2)}, u32[]{:S(2)}) collective-permute-start(bf16[1552,128]{1,0:T(8,128)(2,1)} %get-tuple-element.38), channel_id=1, source_target_pairs={{0,48},{8,56},{32,80},{40,88},{48,96},{56,104},{80,0},{88,8},{112,... | collective-permute-start | bytes 1191944 | tf_op jit(solution)/shard_map/ppermute | solution.py:164
  33.8 1.3 collective-permute-start.3
  35.1 2.1 collective-permute-start.4
  37.4 0.7 fusion.18
  42.1 22.5 %collective-permute-done.2.refs_3_ = bf16[1552,128]{1,0:T(8,128)(2,1)S(1)} collective-permute-done((bf16[1552,128]{1,0:T(8,128)(2,1)}, bf16[1552,128]{1,0:T(8,128)(2,1)S(1)}, u32[]{:S(2)}, u32[]{:S(2)}) %collective-permute-start.2) | collective-permute-done | bytes 397344 | tf_op jit(solution)/shard_map/ppermute | solution.py:164
  64.6 1.9 collective-permute-start.5
  66.6 23.2 %collective-permute-done.3.refs_4_ = bf16[1552,128]{1,0:T(8,128)(2,1)S(1)} collective-permute-done((bf16[1552,128]{1,0:T(8,128)(2,1)S(1)}, bf16[1552,128]{1,0:T(8,128)(2,1)S(1)}, u32[]{:S(2)}, u32[]{:S(2)}) %collective-permute-start.3) | collective-permute-done | bytes 397344 | tf_op jit(solution)/shard_map/ppermute | solution.py:164
  89.8 1.3 collective-permute-start.6
  91.1 4.7 %collective-permute-start.7 = (bf16[1024,128]{1,0:T(8,128)(2,1)S(1)}, bf16[1024,128]{1,0:T(8,128)(2,1)S(1)}, u32[]{:S(2)}, u32[]{:S(2)}) collective-permute-start(bf16[1024,128]{1,0:T(8,128)(2,1)S(1)} %pad_maximum_fusion.8), channel_id=1, source_target_pairs={{0,8},{8,0},{32,40},{40,32},{48,56},{56,48},{80,88},{88,80},{96,10... | collective-permute-start | bytes 786440 | tf_op jit(solution)/shard_map/ppermute | solution.py:166
  95.8 2.1 collective-permute-start.10
  98.0 4.7 %collective-permute-start.11 = (bf16[1024,128]{1,0:T(8,128)(2,1)S(1)}, bf16[1024,128]{1,0:T(8,128)(2,1)S(1)}, u32[]{:S(2)}, u32[]{:S(2)}) collective-permute-start(bf16[1024,128]{1,0:T(8,128)(2,1)S(1)} %slice.137), channel_id=1, source_target_pairs={{0,8},{8,0},{32,40},{40,32},{48,56},{56,48},{80,88},{88,80},{96,10... | collective-permute-start | bytes 786440 | tf_op jit(solution)/shard_map/ppermute | solution.py:166
  102.7 0.7 slice.135
  103.5 3.0 %collective-permute-start.9 = (bf16[1024,128]{1,0:T(8,128)(2,1)}, bf16[1024,128]{1,0:T(8,128)(2,1)}, u32[]{:S(2)}, u32[]{:S(2)}) collective-permute-start(bf16[1024,128]{1,0:T(8,128)(2,1)} %slice.135), channel_id=1, source_target_pairs={{0,8},{8,0},{32,40},{40,32},{48,56},{56,48},{80,88},{88,80},{96,10... | collective-permute-start | bytes 786440 | tf_op jit(solution)/shard_map/ppermute | solution.py:166
  106.4 0.8 slice.138
  107.2 3.8 %collective-permute-start.12 = (bf16[1024,128]{1,0:T(8,128)(2,1)}, bf16[1024,128]{1,0:T(8,128)(2,1)}, u32[]{:S(2)}, u32[]{:S(2)}) collective-permute-start(bf16[1024,128]{1,0:T(8,128)(2,1)} %slice.138), channel_id=1, source_target_pairs={{0,8},{8,0},{32,40},{40,32},{48,56},{56,48},{80,88},{88,80},{96,10... | collective-permute-start | bytes 786440 | tf_op jit(solution)/shard_map/ppermute | solution.py:166
  111.0 0.7 slice.139
  111.7 0.7 slice.140
  112.5 0.7 slice.134
  113.2 3.0 %collective-permute-start.13 = (bf16[1024,128]{1,0:T(8,128)(2,1)}, bf16[1024,128]{1,0:T(8,128)(2,1)}, u32[]{:S(2)}, u32[]{:S(2)}) collective-permute-start(bf16[1024,128]{1,0:T(8,128)(2,1)} %slice.139), channel_id=1, source_target_pairs={{0,8},{8,0},{32,40},{40,32},{48,56},{56,48},{80,88},{88,80},{96,10... | collective-permute-start | bytes 786440 | tf_op jit(solution)/shard_map/ppermute | solution.py:166
  116.2 0.7 copy-done
  116.9 3.8 %collective-permute-start.14 = (bf16[1024,128]{1,0:T(8,128)(2,1)}, bf16[1024,128]{1,0:T(8,128)(2,1)}, u32[]{:S(2)}, u32[]{:S(2)}) collective-permute-start(bf16[1024,128]{1,0:T(8,128)(2,1)} %slice.140), channel_id=1, source_target_pairs={{0,8},{8,0},{32,40},{40,32},{48,56},{56,48},{80,88},{88,80},{96,10... | collective-permute-start | bytes 786440 | tf_op jit(solution)/shard_map/ppermute | solution.py:166
  120.7 0.7 copy-done.2
  121.4 3.0 %collective-permute-start.8 = (bf16[1024,128]{1,0:T(8,128)(2,1)}, bf16[1024,128]{1,0:T(8,128)(2,1)}, u32[]{:S(2)}, u32[]{:S(2)}) collective-permute-start(bf16[1024,128]{1,0:T(8,128)(2,1)} %slice.134), channel_id=1, source_target_pairs={{0,8},{8,0},{32,40},{40,32},{48,56},{56,48},{80,88},{88,80},{96,10... | collective-permute-start | bytes 786440 | tf_op jit(solution)/shard_map/ppermute | solution.py:166
  124.9 4.7 %collective-permute-done.13.refs_14_ = bf16[1024,128]{1,0:T(8,128)(2,1)} collective-permute-done((bf16[1024,128]{1,0:T(8,128)(2,1)}, bf16[1024,128]{1,0:T(8,128)(2,1)}, u32[]{:S(2)}, u32[]{:S(2)}) %collective-permute-start.13) | collective-permute-done | bytes 262176 | tf_op jit(solution)/shard_map/ppermute | solution.py:166
  129.6 5.6 %collective-permute-done.14.refs_15_ = bf16[1024,128]{1,0:T(8,128)(2,1)} collective-permute-done((bf16[1024,128]{1,0:T(8,128)(2,1)}, bf16[1024,128]{1,0:T(8,128)(2,1)}, u32[]{:S(2)}, u32[]{:S(2)}) %collective-permute-start.14) | collective-permute-done | bytes 262176 | tf_op jit(solution)/shard_map/ppermute | solution.py:166
  135.3 5.6 %collective-permute-done.8.refs_9_ = bf16[1024,128]{1,0:T(8,128)(2,1)} collective-permute-done((bf16[1024,128]{1,0:T(8,128)(2,1)}, bf16[1024,128]{1,0:T(8,128)(2,1)}, u32[]{:S(2)}, u32[]{:S(2)}) %collective-permute-start.8) | collective-permute-done | bytes 262176 | tf_op jit(solution)/shard_map/ppermute | solution.py:166
  140.9 0.9 copy-done.1
  141.8 0.9 copy-done.3
  142.8 25.9 %attend.1 = bf16[4096,128]{1,0:T(8,128)(2,1)S(1)} custom-call(s32[512]{0:T(512)S(1)} %reshape.100.lists, s32[32]{0:T(128)S(1)} %select_n.252.counts, bf16[1552,128]{1,0:T(8,128)(2,1)S(1)} %get-tuple-element.36.refs_0_, bf16[1552,128]{1,0:T(8,128)(2,1)S(1)} %collective-permute-done.refs_1_, bf16[1552,128]{1,0:T(8,128)(2,1)S(1)} %collective-permute-done.1.refs_2_, ...), custom_call_target="tpu_custom_call" | custom-call | flops 2147483648 | bytes 6291456 | tf_op jit(solution)/shard_map/attend/pallas_call | solution.py:122
  168.8 1.3 collective-permute-start.15
  170.1 1.9 collective-permute-start.16
  172.0 2.8 %collective-permute-start.17 = (bf16[512,128]{1,0:T(8,128)(2,1)S(1)}, bf16[512,128]{1,0:T(8,128)(2,1)S(1)}, u32[]{:S(2)}, u32[]{:S(2)}) collective-permute-start(bf16[512,128]{1,0:T(8,128)(2,1)S(1)} %get-tuple-element.9), channel_id=1, source_target_pairs={{48,0},{56,8},{80,32},{88,40},{96,48},{104,56},{0,80},{8,88},{32,1... | collective-permute-start | bytes 393224 | tf_op jit(solution)/shard_map/ppermute | solution.py:180
  174.8 1.3 collective-permute-start.18
  176.1 4.2 %collective-permute-start.19 = (bf16[512,128]{1,0:T(8,128)(2,1)S(1)}, bf16[512,128]{1,0:T(8,128)(2,1)S(1)}, u32[]{:S(2)}, u32[]{:S(2)}) collective-permute-start(bf16[512,128]{1,0:T(8,128)(2,1)S(1)} %get-tuple-element.7), channel_id=1, source_target_pairs={{80,0},{88,8},{96,16},{104,24},{0,48},{8,56},{32,80},{40,88},{48,9... | collective-permute-start | bytes 393224 | tf_op jit(solution)/shard_map/ppermute | solution.py:180
  180.4 5.5 %collective-permute-start.20 = (bf16[512,128]{1,0:T(8,128)(2,1)S(1)}, bf16[512,128]{1,0:T(8,128)(2,1)S(1)}, u32[]{:S(2)}, u32[]{:S(2)}) collective-permute-start(bf16[512,128]{1,0:T(8,128)(2,1)S(1)} %get-tuple-element.6), channel_id=1, source_target_pairs={{96,0},{104,8},{0,32},{8,40},{32,64},{40,72},{48,80},{56,88},{80,1... | collective-permute-start | bytes 393224 | tf_op jit(solution)/shard_map/ppermute | solution.py:180
  185.9 1.3 collective-permute-start.21
  187.4 7.9 %collective-permute-done.20 = bf16[512,128]{1,0:T(8,128)(2,1)S(1)} collective-permute-done((bf16[512,128]{1,0:T(8,128)(2,1)S(1)}, bf16[512,128]{1,0:T(8,128)(2,1)S(1)}, u32[]{:S(2)}, u32[]{:S(2)}) %collective-permute-start.20) | collective-permute-done | bytes 131104 | tf_op jit(solution)/shard_map/ppermute | solution.py:180
  195.6 8.9 %convolution_convert_fusion = bf16[512,5120]{1,0:T(8,128)(2,1)} fusion(bf16[512,640]{1,0:T(8,128)(2,1)S(1)} %bitcast_dynamic-update-slice_fusion, bf16[640,5120]{1,0:T(8,128)(2,1)} %param.13), kind=kOutput, calls=%fused_computation | convolution fusion | flops 3358064640 | bytes 12451840 | tf_op jit(solution)/shard_map/dot_general | solution.py:187
  204.5 69.3 %reduce-scatter.2.cloned.1.call-done = bf16[64,5120]{1,0:T(8,128)(2,1)} async-done(((bf16[512,5120]{1,0:T(8,128)(2,1)}), bf16[64,5120]{1,0:T(8,128)(2,1)}) %reduce-scatter.2.cloned.1.call-update) | async-done | bytes 655376 | tf_op jit(solution)/shard_map/reduce_scatter | solution.py:186
  (61 shorter events, 1.5 us)
Async XLA Ops:
  6.5 267.3 %reduce-scatter.2.cloned.1.call-start = ((), (), s32[]{:S(2)}) async-start(), calls=%async_computation.1 | async-start | bytes 5898240 | tf_op jit(solution)/shard_map/reduce_scatter | solution.py:186
  6.5 30.7 %copy-start.4 = (s32[4,16]{1,0:T(4,128)S(1)}, s32[4,16]{1,0:T(4,128)}, u32[]{:S(2)}) copy-start(s32[4,16]{1,0:T(4,128)} %param.11) | copy-start | bytes 772
  6.5 30.7 %copy-start.5 = (s32[2,5]{1,0:T(2,128)S(1)}, s32[2,5]{1,0:T(2,128)}, u32[]{:S(2)}) copy-start(s32[2,5]{1,0:T(2,128)} %constant.288.clone) | copy-start | bytes 124
  19.1 76.8 %collective-permute-start.1 = (bf16[1552,128]{1,0:T(8,128)(2,1)}, bf16[1552,128]{1,0:T(8,128)(2,1)S(1)}, u32[]{:S(2)}, u32[]{:S(2)}) collective-permute-start(bf16[1552,128]{1,0:T(8,128)(2,1)} %get-tuple-element.37), channel_id=1, source_target_pairs={{0,32},{8,40},{16,48},{24,56},{48,80},{56,88},{64,96},{72,104},{96... | collective-permute-start | bytes 1191944 | tf_op jit(solution)/shard_map/ppermute | solution.py:164
  25.9 65.2 %collective-permute-start = (bf16[1552,128]{1,0:T(8,128)(2,1)}, bf16[1552,128]{1,0:T(8,128)(2,1)S(1)}, u32[]{:S(2)}, u32[]{:S(2)}) collective-permute-start(bf16[1552,128]{1,0:T(8,128)(2,1)} %get-tuple-element.43), channel_id=1, source_target_pairs={{16,32},{24,40},{32,48},{40,56},{64,80},{72,88},{80,96},{88,104},{... | collective-permute-start | bytes 1191944 | tf_op jit(solution)/shard_map/ppermute | solution.py:164
  27.2 37.4 %collective-permute-start.2 = (bf16[1552,128]{1,0:T(8,128)(2,1)}, bf16[1552,128]{1,0:T(8,128)(2,1)S(1)}, u32[]{:S(2)}, u32[]{:S(2)}) collective-permute-start(bf16[1552,128]{1,0:T(8,128)(2,1)} %get-tuple-element.38), channel_id=1, source_target_pairs={{0,48},{8,56},{32,80},{40,88},{48,96},{56,104},{80,0},{88,8},{112,... | collective-permute-start | bytes 1191944 | tf_op jit(solution)/shard_map/ppermute | solution.py:164
  33.8 56.0 %collective-permute-start.3 = (bf16[1552,128]{1,0:T(8,128)(2,1)S(1)}, bf16[1552,128]{1,0:T(8,128)(2,1)S(1)}, u32[]{:S(2)}, u32[]{:S(2)}) collective-permute-start(bf16[1552,128]{1,0:T(8,128)(2,1)S(1)} %get-tuple-element.39), channel_id=1, source_target_pairs={{16,80},{24,88},{32,96},{40,104},{64,0},{72,8},{96,32},{104,40},{1... | collective-permute-start | bytes 1191944 | tf_op jit(solution)/shard_map/ppermute | solution.py:164
  35.1 62.9 %collective-permute-start.4 = (bf16[1552,128]{1,0:T(8,128)(2,1)}, bf16[1552,128]{1,0:T(8,128)(2,1)S(1)}, u32[]{:S(2)}, u32[]{:S(2)}) collective-permute-start(bf16[1552,128]{1,0:T(8,128)(2,1)} %get-tuple-element.41), channel_id=1, source_target_pairs={{0,80},{8,88},{16,96},{24,104},{48,0},{56,8},{80,32},{88,40},{96,4... | collective-permute-start | bytes 1191944 | tf_op jit(solution)/shard_map/ppermute | solution.py:164
  64.6 38.1 %collective-permute-start.5 = (bf16[1552,128]{1,0:T(8,128)(2,1)}, bf16[1552,128]{1,0:T(8,128)(2,1)S(1)}, u32[]{:S(2)}, u32[]{:S(2)}) collective-permute-start(bf16[1552,128]{1,0:T(8,128)(2,1)} %get-tuple-element.42), channel_id=1, source_target_pairs={{0,96},{8,104},{32,0},{40,8},{64,32},{72,40},{80,48},{88,56},{112,... | collective-permute-start | bytes 1191944 | tf_op jit(solution)/shard_map/ppermute | solution.py:164
  89.8 12.9 %collective-permute-start.6 = (bf16[1552,128]{1,0:T(8,128)(2,1)}, bf16[1552,128]{1,0:T(8,128)(2,1)S(1)}, u32[]{:S(2)}, u32[]{:S(2)}) collective-permute-start(bf16[1552,128]{1,0:T(8,128)(2,1)} %get-tuple-element.40), channel_id=1, source_target_pairs={{16,0},{24,8},{48,32},{56,40},{64,48},{72,56},{96,80},{104,88},{11... | collective-permute-start | bytes 1191944 | tf_op jit(solution)/shard_map/ppermute | solution.py:164
  91.1 22.0 %collective-permute-start.7 = (bf16[1024,128]{1,0:T(8,128)(2,1)S(1)}, bf16[1024,128]{1,0:T(8,128)(2,1)S(1)}, u32[]{:S(2)}, u32[]{:S(2)}) collective-permute-start(bf16[1024,128]{1,0:T(8,128)(2,1)S(1)} %pad_maximum_fusion.8), channel_id=1, source_target_pairs={{0,8},{8,0},{32,40},{40,32},{48,56},{56,48},{80,88},{88,80},{96,10... | collective-permute-start | bytes 786440 | tf_op jit(solution)/shard_map/ppermute | solution.py:166
  95.8 20.3 %collective-permute-start.10 = (bf16[1024,128]{1,0:T(8,128)(2,1)S(1)}, bf16[1024,128]{1,0:T(8,128)(2,1)S(1)}, u32[]{:S(2)}, u32[]{:S(2)}) collective-permute-start(bf16[1024,128]{1,0:T(8,128)(2,1)S(1)} %slice.136), channel_id=1, source_target_pairs={{0,8},{8,0},{32,40},{40,32},{48,56},{56,48},{80,88},{88,80},{96,10... | collective-permute-start | bytes 786440 | tf_op jit(solution)/shard_map/ppermute | solution.py:166
  98.0 22.7 %collective-permute-start.11 = (bf16[1024,128]{1,0:T(8,128)(2,1)S(1)}, bf16[1024,128]{1,0:T(8,128)(2,1)S(1)}, u32[]{:S(2)}, u32[]{:S(2)}) collective-permute-start(bf16[1024,128]{1,0:T(8,128)(2,1)S(1)} %slice.137), channel_id=1, source_target_pairs={{0,8},{8,0},{32,40},{40,32},{48,56},{56,48},{80,88},{88,80},{96,10... | collective-permute-start | bytes 786440 | tf_op jit(solution)/shard_map/ppermute | solution.py:166
  103.5 21.5 %collective-permute-start.9 = (bf16[1024,128]{1,0:T(8,128)(2,1)}, bf16[1024,128]{1,0:T(8,128)(2,1)}, u32[]{:S(2)}, u32[]{:S(2)}) collective-permute-start(bf16[1024,128]{1,0:T(8,128)(2,1)} %slice.135), channel_id=1, source_target_pairs={{0,8},{8,0},{32,40},{40,32},{48,56},{56,48},{80,88},{88,80},{96,10... | collective-permute-start | bytes 786440 | tf_op jit(solution)/shard_map/ppermute | solution.py:166
  107.2 17.7 %collective-permute-start.12 = (bf16[1024,128]{1,0:T(8,128)(2,1)}, bf16[1024,128]{1,0:T(8,128)(2,1)}, u32[]{:S(2)}, u32[]{:S(2)}) collective-permute-start(bf16[1024,128]{1,0:T(8,128)(2,1)} %slice.138), channel_id=1, source_target_pairs={{0,8},{8,0},{32,40},{40,32},{48,56},{56,48},{80,88},{88,80},{96,10... | collective-permute-start | bytes 786440 | tf_op jit(solution)/shard_map/ppermute | solution.py:166
  113.2 16.5 %collective-permute-start.13 = (bf16[1024,128]{1,0:T(8,128)(2,1)}, bf16[1024,128]{1,0:T(8,128)(2,1)}, u32[]{:S(2)}, u32[]{:S(2)}) collective-permute-start(bf16[1024,128]{1,0:T(8,128)(2,1)} %slice.139), channel_id=1, source_target_pairs={{0,8},{8,0},{32,40},{40,32},{48,56},{56,48},{80,88},{88,80},{96,10... | collective-permute-start | bytes 786440 | tf_op jit(solution)/shard_map/ppermute | solution.py:166
  116.2 0.7 copy-start
  116.9 18.4 %collective-permute-start.14 = (bf16[1024,128]{1,0:T(8,128)(2,1)}, bf16[1024,128]{1,0:T(8,128)(2,1)}, u32[]{:S(2)}, u32[]{:S(2)}) collective-permute-start(bf16[1024,128]{1,0:T(8,128)(2,1)} %slice.140), channel_id=1, source_target_pairs={{0,8},{8,0},{32,40},{40,32},{48,56},{56,48},{80,88},{88,80},{96,10... | collective-permute-start | bytes 786440 | tf_op jit(solution)/shard_map/ppermute | solution.py:166
  120.7 0.7 copy-start.2
  121.4 19.5 %collective-permute-start.8 = (bf16[1024,128]{1,0:T(8,128)(2,1)}, bf16[1024,128]{1,0:T(8,128)(2,1)}, u32[]{:S(2)}, u32[]{:S(2)}) collective-permute-start(bf16[1024,128]{1,0:T(8,128)(2,1)} %slice.134), channel_id=1, source_target_pairs={{0,8},{8,0},{32,40},{40,32},{48,56},{56,48},{80,88},{88,80},{96,10... | collective-permute-start | bytes 786440 | tf_op jit(solution)/shard_map/ppermute | solution.py:166
  140.9 1.0 copy-start.1
  141.8 0.9 copy-start.3
  168.8 11.7 %collective-permute-start.15 = (bf16[512,128]{1,0:T(8,128)(2,1)S(1)}, bf16[512,128]{1,0:T(8,128)(2,1)S(1)}, u32[]{:S(2)}, u32[]{:S(2)}) collective-permute-start(bf16[512,128]{1,0:T(8,128)(2,1)S(1)} %get-tuple-element.11), channel_id=1, source_target_pairs={{32,16},{40,24},{48,32},{56,40},{80,64},{88,72},{96,80},{104,88},{... | collective-permute-start | bytes 393224 | tf_op jit(solution)/shard_map/ppermute | solution.py:180
  170.1 15.9 %collective-permute-start.16 = (bf16[512,128]{1,0:T(8,128)(2,1)S(1)}, bf16[512,128]{1,0:T(8,128)(2,1)S(1)}, u32[]{:S(2)}, u32[]{:S(2)}) collective-permute-start(bf16[512,128]{1,0:T(8,128)(2,1)S(1)} %get-tuple-element.10), channel_id=1, source_target_pairs={{32,0},{40,8},{48,16},{56,24},{80,48},{88,56},{96,64},{104,72},{0,... | collective-permute-start | bytes 393224 | tf_op jit(solution)/shard_map/ppermute | solution.py:180
  172.0 15.3 %collective-permute-start.17 = (bf16[512,128]{1,0:T(8,128)(2,1)S(1)}, bf16[512,128]{1,0:T(8,128)(2,1)S(1)}, u32[]{:S(2)}, u32[]{:S(2)}) collective-permute-start(bf16[512,128]{1,0:T(8,128)(2,1)S(1)} %get-tuple-element.9), channel_id=1, source_target_pairs={{48,0},{56,8},{80,32},{88,40},{96,48},{104,56},{0,80},{8,88},{32,1... | collective-permute-start | bytes 393224 | tf_op jit(solution)/shard_map/ppermute | solution.py:180
  174.8 12.5 %collective-permute-start.18 = (bf16[512,128]{1,0:T(8,128)(2,1)S(1)}, bf16[512,128]{1,0:T(8,128)(2,1)S(1)}, u32[]{:S(2)}, u32[]{:S(2)}) collective-permute-start(bf16[512,128]{1,0:T(8,128)(2,1)S(1)} %get-tuple-element.8), channel_id=1, source_target_pairs={{80,16},{88,24},{96,32},{104,40},{0,64},{8,72},{32,96},{40,104},{4... | collective-permute-start | bytes 393224 | tf_op jit(solution)/shard_map/ppermute | solution.py:180
  176.1 11.2 %collective-permute-start.19 = (bf16[512,128]{1,0:T(8,128)(2,1)S(1)}, bf16[512,128]{1,0:T(8,128)(2,1)S(1)}, u32[]{:S(2)}, u32[]{:S(2)}) collective-permute-start(bf16[512,128]{1,0:T(8,128)(2,1)S(1)} %get-tuple-element.7), channel_id=1, source_target_pairs={{80,0},{88,8},{96,16},{104,24},{0,48},{8,56},{32,80},{40,88},{48,9... | collective-permute-start | bytes 393224 | tf_op jit(solution)/shard_map/ppermute | solution.py:180
  180.4 14.9 %collective-permute-start.20 = (bf16[512,128]{1,0:T(8,128)(2,1)S(1)}, bf16[512,128]{1,0:T(8,128)(2,1)S(1)}, u32[]{:S(2)}, u32[]{:S(2)}) collective-permute-start(bf16[512,128]{1,0:T(8,128)(2,1)S(1)} %get-tuple-element.6), channel_id=1, source_target_pairs={{96,0},{104,8},{0,32},{8,40},{32,64},{40,72},{48,80},{56,88},{80,1... | collective-permute-start | bytes 393224 | tf_op jit(solution)/shard_map/ppermute | solution.py:180
  185.9 9.4 %collective-permute-start.21 = (bf16[512,128]{1,0:T(8,128)(2,1)S(1)}, bf16[512,128]{1,0:T(8,128)(2,1)S(1)}, u32[]{:S(2)}, u32[]{:S(2)}) collective-permute-start(bf16[512,128]{1,0:T(8,128)(2,1)S(1)} %get-tuple-element.5), channel_id=1, source_target_pairs={{0,16},{8,24},{32,48},{40,56},{48,64},{56,72},{80,96},{88,104},{96... | collective-permute-start | bytes 393224 | tf_op jit(solution)/shard_map/ppermute | solution.py:180
Sparse Core Ops, SparseCore 0:
  204.6 69.1 reduce-scatter.1

commit v2 on v0

v2 whole, which is shorter than its diff:
```python
import functools
import math

import jax
import jax.numpy as jnp
from jax import lax
from jax.experimental import pallas as pl
from jax.experimental.pallas import tpu as pltpu
from jax.sharding import PartitionSpec as P

HD = 128
BS = 128
KB = 16
TAB = 16
FIRST = 1536
NZ = 8
NX = 2
NY = 4
FIRST = 1536
LOW = -1e30
FACTOR = math.log2(math.e) / math.sqrt(HD)


def attend_kernel(chunks, first, last, base, flags, q, *refs):
    keys, values = refs[:chunks], refs[chunks : 2 * chunks]
    refs = refs[2 * chunks :]
    heads = q.shape[1] // HD
    per = keys[0].shape[0] // BS
    if first:
        mixed, stats = refs
    else:
        mixed_in, stats_in, mixed, stats = refs[:4]
    acc = refs[4] if last else mixed
    tiles = acc.shape[0]
    if first:
        acc[...] = jnp.zeros_like(acc)
        row = lax.broadcasted_iota(jnp.int32, stats.shape, 1)
        stats[...] = jnp.where(row == 0, LOW, 0.0)
    else:
        acc[...] = mixed_in[base : base + tiles]
        stats[...] = stats_in[base : base + tiles]

    def visit(qb, c, j):
        at = pl.ds(pl.multiple_of(j * BS, BS), BS)
        rows = pl.ds(pl.multiple_of((qb + base // heads) * BS, BS), BS)
        cols = [slice(h * HD, (h + 1) * HD) for h in range(heads)]
        before = [stats[qb * heads + h] for h in range(heads)]
        held = [acc[qb * heads + h] for h in range(heads)]
        scores = [
            lax.dot_general(
                keys[c][at, col], q[rows, col], (((1,), (1,)), ((), ())), preferred_element_type=jnp.float32
            )
            for col in cols
        ]
        after_it = []
        for h in range(heads):
            old, tot = before[h][0:1], before[h][1:2]
            new = jnp.maximum(old, jnp.max(scores[h], axis=0, keepdims=True))
            p = jnp.exp2((scores[h] - new) * FACTOR)
            scale = jnp.exp2((old - new) * FACTOR)
            tot = tot * scale + jnp.sum(p, axis=0, keepdims=True)
            add = lax.dot_general(
                values[c][at, cols[h]],
                p.astype(jnp.bfloat16),
                (((0,), (0,)), ((), ())),
                preferred_element_type=jnp.float32,
            )
            after_it.append((new, tot, held[h] * scale + add))
        for h in range(heads):
            new, tot, total = after_it[h]
            stats[qb * heads + h, 0:1] = new
            stats[qb * heads + h, 1:2] = tot
            acc[qb * heads + h] = total

    def step(n, carry):
        qb, j = n // per, n % per
        for c in range(chunks):

            @pl.when(flags[c, qb + base // heads, j] > 0)
            def _():
                visit(qb, c, j)

        return carry

    lax.fori_loop(0, tiles // heads * per, step, 0)
    if last and base:
        mixed[...] = acc[...].astype(mixed.dtype)
    elif last:
        mixed[...] = acc[...]


def attend(flags, q, keys, values, state, part):
    vmem = pl.BlockSpec(memory_space=pltpu.VMEM)
    smem = pl.BlockSpec(memory_space=pltpu.SMEM)
    last = part is not None
    tiles = q.shape[0] // BS * (q.shape[1] // HD) // (2 if last else 1)
    chunks = len(keys)
    first = state is None
    state = () if first else state
    at = 2 + 2 * chunks
    shape = (tiles, HD, BS)
    return pl.pallas_call(
        functools.partial(attend_kernel, chunks, first, last, tiles * (part or 0)),
        out_shape=(
            jax.ShapeDtypeStruct(shape, jnp.bfloat16 if part else jnp.float32),
            jax.ShapeDtypeStruct((tiles, 8, BS), jnp.float32),
        ),
        in_specs=[smem] + [vmem] * (1 + 2 * chunks + len(state)),
        out_specs=(vmem, vmem),
        input_output_aliases={} if first or last else {at: 0, at + 1: 1},
        scratch_shapes=[pltpu.VMEM(shape, jnp.float32)] if last else [],
        compiler_params=pltpu.CompilerParams(vmem_limit_bytes=24 << 20),
        cost_estimate=pl.CostEstimate(
            flops=tiles * chunks * 100000000, bytes_accessed=4 << 20, transcendentals=chunks << 20
        ),
        name="attend",
    )(flags, q, *keys, *values, *state)


def finish_kernel(mixed, stats, mixed_other, stats_other, out):
    heads = out.shape[1] // HD
    for i in range(mixed.shape[0]):
        m0, l0 = stats[i, 0:1], stats[i, 1:2]
        m1, l1 = stats_other[i, 0:1], stats_other[i, 1:2]
        m = jnp.maximum(m0, m1)
        a0 = jnp.exp2((m0 - m) * FACTOR)
        a1 = jnp.exp2((m1 - m) * FACTOR)
        total = l0 * a0 + l1 * a1
        both = mixed[i] * (a0 / total) + mixed_other[i].astype(jnp.float32) * (a1 / total)
        qb, h = i // heads, i % heads
        out[qb * BS : (qb + 1) * BS, h * HD : (h + 1) * HD] = both.T.astype(out.dtype)


def finish(own, other, shape):
    vmem = pl.BlockSpec(memory_space=pltpu.VMEM)
    return pl.pallas_call(
        finish_kernel,
        out_shape=jax.ShapeDtypeStruct(shape, jnp.bfloat16),
        in_specs=[vmem] * 4,
        out_specs=vmem,
        compiler_params=pltpu.CompilerParams(vmem_limit_bytes=16 << 20),
        cost_estimate=pl.CostEstimate(flops=2000000000, bytes_accessed=4 << 20, transcendentals=1 << 10),
        name="finish",
    )(*own, *other)


def after(x, *behind):
    return lax.optimization_barrier((x,) + behind)[0] if behind else x


def project(attended, weight, head):
    x, y = head // NY, head % NY
    rows = attended.shape[0] // (2 * NY)
    width = weight.shape[1]
    tiles = attended.reshape(2, NY, rows, -1)
    other_x = [(h, (h + NY) % (2 * NY)) for h in range(2 * NY)]

    def part(a, lo, hi):
        return jnp.dot(a, weight[:, lo:hi], preferred_element_type=jnp.float32)

    def narrow(a):
        return a.astype(jnp.bfloat16)

    def wide(a):
        return a.astype(jnp.float32)

    def ring(term, way):
        perm = [(h, h // NY * NY + (h % NY + way) % NY) for h in range(2 * NY)]
        acc = narrow(term((y - way) % NY))
        for s in range(NY - 1):
            acc = lax.ppermute(acc, "head", perm)
            acc = narrow(wide(acc) + term((y - way * (s + 2)) % NY))
        return acc

    cut = FIRST
    mid = cut + (width - cut) // 2
    far = lax.dynamic_index_in_dim(tiles, 1 - x, 0, False).reshape(NY * rows, -1)
    near = lax.dynamic_index_in_dim(tiles, x, 0, False).reshape(NY * rows, -1)
    got = lax.ppermute(narrow(part(far, 0, cut)), "head", other_x)

    def both(i):
        return lax.dynamic_index_in_dim(tiles, i, 1, False).reshape(2 * rows, -1)

    up = ring(lambda i: part(both(i), cut, mid), 1)
    down = ring(lambda i: part(both(i), mid, width), -1)
    half = narrow(wide(got) + part(near, 0, cut)).reshape(NY, rows, cut)
    left = ring(lambda i: wide(lax.dynamic_index_in_dim(half[..., : cut // 2], i, 0, False)), 1)
    right = ring(lambda i: wide(lax.dynamic_index_in_dim(half[..., cut // 2 :], i, 0, False)), -1)
    late = jnp.concatenate([up, down], axis=1).reshape(2, rows, width - cut)
    give = lax.ppermute(lax.dynamic_index_in_dim(late, 1 - x, 0, False), "head", other_x)
    keep = lax.dynamic_index_in_dim(late, x, 0, False)
    return jnp.concatenate([left, right, narrow(wide(give) + wide(keep))], axis=1)


def on_device(queries, keys, values, block_list, block_count, out_weight):
    rows, width = queries.shape
    per = rows // BS
    blk, head = lax.axis_index("blk"), lax.axis_index("head")
    z, xh = blk // NX, blk % NX
    cross = [(b, b ^ 1) for b in range(NZ * NX)]
    up = [(b, (b + NX) % (NZ * NX)) for b in range(NZ * NX)]
    down = [(b, a) for a, b in up]

    asked = lax.ppermute(jnp.concatenate([block_list, block_count[:, None]], axis=1), "blk", cross)
    both = jnp.concatenate([queries, lax.ppermute(queries, "blk", cross)])
    table = jnp.stack([jnp.concatenate([block_list, block_count[:, None]], axis=1), asked])
    listed = jnp.arange(KB, dtype=jnp.int32) < table[..., KB:]
    seen = jnp.any(
        listed[..., None] & (table[..., :KB, None] == jnp.arange(NZ * NX * per, dtype=jnp.int32)), axis=2
    ).astype(jnp.int32)
    seen = lax.dynamic_index_in_dim(seen.reshape(2 * per, NZ, NX, per), xh, 2, False)
    flags = jnp.transpose(seen, (1, 0, 2))[(z - jnp.arange(NZ)) % NZ]

    def visit(stage, state, part=None):
        return attend(
            jnp.stack([flags[d] for d, _, _ in stage]),
            both,
            [k for _, k, _ in stage],
            [v for _, _, v in stage],
            state,
            part,
        )

    stage = ((0, keys, values),)
    state = None
    ups, downs = (keys, values), (keys, values)
    for s in range(1, NZ // 2 + 1):
        if s < NZ // 2:
            ups = tuple(lax.ppermute(a, "blk", up) for a in ups)
            downs = tuple(lax.ppermute(a, "blk", down) for a in downs)
            coming = ((s, *ups), (NZ - s, *downs))
        else:
            coming = ((s, lax.ppermute(ups[0], "blk", up), lax.ppermute(downs[1], "blk", down)),)
        state = visit(stage, state)
        if s < NZ // 2:
            ups = tuple(after(a, state[1]) for a in ups)
            downs = tuple(after(a, state[1]) for a in downs)
        stage = coming
    theirs = visit(stage, state, 1)
    other = [lax.ppermute(a, "blk", cross) for a in theirs]
    mine = visit(stage, state, 0)
    attended = finish(mine, other, (rows, width))
    return project(attended, out_weight, head)


def solution(mesh):
    placed = (
        P(("dp", "blk"), "head"),
        P(("dp", "blk"), "head"),
        P(("dp", "blk"), "head"),
        P(("dp", "blk"), None),
        P(("dp", "blk")),
        P("head", None),
    )
    return jax.shard_map(
        on_device,
        mesh=mesh,
        in_specs=placed,
        out_specs=P(("dp", "blk", "head"), None),
        check_vma=False,
    )
```

time: 661 us -> 190 us (0.29)
  waiting for transfers between devices: 374 us -> 83.7 us
  matrix products: 159 us -> 6.01 us
  local copies, waits for them, and re-layouts: 72.9 us -> 7.87 us
  starting transfers between devices: 0.08 us -> 47.8 us
  Pallas kernels: 0 us -> 40.1 us
  other arithmetic: 33.8 us -> 3.48 us
  between operations: 13.2 us -> 0.5 us
    all_gather x2 -> x0, waiting for transfers between devices: 312 us -> none  [the longest x1 156 us: on_device(): value_piece = lax.all_gather(values, 'blk', axis=0, tiled=True)]
    dot_general x49 -> x10, matrix products: 159 us -> 6.01 us  [part(): return jnp.dot(a, weight[:, lo:hi], preferred_element_type=jnp.float32)]
    ppermute x0 -> x32, waiting for transfers between devices: none -> 83.7 us  [the longest x12 32.3 us: ring(): acc = lax.ppermute(acc, 'head', perm)]
    reduce_scatter x1 -> x0, waiting for transfers between devices: 61.1 us -> none  [on_device(): lax.psum_scatter(jnp.dot(attended, out_weight, preferred_element_type=jnp...]
    ppermute x0 -> x32, starting transfers between devices: none -> 47.8 us  [the longest x6 18 us: on_device(): ups = tuple((lax.ppermute(a, 'blk', up) for a in ups))]
    pallas_call x0 -> x7, Pallas kernels: none -> 40.1 us  [the longest x6 39.7 us: attend(): pl.pallas_call(functools.partial(attend_kernel, chunks, first, last, tile...]
    dynamic_slice x64 -> x4, local copies, waits for them, and re-layouts: 40.1 us -> 0.35 us  [the longest x2 0.16 us: on_device(): lax.dynamic_index_in_dim(seen.reshape(2 * per, NZ, NX, per), xh, 2, False)]
    broadcast_in_dim x16 -> x1, local copies, waits for them, and re-layouts: 25.6 us -> 0.74 us  [on_device(): block_count[:, None]]
  transfers between devices with their start and end apart: 3 -> 32, of which waited for: 3 -> 17; matrix products, arithmetic and copies ran while one was open for 0% -> 7% of each run, Pallas kernels for 0% -> 19%
where the time goes in v2:
time: 190 us
  waiting for transfers between devices  83.7 us (44%)
  starting transfers between devices  47.8 us (25%)
  Pallas kernels  40.1 us (21%)
  local copies, waits for them, and re-layouts  7.87 us (4%)
  matrix products  6.01 us (3%)
  other arithmetic  3.48 us (2%)
    pallas_call x6, Pallas kernels, attend(): pl.pallas_call(functools.partial(attend_kernel, chunks, first, last, tile...  39.7 us
    ppermute x12, waiting for transfers between devices, ring(): acc = lax.ppermute(acc, 'head', perm)  32.3 us
    ppermute x6, waiting for transfers between devices, on_device(): downs = tuple((lax.ppermute(a, 'blk', down) for a in downs))  29.2 us
    ppermute x6, starting transfers between devices, on_device(): ups = tuple((lax.ppermute(a, 'blk', up) for a in ups))  18 us
    ppermute x12, starting transfers between devices, ring(): acc = lax.ppermute(acc, 'head', perm)  14.3 us
    ppermute x1, waiting for transfers between devices, on_device(): both = jnp.concatenate([queries, lax.ppermute(queries, 'blk', cross)])  9.01 us
    dot_general x10, matrix products, part(): return jnp.dot(a, weight[:, lo:hi], preferred_element_type=jnp.float32)  6.01 us
    ppermute x2, waiting for transfers between devices, on_device(): other = [lax.ppermute(a, 'blk', cross) for a in theirs]  5.45 us
  transfers between devices with their start and end apart: 32, of which 17 were waited for; matrix products, arithmetic and copies ran while one was open for 7% of the time, Pallas kernels for 19%

profile of v2, /device:TPU:122, one launch (start us, length us, event | category | flops | bytes accessed | tf_op | source)
XLA Modules:
  0.0 189.5 jit_solution(8746186230723215931)
XLA Ops:
  0.0 3.1 %collective-permute-start.2 = (bf16[512,640]{1,0:T(8,128)(2,1)}, bf16[512,640]{1,0:T(8,128)(2,1)}, u32[]{:S(2)}, u32[]{:S(2)}) collective-permute-start(bf16[512,640]{1,0:T(8,128)(2,1)} %refs_0_.1), channel_id=1, source_target_pairs={{0,16},{8,24},{16,32},{24,40},{32,48},{40,56},{48,64},{56,72},{64,... | collective-permute-start | bytes 1966088 | tf_op jit(solution)/shard_map/ppermute | solution.py:229
  3.9 0.8 pad_add_fusion.4
  4.6 2.1 %collective-permute-start = (s32[4,17]{1,0:T(4,128)S(1)}, s32[4,17]{1,0:T(4,128)S(1)}, u32[]{:S(2)}, u32[]{:S(2)}) collective-permute-start(s32[4,17]{1,0:T(4,128)S(1)} %pad_add_fusion.4), channel_id=1, source_target_pairs={{0,8},{8,0},{16,24},{24,16},{32,40},{40,32},{48,56},{56,48},{64,72... | collective-permute-start | bytes 824 | tf_op jit(solution)/shard_map/ppermute | solution.py:204
  6.8 1.4 collective-permute-start.1
  8.2 3.2 %collective-permute-start.5 = (bf16[512,640]{1,0:T(8,128)(2,1)}, bf16[512,640]{1,0:T(8,128)(2,1)}, u32[]{:S(2)}, u32[]{:S(2)}) collective-permute-start(bf16[512,640]{1,0:T(8,128)(2,1)} %refs_1_.1), channel_id=1, source_target_pairs={{0,16},{8,24},{16,32},{24,40},{32,48},{40,56},{48,64},{56,72},{64,... | collective-permute-start | bytes 1966088 | tf_op jit(solution)/shard_map/ppermute | solution.py:229
  12.2 1.1 constant_dynamic-update-slice_fusion.1
  15.5 9.0 %collective-permute-done.1 = bf16[512,640]{1,0:T(8,128)(2,1)} collective-permute-done((bf16[512,640]{1,0:T(8,128)(2,1)}, bf16[512,640]{1,0:T(8,128)(2,1)}, u32[]{:S(2)}, u32[]{:S(2)}) %collective-permute-start.1) | collective-permute-done | bytes 655392 | tf_op jit(solution)/shard_map/ppermute | solution.py:205
  24.5 1.2 constant_dynamic-update-slice_fusion.q
  25.7 7.6 %attend.6 = (f32[40,128,128]{2,1,0:T(8,128)S(1)}, f32[40,8,128]{2,1,0:T(8,128)S(1)}) custom-call(s32[1,8,4]{2,1,0:T(8,128)S(1)} %copy.35.flags, bf16[1024,640]{1,0:T(8,128)(2,1)S(1)} %constant_dynamic-update-slice_fusion.q, bf16[512,640]{1,0:T(8,128)(2,1)S(1)} %copy-done, bf16[512,640]{1,0:T(8,128)(2,1)S(1)} %copy-done.1), custom_call_target="tpu_custom_call" | custom-call | flops 4000000000 | bytes 4194304 | tf_op jit(solution)/shard_map/attend/pallas_call | solution.py:102
  33.3 1.6 collective-permute-done.6.refs_3_
  34.9 2.7 %collective-permute-start.3 = (bf16[512,640]{1,0:T(8,128)(2,1)}, bf16[512,640]{1,0:T(8,128)(2,1)S(1)}, u32[]{:S(2)}, u32[]{:S(2)}) collective-permute-start(bf16[512,640]{1,0:T(8,128)(2,1)} %collective-permute-done.2.refs_0_), channel_id=1, source_target_pairs={{0,16},{8,24},{16,32},{24,40},{32,48},{40,56},{48,64},{56,72},{64,... | collective-permute-start | bytes 1966088 | tf_op jit(solution)/shard_map/ppermute | solution.py:229
  37.6 3.3 %collective-permute-start.9 = (bf16[512,640]{1,0:T(8,128)(2,1)}, bf16[512,640]{1,0:T(8,128)(2,1)S(1)}, u32[]{:S(2)}, u32[]{:S(2)}) collective-permute-start(bf16[512,640]{1,0:T(8,128)(2,1)} %collective-permute-done.5.refs_2_), channel_id=1, source_target_pairs={{0,16},{8,24},{16,32},{24,40},{32,48},{40,56},{48,64},{56,72},{64,... | collective-permute-start | bytes 1966088 | tf_op jit(solution)/shard_map/ppermute | solution.py:229
  40.8 9.3 %attend.7 = (f32[40,128,128]{2,1,0:T(8,128)S(1)}, f32[40,8,128]{2,1,0:T(8,128)S(1)}) custom-call(s32[2,8,4]{2,1,0:T(8,128)S(1)} %pad_add_fusion.flags, bf16[1024,640]{1,0:T(8,128)(2,1)S(1)} %constant_dynamic-update-slice_fusion.q, bf16[512,640]{1,0:T(8,128)(2,1)} %collective-permute-done.2.refs_0_, ...), custom_call_target="tpu_custom_call", output_to_operand_aliasing={{0}: (6, {}), {1}: (7, {})} | custom-call | flops 8000000000 | bytes 4194304 | tf_op jit(solution)/shard_map/attend/pallas_call | solution.py:102
  50.1 2.9 %collective-permute-done.3.refs_0_ = bf16[512,640]{1,0:T(8,128)(2,1)S(1)} collective-permute-done((bf16[512,640]{1,0:T(8,128)(2,1)}, bf16[512,640]{1,0:T(8,128)(2,1)S(1)}, u32[]{:S(2)}, u32[]{:S(2)}) %collective-permute-start.3) | collective-permute-done | bytes 655392 | tf_op jit(solution)/shard_map/ppermute | solution.py:229
  53.1 3.6 %collective-permute-done.10.refs_3_ = bf16[512,640]{1,0:T(8,128)(2,1)S(1)} collective-permute-done((bf16[512,640]{1,0:T(8,128)(2,1)}, bf16[512,640]{1,0:T(8,128)(2,1)S(1)}, u32[]{:S(2)}, u32[]{:S(2)}) %collective-permute-start.10) | collective-permute-done | bytes 655392 | tf_op jit(solution)/shard_map/ppermute | solution.py:230
  56.6 9.3 %collective-permute-done.8.refs_1_ = bf16[512,640]{1,0:T(8,128)(2,1)S(1)} collective-permute-done((bf16[512,640]{1,0:T(8,128)(2,1)S(1)}, bf16[512,640]{1,0:T(8,128)(2,1)S(1)}, u32[]{:S(2)}, u32[]{:S(2)}) %collective-permute-start.8) | collective-permute-done | bytes 655392 | tf_op jit(solution)/shard_map/ppermute | solution.py:230
  66.7 2.5 %collective-permute-start.7 = (bf16[512,640]{1,0:T(8,128)(2,1)S(1)}, bf16[512,640]{1,0:T(8,128)(2,1)S(1)}, u32[]{:S(2)}, u32[]{:S(2)}) collective-permute-start(bf16[512,640]{1,0:T(8,128)(2,1)S(1)} %collective-permute-done.3.refs_0_), channel_id=1, source_target_pairs={{0,16},{8,24},{16,32},{24,40},{32,48},{40,56},{48,64},{56,72},{64,... | collective-permute-start | bytes 1966088 | tf_op jit(solution)/shard_map/ppermute | solution.py:229
  69.2 3.2 %collective-permute-start.15 = (bf16[512,640]{1,0:T(8,128)(2,1)S(1)}, bf16[512,640]{1,0:T(8,128)(2,1)S(1)}, u32[]{:S(2)}, u32[]{:S(2)}) collective-permute-start(bf16[512,640]{1,0:T(8,128)(2,1)S(1)} %collective-permute-done.9.refs_2_), channel_id=1, source_target_pairs={{0,16},{8,24},{16,32},{24,40},{32,48},{40,56},{48,64},{56,72},{64,... | collective-permute-start | bytes 1966088 | tf_op jit(solution)/shard_map/ppermute | solution.py:229
  72.4 8.5 %attend.8 = (f32[40,128,128]{2,1,0:T(8,128)S(1)}, f32[40,8,128]{2,1,0:T(8,128)S(1)}) custom-call(s32[2,8,4]{2,1,0:T(8,128)S(1)} %pad_add_fusion.1.flags, bf16[1024,640]{1,0:T(8,128)(2,1)S(1)} %constant_dynamic-update-slice_fusion.q, bf16[512,640]{1,0:T(8,128)(2,1)S(1)} %collective-permute-done.3.refs_0_, ...), custom_call_target="tpu_custom_call", output_to_operand_aliasing={{0}: (6, {}), {1}: (7, {})} | custom-call | flops 8000000000 | bytes 4194304 | tf_op jit(solution)/shard_map/attend/pallas_call | solution.py:102
  80.9 3.9 %collective-permute-done.12.refs_3_ = bf16[512,640]{1,0:T(8,128)(2,1)S(1)} collective-permute-done((bf16[512,640]{1,0:T(8,128)(2,1)S(1)}, bf16[512,640]{1,0:T(8,128)(2,1)S(1)}, u32[]{:S(2)}, u32[]{:S(2)}) %collective-permute-start.12) | collective-permute-done | bytes 655392 | tf_op jit(solution)/shard_map/ppermute | solution.py:230
  84.9 3.2 %collective-permute-start.11 = (bf16[512,640]{1,0:T(8,128)(2,1)S(1)}, bf16[512,640]{1,0:T(8,128)(2,1)S(1)}, u32[]{:S(2)}, u32[]{:S(2)}) collective-permute-start(bf16[512,640]{1,0:T(8,128)(2,1)S(1)} %collective-permute-done.7.refs_0_), channel_id=1, source_target_pairs={{0,16},{8,24},{16,32},{24,40},{32,48},{40,56},{48,64},{56,72},{64,... | collective-permute-start | bytes 1966088 | tf_op jit(solution)/shard_map/ppermute | solution.py:233
  88.1 10.8 %collective-permute-done.14.refs_1_ = bf16[512,640]{1,0:T(8,128)(2,1)S(1)} collective-permute-done((bf16[512,640]{1,0:T(8,128)(2,1)S(1)}, bf16[512,640]{1,0:T(8,128)(2,1)S(1)}, u32[]{:S(2)}, u32[]{:S(2)}) %collective-permute-start.14) | collective-permute-done | bytes 655392 | tf_op jit(solution)/shard_map/ppermute | solution.py:230
  98.9 6.9 %attend.9 = (f32[40,128,128]{2,1,0:T(8,128)S(1)}, f32[40,8,128]{2,1,0:T(8,128)S(1)}) custom-call(s32[2,8,4]{2,1,0:T(8,128)S(1)} %pad_add_fusion.2.flags, bf16[1024,640]{1,0:T(8,128)(2,1)S(1)} %constant_dynamic-update-slice_fusion.q, bf16[512,640]{1,0:T(8,128)(2,1)S(1)} %collective-permute-done.7.refs_0_, ...), custom_call_target="tpu_custom_call", output_to_operand_aliasing={{0}: (6, {}), {1}: (7, {})} | custom-call | flops 8000000000 | bytes 4194304 | tf_op jit(solution)/shard_map/attend/pallas_call | solution.py:102
  105.8 2.3 %collective-permute-done.13.refs_1_ = bf16[512,640]{1,0:T(8,128)(2,1)S(1)} collective-permute-done((bf16[512,640]{1,0:T(8,128)(2,1)S(1)}, bf16[512,640]{1,0:T(8,128)(2,1)S(1)}, u32[]{:S(2)}, u32[]{:S(2)}) %collective-permute-start.13) | collective-permute-done | bytes 655392 | tf_op jit(solution)/shard_map/ppermute | solution.py:233
  108.1 3.2 %attend.11 = (bf16[20,128,128]{2,1,0:T(8,128)(2,1)}, f32[20,8,128]{2,1,0:T(8,128)S(1)}) custom-call(s32[1,8,4]{2,1,0:T(8,128)S(1)} %copy.34.flags, bf16[1024,640]{1,0:T(8,128)(2,1)S(1)} %constant_dynamic-update-slice_fusion.q, bf16[512,640]{1,0:T(8,128)(2,1)S(1)} %collective-permute-done.11.refs_0_, bf16[512,640]{1,0:T(8,128)(2,1)S(1)} %collective-permute-done.13.refs_1_, ...), custom_call_target="tpu_custom_call" | custom-call | flops 2000000000 | bytes 4194304 | tf_op jit(solution)/shard_map/attend/pallas_call | solution.py:102
  111.3 4.8 %collective-permute-start.16 = (bf16[20,128,128]{2,1,0:T(8,128)(2,1)}, bf16[20,128,128]{2,1,0:T(8,128)(2,1)S(1)}, u32[]{:S(2)}, u32[]{:S(2)}) collective-permute-start(bf16[20,128,128]{2,1,0:T(8,128)(2,1)} %get-tuple-element.47), channel_id=1, source_target_pairs={{0,8},{8,0},{16,24},{24,16},{32,40},{40,32},{48,56},{56,48},{64,72... | collective-permute-start | bytes 1966088 | tf_op jit(solution)/shard_map/ppermute | solution.py:240
  116.2 1.7 copy-done.3
  117.9 4.4 %attend.10 = (f32[20,128,128]{2,1,0:T(8,128)S(1)}, f32[20,8,128]{2,1,0:T(8,128)S(1)}) custom-call(s32[1,8,4]{2,1,0:T(8,128)S(1)} %copy.34.flags, bf16[1024,640]{1,0:T(8,128)(2,1)S(1)} %constant_dynamic-update-slice_fusion.q, bf16[512,640]{1,0:T(8,128)(2,1)S(1)} %collective-permute-done.11.refs_0_, bf16[512,640]{1,0:T(8,128)(2,1)S(1)} %collective-permute-done.13.refs_1_, ...), custom_call_target="tpu_custom_call" | custom-call | flops 2000000000 | bytes 4194304 | tf_op jit(solution)/shard_map/attend/pallas_call | solution.py:102
  122.3 5.4 %collective-permute-done.17.stats_other = f32[20,8,128]{2,1,0:T(8,128)S(1)} collective-permute-done((f32[20,8,128]{2,1,0:T(8,128)S(1)}, f32[20,8,128]{2,1,0:T(8,128)S(1)}, u32[]{:S(2)}, u32[]{:S(2)}) %collective-permute-start.17) | collective-permute-done | bytes 81952 | tf_op jit(solution)/shard_map/ppermute | solution.py:240
  128.2 1.2 slice-done.1
  129.4 0.8 convolution_convert_fusion
  130.2 2.9 %collective-permute-start.18 = (bf16[256,1536]{1,0:T(8,128)(2,1)S(1)}, bf16[256,1536]{1,0:T(8,128)(2,1)S(1)}, u32[]{:S(2)}, u32[]{:S(2)}) collective-permute-start(bf16[256,1536]{1,0:T(8,128)(2,1)S(1)} %convolution_convert_fusion), channel_id=1, source_target_pairs={{0,4},{1,5},{2,6},{3,7},{4,0},{5,1},{6,2},{7,3},{8,12},{9,13},{10,... | collective-permute-start | bytes 2359304 | tf_op jit(solution)/shard_map/ppermute | solution.py:179
  135.8 2.1 %collective-permute-start.28 = (bf16[128,1792]{1,0:T(8,128)(2,1)S(1)}, bf16[128,1792]{1,0:T(8,128)(2,1)S(1)}, u32[]{:S(2)}, u32[]{:S(2)}) collective-permute-start(bf16[128,1792]{1,0:T(8,128)(2,1)S(1)} %convolution_convert_fusion.1), channel_id=1, source_target_pairs={{0,3},{1,0},{2,1},{3,2},{4,7},{5,4},{6,5},{7,6},{8,11},{9,8},{10,9... | collective-permute-start | bytes 1376264 | tf_op jit(solution)/shard_map/ppermute | solution.py:171
  139.0 8.2 %collective-permute-done.25 = bf16[128,1792]{1,0:T(8,128)(2,1)S(1)} collective-permute-done((bf16[128,1792]{1,0:T(8,128)(2,1)S(1)}, bf16[128,1792]{1,0:T(8,128)(2,1)S(1)}, u32[]{:S(2)}, u32[]{:S(2)}) %collective-permute-start.25) | collective-permute-done | bytes 458784 | tf_op jit(solution)/shard_map/ppermute | solution.py:171
  148.5 1.6 collective-permute-done.28
  150.7 1.1 collective-permute-start.29
  151.8 0.8 add_convert_fusion
  152.7 2.3 %collective-permute-start.19 = (bf16[64,768]{1,0:T(8,128)(2,1)S(1)}, bf16[64,768]{1,0:T(8,128)(2,1)S(1)}, u32[]{:S(2)}, u32[]{:S(2)}) collective-permute-start(bf16[64,768]{1,0:T(8,128)(2,1)S(1)} %dynamic-slice_bitcast_fusion.2), channel_id=1, source_target_pairs={{0,1},{1,2},{2,3},{3,0},{4,5},{5,6},{6,7},{7,4},{8,9},{9,10},{10,1... | collective-permute-start | bytes 294920 | tf_op jit(solution)/shard_map/ppermute | solution.py:171
  155.1 6.0 %collective-permute-done.19 = bf16[64,768]{1,0:T(8,128)(2,1)S(1)} collective-permute-done((bf16[64,768]{1,0:T(8,128)(2,1)S(1)}, bf16[64,768]{1,0:T(8,128)(2,1)S(1)}, u32[]{:S(2)}, u32[]{:S(2)}) %collective-permute-start.19) | collective-permute-done | bytes 98336 | tf_op jit(solution)/shard_map/ppermute | solution.py:171
  161.1 0.9 collective-permute-start.20
  162.0 4.4 %collective-permute-done.22 = bf16[64,768]{1,0:T(8,128)(2,1)S(1)} collective-permute-done((bf16[64,768]{1,0:T(8,128)(2,1)S(1)}, bf16[64,768]{1,0:T(8,128)(2,1)S(1)}, u32[]{:S(2)}, u32[]{:S(2)}) %collective-permute-start.22) | collective-permute-done | bytes 98336 | tf_op jit(solution)/shard_map/ppermute | solution.py:171
  166.6 3.3 %collective-permute-start.27 = (bf16[128,1792]{1,0:T(8,128)(2,1)S(1)}, bf16[128,1792]{1,0:T(8,128)(2,1)S(1)}, u32[]{:S(2)}, u32[]{:S(2)}) collective-permute-start(bf16[128,1792]{1,0:T(8,128)(2,1)S(1)} %add_convert_fusion.5), channel_id=1, source_target_pairs={{0,1},{1,2},{2,3},{3,0},{4,5},{5,6},{6,7},{7,4},{8,9},{9,10},{10,1... | collective-permute-start | bytes 1376264 | tf_op jit(solution)/shard_map/ppermute | solution.py:171
  170.2 3.3 %collective-permute-start.21 = (bf16[64,768]{1,0:T(8,128)(2,1)S(1)}, bf16[64,768]{1,0:T(8,128)(2,1)S(1)}, u32[]{:S(2)}, u32[]{:S(2)}) collective-permute-start(bf16[64,768]{1,0:T(8,128)(2,1)S(1)} %fusion.22), channel_id=1, source_target_pairs={{0,1},{1,2},{2,3},{3,0},{4,5},{5,6},{6,7},{7,4},{8,9},{9,10},{10,1... | collective-permute-start | bytes 294920 | tf_op jit(solution)/shard_map/ppermute | solution.py:171
  173.4 2.5 %collective-permute-done.27 = bf16[128,1792]{1,0:T(8,128)(2,1)S(1)} collective-permute-done((bf16[128,1792]{1,0:T(8,128)(2,1)S(1)}, bf16[128,1792]{1,0:T(8,128)(2,1)S(1)}, u32[]{:S(2)}, u32[]{:S(2)}) %collective-permute-start.27) | collective-permute-done | bytes 458784 | tf_op jit(solution)/shard_map/ppermute | solution.py:171
  176.0 3.8 %collective-permute-done.30 = bf16[128,1792]{1,0:T(8,128)(2,1)S(1)} collective-permute-done((bf16[128,1792]{1,0:T(8,128)(2,1)S(1)}, bf16[128,1792]{1,0:T(8,128)(2,1)S(1)}, u32[]{:S(2)}, u32[]{:S(2)}) %collective-permute-start.30) | collective-permute-done | bytes 458784 | tf_op jit(solution)/shard_map/ppermute | solution.py:171
  180.3 5.8 %collective-permute-done.24 = bf16[64,768]{1,0:T(8,128)(2,1)S(1)} collective-permute-done((bf16[64,768]{1,0:T(8,128)(2,1)S(1)}, bf16[64,768]{1,0:T(8,128)(2,1)S(1)}, u32[]{:S(2)}, u32[]{:S(2)}) %collective-permute-start.24) | collective-permute-done | bytes 98336 | tf_op jit(solution)/shard_map/ppermute | solution.py:171
  186.1 2.5 %collective-permute-done.31 = bf16[64,3584]{1,0:T(8,128)(2,1)S(1)} collective-permute-done((bf16[64,3584]{1,0:T(8,128)(2,1)S(1)}, bf16[64,3584]{1,0:T(8,128)(2,1)S(1)}, u32[]{:S(2)}, u32[]{:S(2)}) %collective-permute-start.31) | collective-permute-done | bytes 458784 | tf_op jit(solution)/shard_map/ppermute | solution.py:190
  188.7 0.9 pad_maximum_fusion.1
  (93 shorter events, 11.6 us)
Async XLA Ops:
  0.0 25.7 %copy-start = (bf16[512,640]{1,0:T(8,128)(2,1)S(1)}, bf16[512,640]{1,0:T(8,128)(2,1)}, u32[]{:S(2)}) copy-start(bf16[512,640]{1,0:T(8,128)(2,1)} %refs_0_.1) | copy-start | bytes 1966084
  0.0 25.7 %copy-start.1 = (bf16[512,640]{1,0:T(8,128)(2,1)S(1)}, bf16[512,640]{1,0:T(8,128)(2,1)}, u32[]{:S(2)}) copy-start(bf16[512,640]{1,0:T(8,128)(2,1)} %refs_1_.1) | copy-start | bytes 1966084
  0.0 33.3 %collective-permute-start.2 = (bf16[512,640]{1,0:T(8,128)(2,1)}, bf16[512,640]{1,0:T(8,128)(2,1)}, u32[]{:S(2)}, u32[]{:S(2)}) collective-permute-start(bf16[512,640]{1,0:T(8,128)(2,1)} %refs_0_.1), channel_id=1, source_target_pairs={{0,16},{8,24},{16,32},{24,40},{32,48},{40,56},{48,64},{56,72},{64,... | collective-permute-start | bytes 1966088 | tf_op jit(solution)/shard_map/ppermute | solution.py:229
  3.1 30.1 %collective-permute-start.4 = (bf16[512,640]{1,0:T(8,128)(2,1)}, bf16[512,640]{1,0:T(8,128)(2,1)S(1)}, u32[]{:S(2)}, u32[]{:S(2)}) collective-permute-start(bf16[512,640]{1,0:T(8,128)(2,1)} %refs_0_.1), channel_id=1, source_target_pairs={{16,0},{24,8},{32,16},{40,24},{48,32},{56,40},{64,48},{72,56},{80,... | collective-permute-start | bytes 1966088 | tf_op jit(solution)/shard_map/ppermute | solution.py:230
  4.6 8.7 %collective-permute-start = (s32[4,17]{1,0:T(4,128)S(1)}, s32[4,17]{1,0:T(4,128)S(1)}, u32[]{:S(2)}, u32[]{:S(2)}) collective-permute-start(s32[4,17]{1,0:T(4,128)S(1)} %pad_add_fusion.4), channel_id=1, source_target_pairs={{0,8},{8,0},{16,24},{24,16},{32,40},{40,32},{48,56},{56,48},{64,72... | collective-permute-start | bytes 824 | tf_op jit(solution)/shard_map/ppermute | solution.py:204
  6.8 17.7 %collective-permute-start.1 = (bf16[512,640]{1,0:T(8,128)(2,1)}, bf16[512,640]{1,0:T(8,128)(2,1)}, u32[]{:S(2)}, u32[]{:S(2)}) collective-permute-start(bf16[512,640]{1,0:T(8,128)(2,1)} %param.6), channel_id=1, source_target_pairs={{0,8},{8,0},{16,24},{24,16},{32,40},{40,32},{48,56},{56,48},{64,72... | collective-permute-start | bytes 1966088 | tf_op jit(solution)/shard_map/ppermute | solution.py:205
  8.2 25.1 %collective-permute-start.5 = (bf16[512,640]{1,0:T(8,128)(2,1)}, bf16[512,640]{1,0:T(8,128)(2,1)}, u32[]{:S(2)}, u32[]{:S(2)}) collective-permute-start(bf16[512,640]{1,0:T(8,128)(2,1)} %refs_1_.1), channel_id=1, source_target_pairs={{0,16},{8,24},{16,32},{24,40},{32,48},{40,56},{48,64},{56,72},{64,... | collective-permute-start | bytes 1966088 | tf_op jit(solution)/shard_map/ppermute | solution.py:229
  13.4 21.5 %collective-permute-start.6 = (bf16[512,640]{1,0:T(8,128)(2,1)}, bf16[512,640]{1,0:T(8,128)(2,1)}, u32[]{:S(2)}, u32[]{:S(2)}) collective-permute-start(bf16[512,640]{1,0:T(8,128)(2,1)} %refs_1_.1), channel_id=1, source_target_pairs={{16,0},{24,8},{32,16},{40,24},{48,32},{56,40},{64,48},{72,56},{80,... | collective-permute-start | bytes 1966088 | tf_op jit(solution)/shard_map/ppermute | solution.py:230
  34.9 18.2 %collective-permute-start.3 = (bf16[512,640]{1,0:T(8,128)(2,1)}, bf16[512,640]{1,0:T(8,128)(2,1)S(1)}, u32[]{:S(2)}, u32[]{:S(2)}) collective-permute-start(bf16[512,640]{1,0:T(8,128)(2,1)} %collective-permute-done.2.refs_0_), channel_id=1, source_target_pairs={{0,16},{8,24},{16,32},{24,40},{32,48},{40,56},{48,64},{56,72},{64,... | collective-permute-start | bytes 1966088 | tf_op jit(solution)/shard_map/ppermute | solution.py:229
  37.5 19.1 %collective-permute-start.10 = (bf16[512,640]{1,0:T(8,128)(2,1)}, bf16[512,640]{1,0:T(8,128)(2,1)S(1)}, u32[]{:S(2)}, u32[]{:S(2)}) collective-permute-start(bf16[512,640]{1,0:T(8,128)(2,1)} %collective-permute-done.6.refs_3_), channel_id=1, source_target_pairs={{16,0},{24,8},{32,16},{40,24},{48,32},{56,40},{64,48},{72,56},{80,... | collective-permute-start | bytes 1966088 | tf_op jit(solution)/shard_map/ppermute | solution.py:230
  37.6 28.4 %collective-permute-start.8 = (bf16[512,640]{1,0:T(8,128)(2,1)S(1)}, bf16[512,640]{1,0:T(8,128)(2,1)S(1)}, u32[]{:S(2)}, u32[]{:S(2)}) collective-permute-start(bf16[512,640]{1,0:T(8,128)(2,1)S(1)} %collective-permute-done.4.refs_1_), channel_id=1, source_target_pairs={{16,0},{24,8},{32,16},{40,24},{48,32},{56,40},{64,48},{72,56},{80,... | collective-permute-start | bytes 1966088 | tf_op jit(solution)/shard_map/ppermute | solution.py:230
  37.6 28.4 %collective-permute-start.9 = (bf16[512,640]{1,0:T(8,128)(2,1)}, bf16[512,640]{1,0:T(8,128)(2,1)S(1)}, u32[]{:S(2)}, u32[]{:S(2)}) collective-permute-start(bf16[512,640]{1,0:T(8,128)(2,1)} %collective-permute-done.5.refs_2_), channel_id=1, source_target_pairs={{0,16},{8,24},{16,32},{24,40},{32,48},{40,56},{48,64},{56,72},{64,... | collective-permute-start | bytes 1966088 | tf_op jit(solution)/shard_map/ppermute | solution.py:229
  66.0 18.9 %collective-permute-start.12 = (bf16[512,640]{1,0:T(8,128)(2,1)S(1)}, bf16[512,640]{1,0:T(8,128)(2,1)S(1)}, u32[]{:S(2)}, u32[]{:S(2)}) collective-permute-start(bf16[512,640]{1,0:T(8,128)(2,1)S(1)} %collective-permute-done.10.refs_3_), channel_id=1, source_target_pairs={{16,0},{24,8},{32,16},{40,24},{48,32},{56,40},{64,48},{72,56},{80,... | collective-permute-start | bytes 1966088 | tf_op jit(solution)/shard_map/ppermute | solution.py:230
  66.7 18.2 %collective-permute-start.7 = (bf16[512,640]{1,0:T(8,128)(2,1)S(1)}, bf16[512,640]{1,0:T(8,128)(2,1)S(1)}, u32[]{:S(2)}, u32[]{:S(2)}) collective-permute-start(bf16[512,640]{1,0:T(8,128)(2,1)S(1)} %collective-permute-done.3.refs_0_), channel_id=1, source_target_pairs={{0,16},{8,24},{16,32},{24,40},{32,48},{40,56},{48,64},{56,72},{64,... | collective-permute-start | bytes 1966088 | tf_op jit(solution)/shard_map/ppermute | solution.py:229
  69.2 29.7 %collective-permute-start.14 = (bf16[512,640]{1,0:T(8,128)(2,1)S(1)}, bf16[512,640]{1,0:T(8,128)(2,1)S(1)}, u32[]{:S(2)}, u32[]{:S(2)}) collective-permute-start(bf16[512,640]{1,0:T(8,128)(2,1)S(1)} %collective-permute-done.8.refs_1_), channel_id=1, source_target_pairs={{16,0},{24,8},{32,16},{40,24},{48,32},{56,40},{64,48},{72,56},{80,... | collective-permute-start | bytes 1966088 | tf_op jit(solution)/shard_map/ppermute | solution.py:230
  69.2 29.7 %collective-permute-start.15 = (bf16[512,640]{1,0:T(8,128)(2,1)S(1)}, bf16[512,640]{1,0:T(8,128)(2,1)S(1)}, u32[]{:S(2)}, u32[]{:S(2)}) collective-permute-start(bf16[512,640]{1,0:T(8,128)(2,1)S(1)} %collective-permute-done.9.refs_2_), channel_id=1, source_target_pairs={{0,16},{8,24},{16,32},{24,40},{32,48},{40,56},{48,64},{56,72},{64,... | collective-permute-start | bytes 1966088 | tf_op jit(solution)/shard_map/ppermute | solution.py:229
  84.9 23.2 %collective-permute-start.13 = (bf16[512,640]{1,0:T(8,128)(2,1)S(1)}, bf16[512,640]{1,0:T(8,128)(2,1)S(1)}, u32[]{:S(2)}, u32[]{:S(2)}) collective-permute-start(bf16[512,640]{1,0:T(8,128)(2,1)S(1)} %collective-permute-done.12.refs_3_), channel_id=1, source_target_pairs={{16,0},{24,8},{32,16},{40,24},{48,32},{56,40},{64,48},{72,56},{80,... | collective-permute-start | bytes 1966088 | tf_op jit(solution)/shard_map/ppermute | solution.py:233
  84.9 23.2 %collective-permute-start.11 = (bf16[512,640]{1,0:T(8,128)(2,1)S(1)}, bf16[512,640]{1,0:T(8,128)(2,1)S(1)}, u32[]{:S(2)}, u32[]{:S(2)}) collective-permute-start(bf16[512,640]{1,0:T(8,128)(2,1)S(1)} %collective-permute-done.7.refs_0_), channel_id=1, source_target_pairs={{0,16},{8,24},{16,32},{24,40},{32,48},{40,56},{48,64},{56,72},{64,... | collective-permute-start | bytes 1966088 | tf_op jit(solution)/shard_map/ppermute | solution.py:233
  105.8 5.5 %copy-start.2 = (f32[40,128,128]{2,1,0:T(8,128)}, f32[40,128,128]{2,1,0:T(8,128)S(1)}, u32[]{:S(2)}) copy-start(f32[40,128,128]{2,1,0:T(8,128)S(1)} %get-tuple-element.43.refs_2_) | copy-start | bytes 7864324
  111.3 16.4 %collective-permute-start.16 = (bf16[20,128,128]{2,1,0:T(8,128)(2,1)}, bf16[20,128,128]{2,1,0:T(8,128)(2,1)S(1)}, u32[]{:S(2)}, u32[]{:S(2)}) collective-permute-start(bf16[20,128,128]{2,1,0:T(8,128)(2,1)} %get-tuple-element.47), channel_id=1, source_target_pairs={{0,8},{8,0},{16,24},{24,16},{32,40},{40,32},{48,56},{56,48},{64,72... | collective-permute-start | bytes 1966088 | tf_op jit(solution)/shard_map/ppermute | solution.py:240
  116.1 11.6 %collective-permute-start.17 = (f32[20,8,128]{2,1,0:T(8,128)S(1)}, f32[20,8,128]{2,1,0:T(8,128)S(1)}, u32[]{:S(2)}, u32[]{:S(2)}) collective-permute-start(f32[20,8,128]{2,1,0:T(8,128)S(1)} %get-tuple-element.48), channel_id=1, source_target_pairs={{0,8},{8,0},{16,24},{24,16},{32,40},{40,32},{48,56},{56,48},{64,72... | collective-permute-start | bytes 245768 | tf_op jit(solution)/shard_map/ppermute | solution.py:240
  116.2 1.7 copy-start.3
  117.9 10.3 %slice-start = ((s8[6553600]{0:T(1024)(128)(4,1)}), s8[4194304]{0:T(1024)(128)(4,1)S(1)}, s32[]{:S(2)}) async-start(s8[6553600]{0:T(1024)(128)(4,1)} %bitcast.61), calls=%async_computation | async-start | bytes 8388608
  127.7 1.7 slice-start.1
  130.2 21.6 %collective-permute-start.18 = (bf16[256,1536]{1,0:T(8,128)(2,1)S(1)}, bf16[256,1536]{1,0:T(8,128)(2,1)S(1)}, u32[]{:S(2)}, u32[]{:S(2)}) collective-permute-start(bf16[256,1536]{1,0:T(8,128)(2,1)S(1)} %convolution_convert_fusion), channel_id=1, source_target_pairs={{0,4},{1,5},{2,6},{3,7},{4,0},{5,1},{6,2},{7,3},{8,12},{9,13},{10,... | collective-permute-start | bytes 2359304 | tf_op jit(solution)/shard_map/ppermute | solution.py:179
  133.8 13.4 %collective-permute-start.25 = (bf16[128,1792]{1,0:T(8,128)(2,1)S(1)}, bf16[128,1792]{1,0:T(8,128)(2,1)S(1)}, u32[]{:S(2)}, u32[]{:S(2)}) collective-permute-start(bf16[128,1792]{1,0:T(8,128)(2,1)S(1)} %convolution_convert_fusion.2), channel_id=1, source_target_pairs={{0,1},{1,2},{2,3},{3,0},{4,5},{5,6},{6,7},{7,4},{8,9},{9,10},{10,1... | collective-permute-start | bytes 1376264 | tf_op jit(solution)/shard_map/ppermute | solution.py:171
  135.8 14.3 %collective-permute-start.28 = (bf16[128,1792]{1,0:T(8,128)(2,1)S(1)}, bf16[128,1792]{1,0:T(8,128)(2,1)S(1)}, u32[]{:S(2)}, u32[]{:S(2)}) collective-permute-start(bf16[128,1792]{1,0:T(8,128)(2,1)S(1)} %convolution_convert_fusion.1), channel_id=1, source_target_pairs={{0,3},{1,0},{2,1},{3,2},{4,7},{5,4},{6,5},{7,6},{8,11},{9,8},{10,9... | collective-permute-start | bytes 1376264 | tf_op jit(solution)/shard_map/ppermute | solution.py:171
  147.7 18.8 %collective-permute-start.26 = (bf16[128,1792]{1,0:T(8,128)(2,1)S(1)}, bf16[128,1792]{1,0:T(8,128)(2,1)S(1)}, u32[]{:S(2)}, u32[]{:S(2)}) collective-permute-start(bf16[128,1792]{1,0:T(8,128)(2,1)S(1)} %add_convert_fusion.6), channel_id=1, source_target_pairs={{0,1},{1,2},{2,3},{3,0},{4,5},{5,6},{6,7},{7,4},{8,9},{9,10},{10,1... | collective-permute-start | bytes 1376264 | tf_op jit(solution)/shard_map/ppermute | solution.py:171
  150.7 19.3 %collective-permute-start.29 = (bf16[128,1792]{1,0:T(8,128)(2,1)S(1)}, bf16[128,1792]{1,0:T(8,128)(2,1)S(1)}, u32[]{:S(2)}, u32[]{:S(2)}) collective-permute-start(bf16[128,1792]{1,0:T(8,128)(2,1)S(1)} %add_convert_fusion.3), channel_id=1, source_target_pairs={{0,3},{1,0},{2,1},{3,2},{4,7},{5,4},{6,5},{7,6},{8,11},{9,8},{10,9... | collective-permute-start | bytes 1376264 | tf_op jit(solution)/shard_map/ppermute | solution.py:171
  152.7 8.4 %collective-permute-start.19 = (bf16[64,768]{1,0:T(8,128)(2,1)S(1)}, bf16[64,768]{1,0:T(8,128)(2,1)S(1)}, u32[]{:S(2)}, u32[]{:S(2)}) collective-permute-start(bf16[64,768]{1,0:T(8,128)(2,1)S(1)} %dynamic-slice_bitcast_fusion.2), channel_id=1, source_target_pairs={{0,1},{1,2},{2,3},{3,0},{4,5},{5,6},{6,7},{7,4},{8,9},{9,10},{10,1... | collective-permute-start | bytes 294920 | tf_op jit(solution)/shard_map/ppermute | solution.py:171
  155.0 11.4 %collective-permute-start.22 = (bf16[64,768]{1,0:T(8,128)(2,1)S(1)}, bf16[64,768]{1,0:T(8,128)(2,1)S(1)}, u32[]{:S(2)}, u32[]{:S(2)}) collective-permute-start(bf16[64,768]{1,0:T(8,128)(2,1)S(1)} %dynamic-slice_bitcast_fusion.1), channel_id=1, source_target_pairs={{0,3},{1,0},{2,1},{3,2},{4,7},{5,4},{6,5},{7,6},{8,11},{9,8},{10,9... | collective-permute-start | bytes 294920 | tf_op jit(solution)/shard_map/ppermute | solution.py:171
  161.1 9.0 %collective-permute-start.20 = (bf16[64,768]{1,0:T(8,128)(2,1)S(1)}, bf16[64,768]{1,0:T(8,128)(2,1)S(1)}, u32[]{:S(2)}, u32[]{:S(2)}) collective-permute-start(bf16[64,768]{1,0:T(8,128)(2,1)S(1)} %fusion.23), channel_id=1, source_target_pairs={{0,1},{1,2},{2,3},{3,0},{4,5},{5,6},{6,7},{7,4},{8,9},{9,10},{10,1... | collective-permute-start | bytes 294920 | tf_op jit(solution)/shard_map/ppermute | solution.py:171
  166.5 13.6 %collective-permute-start.23 = (bf16[64,768]{1,0:T(8,128)(2,1)S(1)}, bf16[64,768]{1,0:T(8,128)(2,1)S(1)}, u32[]{:S(2)}, u32[]{:S(2)}) collective-permute-start(bf16[64,768]{1,0:T(8,128)(2,1)S(1)} %fusion.20), channel_id=1, source_target_pairs={{0,3},{1,0},{2,1},{3,2},{4,7},{5,4},{6,5},{7,6},{8,11},{9,8},{10,9... | collective-permute-start | bytes 294920 | tf_op jit(solution)/shard_map/ppermute | solution.py:171
  166.6 9.3 %collective-permute-start.27 = (bf16[128,1792]{1,0:T(8,128)(2,1)S(1)}, bf16[128,1792]{1,0:T(8,128)(2,1)S(1)}, u32[]{:S(2)}, u32[]{:S(2)}) collective-permute-start(bf16[128,1792]{1,0:T(8,128)(2,1)S(1)} %add_convert_fusion.5), channel_id=1, source_target_pairs={{0,1},{1,2},{2,3},{3,0},{4,5},{5,6},{6,7},{7,4},{8,9},{9,10},{10,1... | collective-permute-start | bytes 1376264 | tf_op jit(solution)/shard_map/ppermute | solution.py:171
  170.0 9.8 %collective-permute-start.30 = (bf16[128,1792]{1,0:T(8,128)(2,1)S(1)}, bf16[128,1792]{1,0:T(8,128)(2,1)S(1)}, u32[]{:S(2)}, u32[]{:S(2)}) collective-permute-start(bf16[128,1792]{1,0:T(8,128)(2,1)S(1)} %add_convert_fusion.2), channel_id=1, source_target_pairs={{0,3},{1,0},{2,1},{3,2},{4,7},{5,4},{6,5},{7,6},{8,11},{9,8},{10,9... | collective-permute-start | bytes 1376264 | tf_op jit(solution)/shard_map/ppermute | solution.py:171
  170.2 10.1 %collective-permute-start.21 = (bf16[64,768]{1,0:T(8,128)(2,1)S(1)}, bf16[64,768]{1,0:T(8,128)(2,1)S(1)}, u32[]{:S(2)}, u32[]{:S(2)}) collective-permute-start(bf16[64,768]{1,0:T(8,128)(2,1)S(1)} %fusion.22), channel_id=1, source_target_pairs={{0,1},{1,2},{2,3},{3,0},{4,5},{5,6},{6,7},{7,4},{8,9},{9,10},{10,1... | collective-permute-start | bytes 294920 | tf_op jit(solution)/shard_map/ppermute | solution.py:171
  180.0 8.6 %collective-permute-start.31 = (bf16[64,3584]{1,0:T(8,128)(2,1)S(1)}, bf16[64,3584]{1,0:T(8,128)(2,1)S(1)}, u32[]{:S(2)}, u32[]{:S(2)}) collective-permute-start(bf16[64,3584]{1,0:T(8,128)(2,1)S(1)} %dynamic-slice_bitcast_fusion), channel_id=1, source_target_pairs={{0,4},{1,5},{2,6},{3,7},{4,0},{5,1},{6,2},{7,3},{8,12},{9,13},{10,... | collective-permute-start | bytes 1376264 | tf_op jit(solution)/shard_map/ppermute | solution.py:190
  180.1 5.9 %collective-permute-start.24 = (bf16[64,768]{1,0:T(8,128)(2,1)S(1)}, bf16[64,768]{1,0:T(8,128)(2,1)S(1)}, u32[]{:S(2)}, u32[]{:S(2)}) collective-permute-start(bf16[64,768]{1,0:T(8,128)(2,1)S(1)} %fusion.19), channel_id=1, source_target_pairs={{0,3},{1,0},{2,1},{3,2},{4,7},{5,4},{6,5},{7,6},{8,11},{9,8},{10,9... | collective-permute-start | bytes 294920 | tf_op jit(solution)/shard_map/ppermute | solution.py:171

commit v3 on v2

--- a/solution.py
+++ b/solution.py
@@ -12,11 +12,9 @@
 BS = 128
 KB = 16
 TAB = 16
-FIRST = 1536
 NZ = 8
 NX = 2
 NY = 4
-FIRST = 1536
 LOW = -1e30
 FACTOR = math.log2(math.e) / math.sqrt(HD)
 
@@ -118,7 +116,7 @@
 
 
 def finish_kernel(mixed, stats, mixed_other, stats_other, out):
-    heads = out.shape[1] // HD
+    heads, rows = out.shape[3] // HD, out.shape[2]
     for i in range(mixed.shape[0]):
         m0, l0 = stats[i, 0:1], stats[i, 1:2]
         m1, l1 = stats_other[i, 0:1], stats_other[i, 1:2]
@@ -128,7 +126,10 @@
         total = l0 * a0 + l1 * a1
         both = mixed[i] * (a0 / total) + mixed_other[i].astype(jnp.float32) * (a1 / total)
         qb, h = i // heads, i % heads
-        out[qb * BS : (qb + 1) * BS, h * HD : (h + 1) * HD] = both.T.astype(out.dtype)
+        done = both.T.astype(out.dtype)
+        for t in range(BS // rows):
+            x, y = divmod(qb * (BS // rows) + t, NY)
+            out[x, y, :, h * HD : (h + 1) * HD] = done[t * rows : (t + 1) * rows]
 
 
 def finish(own, other, shape):
@@ -148,54 +149,57 @@
     return lax.optimization_barrier((x,) + behind)[0] if behind else x
 
 
-def project(attended, weight, head):
+def over_x(a):
+    return lax.ppermute(a, "head", [(h, (h + NY) % (2 * NY)) for h in range(2 * NY)])
+
+
+def over_dp(a):
+    return lax.ppermute(a, "dp", [(0, 1), (1, 0)])
+
+
+def project(attended, weights, head, core):
     x, y = head // NY, head % NY
-    rows = attended.shape[0] // (2 * NY)
-    width = weight.shape[1]
-    tiles = attended.reshape(2, NY, rows, -1)
-    other_x = [(h, (h + NY) % (2 * NY)) for h in range(2 * NY)]
-
-    def part(a, lo, hi):
-        return jnp.dot(a, weight[:, lo:hi], preferred_element_type=jnp.float32)
+
+    def at(a, i):
+        return lax.dynamic_index_in_dim(a, i % NY, 0, False)
+
+    give = lax.dynamic_index_in_dim(attended, 1 - x, 0, False)
+    keep = lax.dynamic_index_in_dim(attended, x, 0, False)
+    order = (y - 1, y + 1, y + 2, y)
+    got = [over_x(jnp.concatenate([at(give, i) for i in pair])) for pair in (order[:2], order[2:])]
+    local = jnp.concatenate([at(keep, i) for i in order])
+
+    rows = got[0].shape[0]
+    base = [jnp.dot(local, pair[0], preferred_element_type=jnp.float32) for pair in weights]
+
+    def terms(n, acts, half):
+        part = jnp.dot(acts, weights[half][1], preferred_element_type=jnp.float32)
+        return jnp.split(part + base[half][n * rows : (n + 1) * rows], 2)
 
     def narrow(a):
         return a.astype(jnp.bfloat16)
 
-    def wide(a):
-        return a.astype(jnp.float32)
-
-    def ring(term, way):
-        perm = [(h, h // NY * NY + (h % NY + way) % NY) for h in range(2 * NY)]
-        acc = narrow(term((y - way) % NY))
-        for s in range(NY - 1):
-            acc = lax.ppermute(acc, "head", perm)
-            acc = narrow(wide(acc) + term((y - way * (s + 2)) % NY))
-        return acc
-
-    cut = FIRST
-    mid = cut + (width - cut) // 2
-    far = lax.dynamic_index_in_dim(tiles, 1 - x, 0, False).reshape(NY * rows, -1)
-    near = lax.dynamic_index_in_dim(tiles, x, 0, False).reshape(NY * rows, -1)
-    got = lax.ppermute(narrow(part(far, 0, cut)), "head", other_x)
-
-    def both(i):
-        return lax.dynamic_index_in_dim(tiles, i, 1, False).reshape(2 * rows, -1)
-
-    up = ring(lambda i: part(both(i), cut, mid), 1)
-    down = ring(lambda i: part(both(i), mid, width), -1)
-    half = narrow(wide(got) + part(near, 0, cut)).reshape(NY, rows, cut)
-    left = ring(lambda i: wide(lax.dynamic_index_in_dim(half[..., : cut // 2], i, 0, False)), 1)
-    right = ring(lambda i: wide(lax.dynamic_index_in_dim(half[..., cut // 2 :], i, 0, False)), -1)
-    late = jnp.concatenate([up, down], axis=1).reshape(2, rows, width - cut)
-    give = lax.ppermute(lax.dynamic_index_in_dim(late, 1 - x, 0, False), "head", other_x)
-    keep = lax.dynamic_index_in_dim(late, x, 0, False)
-    return jnp.concatenate([left, right, narrow(wide(give) + wide(keep))], axis=1)
+    def turn(a, way):
+        to = [(h, h // NY * NY + (h % NY + way) % NY) for h in range(2 * NY)]
+        return lax.ppermute(a, "head", to).astype(jnp.float32)
+
+    before, ahead = terms(0, got[0], 0)
+    before_down, ahead_down = terms(0, got[0], 1)
+    up, down, late = lax.optimization_barrier((narrow(before), narrow(ahead_down), got[1]))
+    over, own = terms(1, late, 0)
+    over_down, own_down = terms(1, late, 1)
+    up = narrow(turn(up, 1) + over)
+    down = narrow(turn(down, -1) + over_down)
+    for here, here_down in ((ahead, before_down), (own, own_down)):
+        up = narrow(turn(up, 1) + here)
+        down = narrow(turn(down, -1) + here_down)
+    return jnp.where(core == 0, jnp.concatenate([up, down], axis=1), jnp.concatenate([down, up], axis=1))
 
 
 def on_device(queries, keys, values, block_list, block_count, out_weight):
     rows, width = queries.shape
     per = rows // BS
-    blk, head = lax.axis_index("blk"), lax.axis_index("head")
+    blk, head, core = lax.axis_index("blk"), lax.axis_index("head"), lax.axis_index("dp")
     z, xh = blk // NX, blk % NX
     cross = [(b, b ^ 1) for b in range(NZ * NX)]
     up = [(b, (b + NX) % (NZ * NX)) for b in range(NZ * NX)]
@@ -231,6 +235,12 @@
             coming = ((s, *ups), (NZ - s, *downs))
         else:
             coming = ((s, lax.ppermute(ups[0], "blk", up), lax.ppermute(downs[1], "blk", down)),)
+        if s == 1:
+            half = out_weight.shape[1] // 2
+            held = after(out_weight, ups[0])
+            ours = lax.dynamic_slice_in_dim(held, core * half, half, 1)
+            rest = lax.dynamic_slice_in_dim(held, (1 - core) * half, half, 1)
+            fetched = over_x(ours)
         state = visit(stage, state)
         if s < NZ // 2:
             ups = tuple(after(a, state[1]) for a in ups)
@@ -239,8 +249,9 @@
     theirs = visit(stage, state, 1)
     other = [lax.ppermute(a, "blk", cross) for a in theirs]
     mine = visit(stage, state, 0)
-    attended = finish(mine, other, (rows, width))
-    return project(attended, out_weight, head)
+    swapped = over_dp(after(fetched, state[1]))
+    attended = finish(mine, other, (2, NY, rows // (2 * NY), width))
+    return project(attended, ((ours, fetched), (rest, swapped)), head, core)
 
 
 def solution(mesh):

time: 190 us -> 189 us (level)
  starting transfers between devices: 47.8 us -> 35.7 us
  Pallas kernels: 40.1 us -> 30.7 us
  matrix products: 6.01 us -> 14.7 us
  waiting for transfers between devices: 83.7 us -> 89.7 us
  local copies, waits for them, and re-layouts: 7.87 us -> 13.6 us
    ppermute x6, waiting for transfers between devices: 2.93 us -> 27.2 us  [on_device(): ups = tuple((lax.ppermute(a, 'blk', up) for a in ups))]
    ppermute x14 -> x10, waiting for transfers between devices: 34.8 us -> 16.1 us  [the longest x6 16.1 us: turn(): return lax.ppermute(a, 'head', to).astype(jnp.float32)]
    ppermute x1, waiting for transfers between devices: 0.01 us -> 14.9 us  [on_device(): lax.ppermute(ups[0], 'blk', up)]
    ppermute x6, waiting for transfers between devices: 29.2 us -> 16.4 us  [on_device(): downs = tuple((lax.ppermute(a, 'blk', down) for a in downs))]
    pallas_call x6, Pallas kernels: 39.7 us -> 30.3 us  [attend(): pl.pallas_call(functools.partial(attend_kernel, chunks, first, last, tile...]
    dot_general x10 -> x6, matrix products: 6.01 us -> 14.7 us  [the longest x4 10.4 us: terms(): part = jnp.dot(acts, weights[half][1], preferred_element_type=jnp.float32)]
    ppermute x14 -> x10, starting transfers between devices: 17.4 us -> 9.29 us  [the longest x6 6.55 us: turn(): return lax.ppermute(a, 'head', to).astype(jnp.float32)]
    ppermute x1, waiting for transfers between devices: 9.01 us -> 1.25 us  [on_device(): both = jnp.concatenate([queries, lax.ppermute(queries, 'blk', cross)])]
  transfers between devices with their start and end apart: 32 -> 28, of which waited for: 17 -> 14; matrix products, arithmetic and copies ran while one was open for 7% -> 14% of each run, Pallas kernels for 19% -> 16%
where the time goes in v3:
time: 189 us; the launch traced here: 188 us
  waiting for transfers between devices  89.7 us (47%)
  starting transfers between devices  35.7 us (19%)
  Pallas kernels  30.7 us (16%)
  matrix products  14.7 us (8%)
  local copies, waits for them, and re-layouts  13.6 us (7%)
  other arithmetic  3.4 us (2%)
    pallas_call x6, Pallas kernels, attend(): pl.pallas_call(functools.partial(attend_kernel, chunks, first, last, tile...  30.3 us
    ppermute x6, waiting for transfers between devices, on_device(): ups = tuple((lax.ppermute(a, 'blk', up) for a in ups))  27.2 us
    ppermute x6, waiting for transfers between devices, on_device(): downs = tuple((lax.ppermute(a, 'blk', down) for a in downs))  16.4 us
    ppermute x6, waiting for transfers between devices, turn(): return lax.ppermute(a, 'head', to).astype(jnp.float32)  16.1 us
    ppermute x6, starting transfers between devices, on_device(): ups = tuple((lax.ppermute(a, 'blk', up) for a in ups))  16.1 us
    ppermute x1, waiting for transfers between devices, on_device(): lax.ppermute(ups[0], 'blk', up)  14.9 us
    ppermute x2, waiting for transfers between devices, on_device(): other = [lax.ppermute(a, 'blk', cross) for a in theirs]  10.7 us
    dot_general x4, matrix products, terms(): part = jnp.dot(acts, weights[half][1], preferred_element_type=jnp.float32)  10.4 us
  transfers between devices with their start and end apart: 28, of which 14 were waited for; matrix products, arithmetic and copies ran while one was open for 14% of the time, Pallas kernels for 16%

profile of v3, /device:TPU:122, one launch (start us, length us, event | category | flops | bytes accessed | tf_op | source)
XLA Modules:
  0.0 188.2 jit_solution(7022723883630035619)
XLA Ops:
  0.0 3.1 %collective-permute-start.2 = (bf16[512,640]{1,0:T(8,128)(2,1)}, bf16[512,640]{1,0:T(8,128)(2,1)}, u32[]{:S(2)}, u32[]{:S(2)}) collective-permute-start(bf16[512,640]{1,0:T(8,128)(2,1)} %refs_0_.1), channel_id=1, source_target_pairs={{0,16},{8,24},{16,32},{24,40},{32,48},{40,56},{48,64},{56,72},{64,... | collective-permute-start | bytes 1966088 | tf_op jit(solution)/shard_map/ppermute | solution.py:233
  4.6 2.1 %collective-permute-start = (s32[4,17]{1,0:T(4,128)S(1)}, s32[4,17]{1,0:T(4,128)S(1)}, u32[]{:S(2)}, u32[]{:S(2)}) collective-permute-start(s32[4,17]{1,0:T(4,128)S(1)} %pad_add_fusion.4), channel_id=1, source_target_pairs={{0,8},{8,0},{16,24},{24,16},{32,40},{40,32},{48,56},{56,48},{64,72... | collective-permute-start | bytes 824 | tf_op jit(solution)/shard_map/ppermute | solution.py:208
  6.8 1.4 collective-permute-start.1
  8.2 1.2 constant_dynamic-update-slice_fusion.1
  9.4 0.8 fusion.26
  10.2 3.2 %collective-permute-start.5 = (bf16[512,640]{1,0:T(8,128)(2,1)}, bf16[512,640]{1,0:T(8,128)(2,1)}, u32[]{:S(2)}, u32[]{:S(2)}) collective-permute-start(bf16[512,640]{1,0:T(8,128)(2,1)} %refs_1_.1), channel_id=1, source_target_pairs={{0,16},{8,24},{16,32},{24,40},{32,48},{40,56},{48,64},{56,72},{64,... | collective-permute-start | bytes 1966088 | tf_op jit(solution)/shard_map/ppermute | solution.py:233
  14.8 3.8 %collective-permute-done.2.refs_0_ = bf16[512,640]{1,0:T(8,128)(2,1)} collective-permute-done((bf16[512,640]{1,0:T(8,128)(2,1)}, bf16[512,640]{1,0:T(8,128)(2,1)}, u32[]{:S(2)}, u32[]{:S(2)}) %collective-permute-start.2) | collective-permute-done | bytes 655392 | tf_op jit(solution)/shard_map/ppermute | solution.py:233
  18.6 3.9 %constant_dynamic-slice_fusion = bf16[640,2560]{1,0:T(8,128)(2,1)} fusion(bf16[640,5120]{1,0:T(8,128)(2,1)} %param.11, s32[]{:T(128)S(6)} %select_n.135), kind=kLoop, calls=%fused_computation.48 | loop fusion | bytes 6553604 | tf_op jit(solution)/shard_map/dynamic_slice | solution.py:241
  23.6 1.3 collective-permute-done.1
  24.8 1.2 constant_dynamic-update-slice_fusion.q
  26.0 5.5 %attend.6 = (f32[40,128,128]{2,1,0:T(8,128)S(1)}, f32[40,8,128]{2,1,0:T(8,128)S(1)}) custom-call(s32[1,8,4]{2,1,0:T(8,128)S(1)} %copy.35.flags, bf16[1024,640]{1,0:T(8,128)(2,1)S(1)} %constant_dynamic-update-slice_fusion.q, bf16[512,640]{1,0:T(8,128)(2,1)S(1)} %copy-done.1, bf16[512,640]{1,0:T(8,128)(2,1)S(1)} %copy-done), custom_call_target="tpu_custom_call" | custom-call | flops 4000000000 | bytes 4194304 | tf_op jit(solution)/shard_map/attend/pallas_call | solution.py:100
  31.5 3.2 %collective-permute-done.6.refs_3_ = bf16[512,640]{1,0:T(8,128)(2,1)S(1)} collective-permute-done((bf16[512,640]{1,0:T(8,128)(2,1)}, bf16[512,640]{1,0:T(8,128)(2,1)S(1)}, u32[]{:S(2)}, u32[]{:S(2)}) %collective-permute-start.6) | collective-permute-done | bytes 655392 | tf_op jit(solution)/shard_map/ppermute | solution.py:234
  34.8 1.5 collective-permute-start.3
  36.8 2.7 %collective-permute-start.9 = (bf16[512,640]{1,0:T(8,128)(2,1)}, bf16[512,640]{1,0:T(8,128)(2,1)S(1)}, u32[]{:S(2)}, u32[]{:S(2)}) collective-permute-start(bf16[512,640]{1,0:T(8,128)(2,1)} %collective-permute-done.5.refs_2_), channel_id=1, source_target_pairs={{0,16},{8,24},{16,32},{24,40},{32,48},{40,56},{48,64},{56,72},{64,... | collective-permute-start | bytes 1966088 | tf_op jit(solution)/shard_map/ppermute | solution.py:233
  39.6 6.8 %attend.7 = (f32[40,128,128]{2,1,0:T(8,128)S(1)}, f32[40,8,128]{2,1,0:T(8,128)S(1)}) custom-call(s32[2,8,4]{2,1,0:T(8,128)S(1)} %pad_add_fusion.flags, bf16[1024,640]{1,0:T(8,128)(2,1)S(1)} %constant_dynamic-update-slice_fusion.q, bf16[512,640]{1,0:T(8,128)(2,1)} %collective-permute-done.2.refs_0_, ...), custom_call_target="tpu_custom_call", output_to_operand_aliasing={{0}: (6, {}), {1}: (7, {})} | custom-call | flops 8000000000 | bytes 4194304 | tf_op jit(solution)/shard_map/attend/pallas_call | solution.py:100
  46.4 6.3 %collective-permute-done.3.refs_0_ = bf16[512,640]{1,0:T(8,128)(2,1)S(1)} collective-permute-done((bf16[512,640]{1,0:T(8,128)(2,1)}, bf16[512,640]{1,0:T(8,128)(2,1)S(1)}, u32[]{:S(2)}, u32[]{:S(2)}) %collective-permute-start.3) | collective-permute-done | bytes 655392 | tf_op jit(solution)/shard_map/ppermute | solution.py:233
  52.7 2.7 %collective-permute-start.7 = (bf16[512,640]{1,0:T(8,128)(2,1)S(1)}, bf16[512,640]{1,0:T(8,128)(2,1)}, u32[]{:S(2)}, u32[]{:S(2)}) collective-permute-start(bf16[512,640]{1,0:T(8,128)(2,1)S(1)} %collective-permute-done.3.refs_0_), channel_id=1, source_target_pairs={{0,16},{8,24},{16,32},{24,40},{32,48},{40,56},{48,64},{56,72},{64,... | collective-permute-start | bytes 1966088 | tf_op jit(solution)/shard_map/ppermute | solution.py:233
  55.4 11.3 %collective-permute-done.9.refs_2_ = bf16[512,640]{1,0:T(8,128)(2,1)S(1)} collective-permute-done((bf16[512,640]{1,0:T(8,128)(2,1)}, bf16[512,640]{1,0:T(8,128)(2,1)S(1)}, u32[]{:S(2)}, u32[]{:S(2)}) %collective-permute-start.9) | collective-permute-done | bytes 655392 | tf_op jit(solution)/shard_map/ppermute | solution.py:233
  66.7 2.7 %collective-permute-start.15 = (bf16[512,640]{1,0:T(8,128)(2,1)S(1)}, bf16[512,640]{1,0:T(8,128)(2,1)S(1)}, u32[]{:S(2)}, u32[]{:S(2)}) collective-permute-start(bf16[512,640]{1,0:T(8,128)(2,1)S(1)} %collective-permute-done.9.refs_2_), channel_id=1, source_target_pairs={{0,16},{8,24},{16,32},{24,40},{32,48},{40,56},{48,64},{56,72},{64,... | collective-permute-start | bytes 1966088 | tf_op jit(solution)/shard_map/ppermute | solution.py:233
  69.5 5.6 %attend.8 = (f32[40,128,128]{2,1,0:T(8,128)S(1)}, f32[40,8,128]{2,1,0:T(8,128)S(1)}) custom-call(s32[2,8,4]{2,1,0:T(8,128)S(1)} %pad_add_fusion.1.flags, bf16[1024,640]{1,0:T(8,128)(2,1)S(1)} %constant_dynamic-update-slice_fusion.q, bf16[512,640]{1,0:T(8,128)(2,1)S(1)} %collective-permute-done.3.refs_0_, ...), custom_call_target="tpu_custom_call", output_to_operand_aliasing={{0}: (6, {}), {1}: (7, {})} | custom-call | flops 8000000000 | bytes 4194304 | tf_op jit(solution)/shard_map/attend/pallas_call | solution.py:100
  75.1 5.8 %collective-permute-done.7.refs_0_ = bf16[512,640]{1,0:T(8,128)(2,1)} collective-permute-done((bf16[512,640]{1,0:T(8,128)(2,1)S(1)}, bf16[512,640]{1,0:T(8,128)(2,1)}, u32[]{:S(2)}, u32[]{:S(2)}) %collective-permute-start.7) | collective-permute-done | bytes 655392 | tf_op jit(solution)/shard_map/ppermute | solution.py:233
  80.9 13.2 %collective-permute-done.12.refs_3_ = bf16[512,640]{1,0:T(8,128)(2,1)S(1)} collective-permute-done((bf16[512,640]{1,0:T(8,128)(2,1)S(1)}, bf16[512,640]{1,0:T(8,128)(2,1)S(1)}, u32[]{:S(2)}, u32[]{:S(2)}) %collective-permute-start.12) | collective-permute-done | bytes 655392 | tf_op jit(solution)/shard_map/ppermute | solution.py:234
  94.1 6.8 %attend.9 = (f32[40,128,128]{2,1,0:T(8,128)S(1)}, f32[40,8,128]{2,1,0:T(8,128)S(1)}) custom-call(s32[2,8,4]{2,1,0:T(8,128)S(1)} %pad_add_fusion.2.flags, bf16[1024,640]{1,0:T(8,128)(2,1)S(1)} %constant_dynamic-update-slice_fusion.q, bf16[512,640]{1,0:T(8,128)(2,1)} %collective-permute-done.7.refs_0_, ...), custom_call_target="tpu_custom_call", output_to_operand_aliasing={{0}: (6, {}), {1}: (7, {})} | custom-call | flops 8000000000 | bytes 4194304 | tf_op jit(solution)/shard_map/attend/pallas_call | solution.py:100
  100.9 1.5 copy-done.2
  102.4 2.7 %collective-permute-start.11 = (bf16[512,640]{1,0:T(8,128)(2,1)}, bf16[512,640]{1,0:T(8,128)(2,1)S(1)}, u32[]{:S(2)}, u32[]{:S(2)}) collective-permute-start(bf16[512,640]{1,0:T(8,128)(2,1)} %collective-permute-done.7.refs_0_), channel_id=1, source_target_pairs={{0,16},{8,24},{16,32},{24,40},{32,48},{40,56},{48,64},{56,72},{64,... | collective-permute-start | bytes 1966088 | tf_op jit(solution)/shard_map/ppermute | solution.py:237
  105.2 14.9 %collective-permute-done.11.refs_0_ = bf16[512,640]{1,0:T(8,128)(2,1)S(1)} collective-permute-done((bf16[512,640]{1,0:T(8,128)(2,1)}, bf16[512,640]{1,0:T(8,128)(2,1)S(1)}, u32[]{:S(2)}, u32[]{:S(2)}) %collective-permute-start.11) | collective-permute-done | bytes 655392 | tf_op jit(solution)/shard_map/ppermute | solution.py:237
  120.1 3.1 %collective-permute-done.13.refs_1_ = bf16[512,640]{1,0:T(8,128)(2,1)S(1)} collective-permute-done((bf16[512,640]{1,0:T(8,128)(2,1)S(1)}, bf16[512,640]{1,0:T(8,128)(2,1)S(1)}, u32[]{:S(2)}, u32[]{:S(2)}) %collective-permute-start.13) | collective-permute-done | bytes 655392 | tf_op jit(solution)/shard_map/ppermute | solution.py:237
  123.2 1.7 copy-done.3
  125.0 4.4 %attend.11 = (bf16[20,128,128]{2,1,0:T(8,128)(2,1)}, f32[20,8,128]{2,1,0:T(8,128)S(1)}) custom-call(s32[1,8,4]{2,1,0:T(8,128)S(1)} %copy.34.flags, bf16[1024,640]{1,0:T(8,128)(2,1)S(1)} %constant_dynamic-update-slice_fusion.q, bf16[512,640]{1,0:T(8,128)(2,1)S(1)} %collective-permute-done.11.refs_0_, bf16[512,640]{1,0:T(8,128)(2,1)S(1)} %collective-permute-done.13.refs_1_, ...), custom_call_target="tpu_custom_call" | custom-call | flops 2000000000 | bytes 4194304 | tf_op jit(solution)/shard_map/attend/pallas_call | solution.py:100
  129.4 3.5 %collective-permute-start.17 = (f32[20,8,128]{2,1,0:T(8,128)S(1)}, f32[20,8,128]{2,1,0:T(8,128)S(1)}, u32[]{:S(2)}, u32[]{:S(2)}) collective-permute-start(f32[20,8,128]{2,1,0:T(8,128)S(1)} %get-tuple-element.53), channel_id=1, source_target_pairs={{0,8},{8,0},{16,24},{24,16},{32,40},{40,32},{48,56},{56,48},{64,72... | collective-permute-start | bytes 245768 | tf_op jit(solution)/shard_map/ppermute | solution.py:250
  132.9 1.7 copy-done.4
  134.6 1.1 attend.10
  135.7 10.7 %collective-permute-done.17.stats_other = f32[20,8,128]{2,1,0:T(8,128)S(1)} collective-permute-done((f32[20,8,128]{2,1,0:T(8,128)S(1)}, f32[20,8,128]{2,1,0:T(8,128)S(1)}, u32[]{:S(2)}, u32[]{:S(2)}) %collective-permute-start.17) | collective-permute-done | bytes 81952 | tf_op jit(solution)/shard_map/ppermute | solution.py:250
  147.6 1.6 collective-permute-start.21
  149.2 3.1 %fusion.10 = f32[256,2560]{1,0:T(8,128)S(1)} fusion(bf16[640,2560]{1,0:T(8,128)(2,1)} %constant_dynamic-slice_fusion, bf16[64,640]{1,0:T(8,128)(2,1)S(1)} %get-tuple-element.61, bf16[64,640]{1,0:T(8,128)(2,1)S(1)} %get-tuple-element.62, bf16[64,640]{1,0:T(8,128)(2,1)S(1)} %get-tuple-element.63, bf16[64,640]{1,0:T(8,128)(2,1)S(1)} %get-tuple-element.64), kind=kOutput, calls=%fused_computation.36 | convolution fusion | flops 840171520 | bytes 6225920 | tf_op jit(solution)/shard_map/dot_general | solution.py:173
  152.3 1.2 fusion
  153.5 2.6 %convolution_add_fusion.3 = f32[128,2560]{1,0:T(8,128)S(1)} fusion(bf16[128,640]{1,0:T(8,128)(2,1)S(1)} %collective-permute-done.18, bf16[640,2560]{1,0:T(8,128)(2,1)} %collective-permute-done.19, f32[256,2560]{1,0:T(8,128)S(1)} %fusion.10), kind=kOutput, calls=%fused_computation.4 | convolution fusion | flops 419758080 | bytes 6062080 | tf_op jit(solution)/shard_map/dot_general | solution.py:176
  156.2 2.6 %convolution_add_fusion.2 = f32[128,2560]{1,0:T(8,128)S(1)} fusion(bf16[128,640]{1,0:T(8,128)(2,1)S(1)} %collective-permute-done.18, bf16[640,2560]{1,0:T(8,128)(2,1)} %collective-permute-done.20, f32[256,2560]{1,0:T(8,128)S(1)} %fusion), kind=kOutput, calls=%fused_computation.3 | convolution fusion | flops 419758080 | bytes 6062080 | tf_op jit(solution)/shard_map/dot_general | solution.py:176
  159.1 1.8 collective-permute-start.25
  161.0 2.6 %convolution_add_fusion = f32[128,2560]{1,0:T(8,128)S(1)} fusion(bf16[128,640]{1,0:T(8,128)(2,1)S(1)} %collective-permute-done.21, bf16[640,2560]{1,0:T(8,128)(2,1)} %collective-permute-done.20, f32[256,2560]{1,0:T(8,128)S(1)} %fusion), kind=kOutput, calls=%fused_computation.1 | convolution fusion | flops 419758080 | bytes 6062080 | tf_op jit(solution)/shard_map/dot_general | solution.py:176
  163.6 2.6 %convolution_add_fusion.1 = f32[128,2560]{1,0:T(8,128)S(1)} fusion(bf16[128,640]{1,0:T(8,128)(2,1)S(1)} %collective-permute-done.21, bf16[640,2560]{1,0:T(8,128)(2,1)} %collective-permute-done.19, f32[256,2560]{1,0:T(8,128)S(1)} %fusion.10), kind=kOutput, calls=%fused_computation.2 | convolution fusion | flops 419758080 | bytes 6062080 | tf_op jit(solution)/shard_map/dot_general | solution.py:176
  166.2 1.9 %collective-permute-done.22 = bf16[64,2560]{1,0:T(8,128)(2,1)S(1)} collective-permute-done((bf16[64,2560]{1,0:T(8,128)(2,1)S(1)}, bf16[64,2560]{1,0:T(8,128)(2,1)S(1)}, u32[]{:S(2)}, u32[]{:S(2)}) %collective-permute-start.22) | collective-permute-done | bytes 327712 | tf_op jit(solution)/shard_map/ppermute | solution.py:184
  168.3 2.1 %collective-permute-start.26 = (bf16[64,2560]{1,0:T(8,128)(2,1)S(1)}, bf16[64,2560]{1,0:T(8,128)(2,1)S(1)}, u32[]{:S(2)}, u32[]{:S(2)}) collective-permute-start(bf16[64,2560]{1,0:T(8,128)(2,1)S(1)} %fusion.4), channel_id=1, source_target_pairs={{0,3},{1,0},{2,1},{3,2},{4,7},{5,4},{6,5},{7,6},{8,11},{9,8},{10,9... | collective-permute-start | bytes 983048 | tf_op jit(solution)/shard_map/ppermute | solution.py:184
  170.4 8.1 %collective-permute-done.23 = bf16[64,2560]{1,0:T(8,128)(2,1)S(1)} collective-permute-done((bf16[64,2560]{1,0:T(8,128)(2,1)S(1)}, bf16[64,2560]{1,0:T(8,128)(2,1)S(1)}, u32[]{:S(2)}, u32[]{:S(2)}) %collective-permute-start.23) | collective-permute-done | bytes 327712 | tf_op jit(solution)/shard_map/ppermute | solution.py:184
  178.8 2.2 %collective-permute-start.27 = (bf16[64,2560]{1,0:T(8,128)(2,1)S(1)}, bf16[64,2560]{1,0:T(8,128)(2,1)S(1)}, u32[]{:S(2)}, u32[]{:S(2)}) collective-permute-start(bf16[64,2560]{1,0:T(8,128)(2,1)S(1)} %fusion.3), channel_id=1, source_target_pairs={{0,3},{1,0},{2,1},{3,2},{4,7},{5,4},{6,5},{7,6},{8,11},{9,8},{10,9... | collective-permute-start | bytes 983048 | tf_op jit(solution)/shard_map/ppermute | solution.py:184
  181.0 4.8 %collective-permute-done.24 = bf16[64,2560]{1,0:T(8,128)(2,1)S(1)} collective-permute-done((bf16[64,2560]{1,0:T(8,128)(2,1)S(1)}, bf16[64,2560]{1,0:T(8,128)(2,1)S(1)}, u32[]{:S(2)}, u32[]{:S(2)}) %collective-permute-start.24) | collective-permute-done | bytes 327712 | tf_op jit(solution)/shard_map/ppermute | solution.py:184
  185.8 1.3 collective-permute-done.27
  187.2 1.0 maximum_select_fusion
  (77 shorter events, 6.7 us)
Async XLA Ops:
  0.0 18.6 %collective-permute-start.2 = (bf16[512,640]{1,0:T(8,128)(2,1)}, bf16[512,640]{1,0:T(8,128)(2,1)}, u32[]{:S(2)}, u32[]{:S(2)}) collective-permute-start(bf16[512,640]{1,0:T(8,128)(2,1)} %refs_0_.1), channel_id=1, source_target_pairs={{0,16},{8,24},{16,32},{24,40},{32,48},{40,56},{48,64},{56,72},{64,... | collective-permute-start | bytes 1966088 | tf_op jit(solution)/shard_map/ppermute | solution.py:233
  3.1 31.7 %collective-permute-start.4 = (bf16[512,640]{1,0:T(8,128)(2,1)}, bf16[512,640]{1,0:T(8,128)(2,1)}, u32[]{:S(2)}, u32[]{:S(2)}) collective-permute-start(bf16[512,640]{1,0:T(8,128)(2,1)} %refs_0_.1), channel_id=1, source_target_pairs={{16,0},{24,8},{32,16},{40,24},{48,32},{56,40},{64,48},{72,56},{80,... | collective-permute-start | bytes 1966088 | tf_op jit(solution)/shard_map/ppermute | solution.py:234
  4.6 5.5 %collective-permute-start = (s32[4,17]{1,0:T(4,128)S(1)}, s32[4,17]{1,0:T(4,128)S(1)}, u32[]{:S(2)}, u32[]{:S(2)}) collective-permute-start(s32[4,17]{1,0:T(4,128)S(1)} %pad_add_fusion.4), channel_id=1, source_target_pairs={{0,8},{8,0},{16,24},{24,16},{32,40},{40,32},{48,56},{56,48},{64,72... | collective-permute-start | bytes 824 | tf_op jit(solution)/shard_map/ppermute | solution.py:208
  6.8 18.1 %collective-permute-start.1 = (bf16[512,640]{1,0:T(8,128)(2,1)}, bf16[512,640]{1,0:T(8,128)(2,1)}, u32[]{:S(2)}, u32[]{:S(2)}) collective-permute-start(bf16[512,640]{1,0:T(8,128)(2,1)} %param.6), channel_id=1, source_target_pairs={{0,8},{8,0},{16,24},{24,16},{32,40},{40,32},{48,56},{56,48},{64,72... | collective-permute-start | bytes 1966088 | tf_op jit(solution)/shard_map/ppermute | solution.py:209
  8.2 26.6 %collective-permute-start.6 = (bf16[512,640]{1,0:T(8,128)(2,1)}, bf16[512,640]{1,0:T(8,128)(2,1)S(1)}, u32[]{:S(2)}, u32[]{:S(2)}) collective-permute-start(bf16[512,640]{1,0:T(8,128)(2,1)} %refs_1_.1), channel_id=1, source_target_pairs={{16,0},{24,8},{32,16},{40,24},{48,32},{56,40},{64,48},{72,56},{80,... | collective-permute-start | bytes 1966088 | tf_op jit(solution)/shard_map/ppermute | solution.py:234
  10.2 24.6 %collective-permute-start.5 = (bf16[512,640]{1,0:T(8,128)(2,1)}, bf16[512,640]{1,0:T(8,128)(2,1)}, u32[]{:S(2)}, u32[]{:S(2)}) collective-permute-start(bf16[512,640]{1,0:T(8,128)(2,1)} %refs_1_.1), channel_id=1, source_target_pairs={{0,16},{8,24},{16,32},{24,40},{32,48},{40,56},{48,64},{56,72},{64,... | collective-permute-start | bytes 1966088 | tf_op jit(solution)/shard_map/ppermute | solution.py:233
  14.7 11.3 %copy-start = (bf16[512,640]{1,0:T(8,128)(2,1)S(1)}, bf16[512,640]{1,0:T(8,128)(2,1)}, u32[]{:S(2)}) copy-start(bf16[512,640]{1,0:T(8,128)(2,1)} %refs_1_.1) | copy-start | bytes 1966084
  14.7 11.3 %copy-start.1 = (bf16[512,640]{1,0:T(8,128)(2,1)S(1)}, bf16[512,640]{1,0:T(8,128)(2,1)}, u32[]{:S(2)}) copy-start(bf16[512,640]{1,0:T(8,128)(2,1)} %refs_0_.1) | copy-start | bytes 1966084
  22.4 80.0 %collective-permute-start.19 = (bf16[640,2560]{1,0:T(8,128)(2,1)}, bf16[640,2560]{1,0:T(8,128)(2,1)}, u32[]{:S(2)}, u32[]{:S(2)}) collective-permute-start(bf16[640,2560]{1,0:T(8,128)(2,1)} %constant_dynamic-slice_fusion), channel_id=1, source_target_pairs={{0,4},{1,5},{2,6},{3,7},{4,0},{5,1},{6,2},{7,3},{8,12},{9,13},{10,... | collective-permute-start | bytes 9830408 | tf_op jit(solution)/shard_map/ppermute | solution.py:153
  34.8 17.9 %collective-permute-start.3 = (bf16[512,640]{1,0:T(8,128)(2,1)}, bf16[512,640]{1,0:T(8,128)(2,1)S(1)}, u32[]{:S(2)}, u32[]{:S(2)}) collective-permute-start(bf16[512,640]{1,0:T(8,128)(2,1)} %collective-permute-done.2.refs_0_), channel_id=1, source_target_pairs={{0,16},{8,24},{16,32},{24,40},{32,48},{40,56},{48,64},{56,72},{64,... | collective-permute-start | bytes 1966088 | tf_op jit(solution)/shard_map/ppermute | solution.py:233
  36.3 19.1 %collective-permute-start.8 = (bf16[512,640]{1,0:T(8,128)(2,1)}, bf16[512,640]{1,0:T(8,128)(2,1)S(1)}, u32[]{:S(2)}, u32[]{:S(2)}) collective-permute-start(bf16[512,640]{1,0:T(8,128)(2,1)} %collective-permute-done.4.refs_1_), channel_id=1, source_target_pairs={{16,0},{24,8},{32,16},{40,24},{48,32},{56,40},{64,48},{72,56},{80,... | collective-permute-start | bytes 1966088 | tf_op jit(solution)/shard_map/ppermute | solution.py:234
  36.8 29.9 %collective-permute-start.9 = (bf16[512,640]{1,0:T(8,128)(2,1)}, bf16[512,640]{1,0:T(8,128)(2,1)S(1)}, u32[]{:S(2)}, u32[]{:S(2)}) collective-permute-start(bf16[512,640]{1,0:T(8,128)(2,1)} %collective-permute-done.5.refs_2_), channel_id=1, source_target_pairs={{0,16},{8,24},{16,32},{24,40},{32,48},{40,56},{48,64},{56,72},{64,... | collective-permute-start | bytes 1966088 | tf_op jit(solution)/shard_map/ppermute | solution.py:233
  39.6 29.9 %collective-permute-start.10 = (bf16[512,640]{1,0:T(8,128)(2,1)S(1)}, bf16[512,640]{1,0:T(8,128)(2,1)S(1)}, u32[]{:S(2)}, u32[]{:S(2)}) collective-permute-start(bf16[512,640]{1,0:T(8,128)(2,1)S(1)} %collective-permute-done.6.refs_3_), channel_id=1, source_target_pairs={{16,0},{24,8},{32,16},{40,24},{48,32},{56,40},{64,48},{72,56},{80,... | collective-permute-start | bytes 1966088 | tf_op jit(solution)/shard_map/ppermute | solution.py:234
  52.7 28.2 %collective-permute-start.7 = (bf16[512,640]{1,0:T(8,128)(2,1)S(1)}, bf16[512,640]{1,0:T(8,128)(2,1)}, u32[]{:S(2)}, u32[]{:S(2)}) collective-permute-start(bf16[512,640]{1,0:T(8,128)(2,1)S(1)} %collective-permute-done.3.refs_0_), channel_id=1, source_target_pairs={{0,16},{8,24},{16,32},{24,40},{32,48},{40,56},{48,64},{56,72},{64,... | collective-permute-start | bytes 1966088 | tf_op jit(solution)/shard_map/ppermute | solution.py:233
  55.4 38.6 %collective-permute-start.14 = (bf16[512,640]{1,0:T(8,128)(2,1)S(1)}, bf16[512,640]{1,0:T(8,128)(2,1)S(1)}, u32[]{:S(2)}, u32[]{:S(2)}) collective-permute-start(bf16[512,640]{1,0:T(8,128)(2,1)S(1)} %collective-permute-done.8.refs_1_), channel_id=1, source_target_pairs={{16,0},{24,8},{32,16},{40,24},{48,32},{56,40},{64,48},{72,56},{80,... | collective-permute-start | bytes 1966088 | tf_op jit(solution)/shard_map/ppermute | solution.py:234
  66.7 27.3 %collective-permute-start.15 = (bf16[512,640]{1,0:T(8,128)(2,1)S(1)}, bf16[512,640]{1,0:T(8,128)(2,1)S(1)}, u32[]{:S(2)}, u32[]{:S(2)}) collective-permute-start(bf16[512,640]{1,0:T(8,128)(2,1)S(1)} %collective-permute-done.9.refs_2_), channel_id=1, source_target_pairs={{0,16},{8,24},{16,32},{24,40},{32,48},{40,56},{48,64},{56,72},{64,... | collective-permute-start | bytes 1966088 | tf_op jit(solution)/shard_map/ppermute | solution.py:233
  69.5 24.6 %collective-permute-start.12 = (bf16[512,640]{1,0:T(8,128)(2,1)S(1)}, bf16[512,640]{1,0:T(8,128)(2,1)S(1)}, u32[]{:S(2)}, u32[]{:S(2)}) collective-permute-start(bf16[512,640]{1,0:T(8,128)(2,1)S(1)} %collective-permute-done.10.refs_3_), channel_id=1, source_target_pairs={{16,0},{24,8},{32,16},{40,24},{48,32},{56,40},{64,48},{72,56},{80,... | collective-permute-start | bytes 1966088 | tf_op jit(solution)/shard_map/ppermute | solution.py:234
  100.9 1.5 copy-start.2
  102.4 53.7 %collective-permute-start.20 = (bf16[640,2560]{1,0:T(8,128)(2,1)}, bf16[640,2560]{1,0:T(8,128)(2,1)}, u32[]{:S(2)}, u32[]{:S(2)}) collective-permute-start(bf16[640,2560]{1,0:T(8,128)(2,1)} %collective-permute-done.19), channel_id=1, source_target_pairs={{0,128},{128,0},{1,129},{129,1},{2,130},{130,2},{3,131},{131,3},{4... | collective-permute-start | bytes 9830408 | tf_op jit(solution)/shard_map/ppermute | solution.py:157
  102.4 17.7 %collective-permute-start.11 = (bf16[512,640]{1,0:T(8,128)(2,1)}, bf16[512,640]{1,0:T(8,128)(2,1)S(1)}, u32[]{:S(2)}, u32[]{:S(2)}) collective-permute-start(bf16[512,640]{1,0:T(8,128)(2,1)} %collective-permute-done.7.refs_0_), channel_id=1, source_target_pairs={{0,16},{8,24},{16,32},{24,40},{32,48},{40,56},{48,64},{56,72},{64,... | collective-permute-start | bytes 1966088 | tf_op jit(solution)/shard_map/ppermute | solution.py:237
  105.2 18.1 %collective-permute-start.13 = (bf16[512,640]{1,0:T(8,128)(2,1)S(1)}, bf16[512,640]{1,0:T(8,128)(2,1)S(1)}, u32[]{:S(2)}, u32[]{:S(2)}) collective-permute-start(bf16[512,640]{1,0:T(8,128)(2,1)S(1)} %collective-permute-done.12.refs_3_), channel_id=1, source_target_pairs={{16,0},{24,8},{32,16},{40,24},{48,32},{56,40},{64,48},{72,56},{80,... | collective-permute-start | bytes 1966088 | tf_op jit(solution)/shard_map/ppermute | solution.py:237
  123.2 1.7 copy-start.3
  129.4 17.1 %collective-permute-start.16 = (bf16[20,128,128]{2,1,0:T(8,128)(2,1)}, bf16[20,128,128]{2,1,0:T(8,128)(2,1)S(1)}, u32[]{:S(2)}, u32[]{:S(2)}) collective-permute-start(bf16[20,128,128]{2,1,0:T(8,128)(2,1)} %get-tuple-element.52), channel_id=1, source_target_pairs={{0,8},{8,0},{16,24},{24,16},{32,40},{40,32},{48,56},{56,48},{64,72... | collective-permute-start | bytes 1966088 | tf_op jit(solution)/shard_map/ppermute | solution.py:250
  129.4 17.1 %collective-permute-start.17 = (f32[20,8,128]{2,1,0:T(8,128)S(1)}, f32[20,8,128]{2,1,0:T(8,128)S(1)}, u32[]{:S(2)}, u32[]{:S(2)}) collective-permute-start(f32[20,8,128]{2,1,0:T(8,128)S(1)} %get-tuple-element.53), channel_id=1, source_target_pairs={{0,8},{8,0},{16,24},{24,16},{32,40},{40,32},{48,56},{56,48},{64,72... | collective-permute-start | bytes 245768 | tf_op jit(solution)/shard_map/ppermute | solution.py:250
  132.9 1.7 copy-start.4
  146.4 5.8 %slice-start = ((s8[6553600]{0:T(1024)(128)(4,1)}), s8[2359296]{0:T(1024)(128)(4,1)S(1)}, s32[]{:S(2)}) async-start(s8[6553600]{0:T(1024)(128)(4,1)} %bitcast.34), calls=%async_computation | async-start | bytes 4718592
  146.8 5.5 %slice-start.1 = ((s8[6553600]{0:T(1024)(128)(4,1)}), s8[4194304]{0:T(1024)(128)(4,1)S(1)}, s32[]{:S(2)}) async-start(s8[6553600]{0:T(1024)(128)(4,1)} %bitcast.34), calls=%async_computation.1 | async-start | bytes 8388608
  147.0 6.6 %collective-permute-start.18 = (bf16[128,640]{1,0:T(8,128)(2,1)S(1)}, bf16[128,640]{1,0:T(8,128)(2,1)S(1)}, u32[]{:S(2)}, u32[]{:S(2)}) collective-permute-start(bf16[128,640]{1,0:T(8,128)(2,1)S(1)} %pad_maximum_fusion.1), channel_id=1, source_target_pairs={{0,4},{1,5},{2,6},{3,7},{4,0},{5,1},{6,2},{7,3},{8,12},{9,13},{10,... | collective-permute-start | bytes 491528 | tf_op jit(solution)/shard_map/ppermute | solution.py:153
  147.6 11.2 %collective-permute-start.21 = (bf16[128,640]{1,0:T(8,128)(2,1)S(1)}, bf16[128,640]{1,0:T(8,128)(2,1)S(1)}, u32[]{:S(2)}, u32[]{:S(2)}) collective-permute-start(bf16[128,640]{1,0:T(8,128)(2,1)S(1)} %pad_maximum_fusion.2), channel_id=1, source_target_pairs={{0,4},{1,5},{2,6},{3,7},{4,0},{5,1},{6,2},{7,3},{8,12},{9,13},{10,... | collective-permute-start | bytes 491528 | tf_op jit(solution)/shard_map/ppermute | solution.py:153
  158.9 9.2 %collective-permute-start.22 = (bf16[64,2560]{1,0:T(8,128)(2,1)S(1)}, bf16[64,2560]{1,0:T(8,128)(2,1)S(1)}, u32[]{:S(2)}, u32[]{:S(2)}) collective-permute-start(bf16[64,2560]{1,0:T(8,128)(2,1)S(1)} %split.63), channel_id=1, source_target_pairs={{0,1},{1,2},{2,3},{3,0},{4,5},{5,6},{6,7},{7,4},{8,9},{9,10},{10,1... | collective-permute-start | bytes 983048 | tf_op jit(solution)/shard_map/ppermute | solution.py:184
  159.1 9.1 %collective-permute-start.25 = (bf16[64,2560]{1,0:T(8,128)(2,1)S(1)}, bf16[64,2560]{1,0:T(8,128)(2,1)S(1)}, u32[]{:S(2)}, u32[]{:S(2)}) collective-permute-start(bf16[64,2560]{1,0:T(8,128)(2,1)S(1)} %split.62), channel_id=1, source_target_pairs={{0,3},{1,0},{2,1},{3,2},{4,7},{5,4},{6,5},{7,6},{8,11},{9,8},{10,9... | collective-permute-start | bytes 983048 | tf_op jit(solution)/shard_map/ppermute | solution.py:184
  168.2 10.4 %collective-permute-start.23 = (bf16[64,2560]{1,0:T(8,128)(2,1)S(1)}, bf16[64,2560]{1,0:T(8,128)(2,1)S(1)}, u32[]{:S(2)}, u32[]{:S(2)}) collective-permute-start(bf16[64,2560]{1,0:T(8,128)(2,1)S(1)} %fusion.7), channel_id=1, source_target_pairs={{0,1},{1,2},{2,3},{3,0},{4,5},{5,6},{6,7},{7,4},{8,9},{9,10},{10,1... | collective-permute-start | bytes 983048 | tf_op jit(solution)/shard_map/ppermute | solution.py:184
  168.3 10.4 %collective-permute-start.26 = (bf16[64,2560]{1,0:T(8,128)(2,1)S(1)}, bf16[64,2560]{1,0:T(8,128)(2,1)S(1)}, u32[]{:S(2)}, u32[]{:S(2)}) collective-permute-start(bf16[64,2560]{1,0:T(8,128)(2,1)S(1)} %fusion.4), channel_id=1, source_target_pairs={{0,3},{1,0},{2,1},{3,2},{4,7},{5,4},{6,5},{7,6},{8,11},{9,8},{10,9... | collective-permute-start | bytes 983048 | tf_op jit(solution)/shard_map/ppermute | solution.py:184
  178.6 7.2 %collective-permute-start.24 = (bf16[64,2560]{1,0:T(8,128)(2,1)S(1)}, bf16[64,2560]{1,0:T(8,128)(2,1)S(1)}, u32[]{:S(2)}, u32[]{:S(2)}) collective-permute-start(bf16[64,2560]{1,0:T(8,128)(2,1)S(1)} %fusion.6), channel_id=1, source_target_pairs={{0,1},{1,2},{2,3},{3,0},{4,5},{5,6},{6,7},{7,4},{8,9},{9,10},{10,1... | collective-permute-start | bytes 983048 | tf_op jit(solution)/shard_map/ppermute | solution.py:184
  178.8 8.4 %collective-permute-start.27 = (bf16[64,2560]{1,0:T(8,128)(2,1)S(1)}, bf16[64,2560]{1,0:T(8,128)(2,1)S(1)}, u32[]{:S(2)}, u32[]{:S(2)}) collective-permute-start(bf16[64,2560]{1,0:T(8,128)(2,1)S(1)} %fusion.3), channel_id=1, source_target_pairs={{0,3},{1,0},{2,1},{3,2},{4,7},{5,4},{6,5},{7,6},{8,11},{9,8},{10,9... | collective-permute-start | bytes 983048 | tf_op jit(solution)/shard_map/ppermute | solution.py:184

commit v4 on v3

--- a/solution.py
+++ b/solution.py
@@ -248,8 +248,8 @@
         stage = coming
     theirs = visit(stage, state, 1)
     other = [lax.ppermute(a, "blk", cross) for a in theirs]
-    mine = visit(stage, state, 0)
-    swapped = over_dp(after(fetched, state[1]))
+    mine = visit(stage, (state[0], after(state[1], theirs[1])), 0)
+    swapped = over_dp(after(fetched, theirs[1]))
     attended = finish(mine, other, (2, NY, rows // (2 * NY), width))
     return project(attended, ((ours, fetched), (rest, swapped)), head, core)
 

time: 189 us -> 176 us (0.931)
  Pallas kernels: 30.7 us -> 21.8 us
  local copies, waits for them, and re-layouts: 13.6 us -> 10.4 us
  starting transfers between devices: 35.7 us -> 32.9 us
    pallas_call x6, Pallas kernels: 30.3 us -> 20.2 us  [attend(): pl.pallas_call(functools.partial(attend_kernel, chunks, first, last, tile...]
    ppermute x1, waiting for transfers between devices: 14.9 us -> 8.45 us  [on_device(): lax.ppermute(ups[0], 'blk', up)]
    ppermute x6, waiting for transfers between devices: 27.2 us -> 31.9 us  [on_device(): ups = tuple((lax.ppermute(a, 'blk', up) for a in ups))]
    ppermute x6, starting transfers between devices: 16.1 us -> 11.6 us  [on_device(): ups = tuple((lax.ppermute(a, 'blk', up) for a in ups))]
    unnamed x23 -> x21, local copies, waits for them, and re-layouts: 6.83 us -> 3.55 us
    ppermute x2, waiting for transfers between devices: 10.7 us -> 13.5 us  [on_device(): other = [lax.ppermute(a, 'blk', cross) for a in theirs]]
    ppermute x6, starting transfers between devices: 0.52 us -> 2.96 us  [on_device(): downs = tuple((lax.ppermute(a, 'blk', down) for a in downs))]
  transfers between devices with their start and end apart: 28 -> 28, of which waited for: 14 -> 16; matrix products, arithmetic and copies ran while one was open for 14% -> 15% of each run, Pallas kernels for 16% -> 13%
where the time goes in v4:
time: 176 us; the launch traced here: 174 us
  waiting for transfers between devices  89.8 us (51%)
  starting transfers between devices  32.9 us (19%)
  Pallas kernels  21.8 us (12%)
  matrix products  15 us (9%)
  local copies, waits for them, and re-layouts  10.4 us (6%)
  other arithmetic  3.41 us (2%)
    ppermute x6, waiting for transfers between devices, on_device(): ups = tuple((lax.ppermute(a, 'blk', up) for a in ups))  31.9 us
    pallas_call x6, Pallas kernels, attend(): pl.pallas_call(functools.partial(attend_kernel, chunks, first, last, tile...  20.2 us
    ppermute x6, waiting for transfers between devices, on_device(): downs = tuple((lax.ppermute(a, 'blk', down) for a in downs))  16.1 us
    ppermute x6, waiting for transfers between devices, turn(): return lax.ppermute(a, 'head', to).astype(jnp.float32)  14.5 us
    ppermute x2, waiting for transfers between devices, on_device(): other = [lax.ppermute(a, 'blk', cross) for a in theirs]  13.5 us
    ppermute x6, starting transfers between devices, on_device(): ups = tuple((lax.ppermute(a, 'blk', up) for a in ups))  11.6 us
    dot_general x4, matrix products, terms(): part = jnp.dot(acts, weights[half][1], preferred_element_type=jnp.float32)  10.7 us
    ppermute x1, waiting for transfers between devices, on_device(): lax.ppermute(ups[0], 'blk', up)  8.45 us
  transfers between devices with their start and end apart: 28, of which 16 were waited for; matrix products, arithmetic and copies ran while one was open for 15% of the time, Pallas kernels for 13%

profile of v4, /device:TPU:122, one launch (start us, length us, event | category | flops | bytes accessed | tf_op | source)
XLA Modules:
  0.0 173.6 jit_solution(14927878538984817147)
XLA Ops:
  0.0 3.1 %collective-permute-start.2 = (bf16[512,640]{1,0:T(8,128)(2,1)}, bf16[512,640]{1,0:T(8,128)(2,1)}, u32[]{:S(2)}, u32[]{:S(2)}) collective-permute-start(bf16[512,640]{1,0:T(8,128)(2,1)} %refs_0_.1), channel_id=1, source_target_pairs={{0,16},{8,24},{16,32},{24,40},{32,48},{40,56},{48,64},{56,72},{64,... | collective-permute-start | bytes 1966088 | tf_op jit(solution)/shard_map/ppermute | solution.py:233
  3.9 0.8 pad_add_fusion.4
  4.6 2.1 %collective-permute-start = (s32[4,17]{1,0:T(4,128)S(1)}, s32[4,17]{1,0:T(4,128)S(1)}, u32[]{:S(2)}, u32[]{:S(2)}) collective-permute-start(s32[4,17]{1,0:T(4,128)S(1)} %pad_add_fusion.4), channel_id=1, source_target_pairs={{0,8},{8,0},{16,24},{24,16},{32,40},{40,32},{48,56},{56,48},{64,72... | collective-permute-start | bytes 824 | tf_op jit(solution)/shard_map/ppermute | solution.py:208
  6.8 1.4 collective-permute-start.1
  8.2 0.8 fusion.26
  8.9 1.1 constant_dynamic-update-slice_fusion.1
  10.1 3.3 %collective-permute-start.5 = (bf16[512,640]{1,0:T(8,128)(2,1)}, bf16[512,640]{1,0:T(8,128)(2,1)}, u32[]{:S(2)}, u32[]{:S(2)}) collective-permute-start(bf16[512,640]{1,0:T(8,128)(2,1)} %refs_1_.1), channel_id=1, source_target_pairs={{0,16},{8,24},{16,32},{24,40},{32,48},{40,56},{48,64},{56,72},{64,... | collective-permute-start | bytes 1966088 | tf_op jit(solution)/shard_map/ppermute | solution.py:233
  15.1 3.5 %collective-permute-done.2.refs_0_ = bf16[512,640]{1,0:T(8,128)(2,1)} collective-permute-done((bf16[512,640]{1,0:T(8,128)(2,1)}, bf16[512,640]{1,0:T(8,128)(2,1)}, u32[]{:S(2)}, u32[]{:S(2)}) %collective-permute-start.2) | collective-permute-done | bytes 655392 | tf_op jit(solution)/shard_map/ppermute | solution.py:233
  18.6 3.8 %constant_dynamic-slice_fusion = bf16[640,2560]{1,0:T(8,128)(2,1)} fusion(bf16[640,5120]{1,0:T(8,128)(2,1)} %param.11, s32[]{:T(128)S(6)} %select_n.135), kind=kLoop, calls=%fused_computation.48 | loop fusion | bytes 6553604 | tf_op jit(solution)/shard_map/dynamic_slice | solution.py:241
  23.3 1.5 collective-permute-done.1
  24.8 1.2 constant_dynamic-update-slice_fusion.q
  26.0 4.3 %attend.6 = (f32[40,128,128]{2,1,0:T(8,128)S(1)}, f32[40,8,128]{2,1,0:T(8,128)S(1)}) custom-call(s32[1,8,4]{2,1,0:T(8,128)S(1)} %copy.35.flags, bf16[1024,640]{1,0:T(8,128)(2,1)S(1)} %constant_dynamic-update-slice_fusion.q, bf16[512,640]{1,0:T(8,128)(2,1)S(1)} %copy-done.1, bf16[512,640]{1,0:T(8,128)(2,1)S(1)} %copy-done), custom_call_target="tpu_custom_call" | custom-call | flops 4000000000 | bytes 4194304 | tf_op jit(solution)/shard_map/attend/pallas_call | solution.py:100
  30.3 4.4 %collective-permute-done.6.refs_3_ = bf16[512,640]{1,0:T(8,128)(2,1)S(1)} collective-permute-done((bf16[512,640]{1,0:T(8,128)(2,1)}, bf16[512,640]{1,0:T(8,128)(2,1)S(1)}, u32[]{:S(2)}, u32[]{:S(2)}) %collective-permute-start.6) | collective-permute-done | bytes 655392 | tf_op jit(solution)/shard_map/ppermute | solution.py:234
  35.2 1.6 collective-permute-start.8
  36.8 1.6 collective-permute-start.9
  38.8 4.4 %attend.7 = (f32[40,128,128]{2,1,0:T(8,128)S(1)}, f32[40,8,128]{2,1,0:T(8,128)S(1)}) custom-call(s32[2,8,4]{2,1,0:T(8,128)S(1)} %pad_add_fusion.flags, bf16[1024,640]{1,0:T(8,128)(2,1)S(1)} %constant_dynamic-update-slice_fusion.q, bf16[512,640]{1,0:T(8,128)(2,1)} %collective-permute-done.2.refs_0_, ...), custom_call_target="tpu_custom_call", output_to_operand_aliasing={{0}: (6, {}), {1}: (7, {})} | custom-call | flops 8000000000 | bytes 4194304 | tf_op jit(solution)/shard_map/attend/pallas_call | solution.py:100
  43.3 9.4 %collective-permute-done.3.refs_0_ = bf16[512,640]{1,0:T(8,128)(2,1)S(1)} collective-permute-done((bf16[512,640]{1,0:T(8,128)(2,1)}, bf16[512,640]{1,0:T(8,128)(2,1)S(1)}, u32[]{:S(2)}, u32[]{:S(2)}) %collective-permute-start.3) | collective-permute-done | bytes 655392 | tf_op jit(solution)/shard_map/ppermute | solution.py:233
  52.7 1.6 collective-permute-start.7
  54.7 12.0 %collective-permute-done.9.refs_2_ = bf16[512,640]{1,0:T(8,128)(2,1)S(1)} collective-permute-done((bf16[512,640]{1,0:T(8,128)(2,1)}, bf16[512,640]{1,0:T(8,128)(2,1)S(1)}, u32[]{:S(2)}, u32[]{:S(2)}) %collective-permute-start.9) | collective-permute-done | bytes 655392 | tf_op jit(solution)/shard_map/ppermute | solution.py:233
  66.7 1.6 collective-permute-start.15
  68.8 5.6 %attend.8 = (f32[40,128,128]{2,1,0:T(8,128)S(1)}, f32[40,8,128]{2,1,0:T(8,128)S(1)}) custom-call(s32[2,8,4]{2,1,0:T(8,128)S(1)} %pad_add_fusion.1.flags, bf16[1024,640]{1,0:T(8,128)(2,1)S(1)} %constant_dynamic-update-slice_fusion.q, bf16[512,640]{1,0:T(8,128)(2,1)S(1)} %collective-permute-done.3.refs_0_, ...), custom_call_target="tpu_custom_call", output_to_operand_aliasing={{0}: (6, {}), {1}: (7, {})} | custom-call | flops 8000000000 | bytes 4194304 | tf_op jit(solution)/shard_map/attend/pallas_call | solution.py:100
  74.4 6.4 %collective-permute-done.7.refs_0_ = bf16[512,640]{1,0:T(8,128)(2,1)S(1)} collective-permute-done((bf16[512,640]{1,0:T(8,128)(2,1)S(1)}, bf16[512,640]{1,0:T(8,128)(2,1)S(1)}, u32[]{:S(2)}, u32[]{:S(2)}) %collective-permute-start.7) | collective-permute-done | bytes 655392 | tf_op jit(solution)/shard_map/ppermute | solution.py:233
  80.8 1.6 collective-permute-start.11
  82.4 11.7 %collective-permute-done.12.refs_3_ = bf16[512,640]{1,0:T(8,128)(2,1)S(1)} collective-permute-done((bf16[512,640]{1,0:T(8,128)(2,1)S(1)}, bf16[512,640]{1,0:T(8,128)(2,1)S(1)}, u32[]{:S(2)}, u32[]{:S(2)}) %collective-permute-start.12) | collective-permute-done | bytes 655392 | tf_op jit(solution)/shard_map/ppermute | solution.py:234
  94.8 3.2 %attend.9 = (f32[40,128,128]{2,1,0:T(8,128)S(1)}, f32[40,8,128]{2,1,0:T(8,128)S(1)}) custom-call(s32[2,8,4]{2,1,0:T(8,128)S(1)} %pad_add_fusion.2.flags, bf16[1024,640]{1,0:T(8,128)(2,1)S(1)} %constant_dynamic-update-slice_fusion.q, bf16[512,640]{1,0:T(8,128)(2,1)S(1)} %collective-permute-done.7.refs_0_, ...), custom_call_target="tpu_custom_call", output_to_operand_aliasing={{0}: (6, {}), {1}: (7, {})} | custom-call | flops 8000000000 | bytes 4194304 | tf_op jit(solution)/shard_map/attend/pallas_call | solution.py:100
  98.0 8.4 %collective-permute-done.11.refs_0_ = bf16[512,640]{1,0:T(8,128)(2,1)S(1)} collective-permute-done((bf16[512,640]{1,0:T(8,128)(2,1)S(1)}, bf16[512,640]{1,0:T(8,128)(2,1)S(1)}, u32[]{:S(2)}, u32[]{:S(2)}) %collective-permute-start.11) | collective-permute-done | bytes 655392 | tf_op jit(solution)/shard_map/ppermute | solution.py:237
  106.5 3.2 %collective-permute-done.13.refs_1_ = bf16[512,640]{1,0:T(8,128)(2,1)S(1)} collective-permute-done((bf16[512,640]{1,0:T(8,128)(2,1)S(1)}, bf16[512,640]{1,0:T(8,128)(2,1)S(1)}, u32[]{:S(2)}, u32[]{:S(2)}) %collective-permute-start.13) | collective-permute-done | bytes 655392 | tf_op jit(solution)/shard_map/ppermute | solution.py:237
  109.7 1.1 attend.10
  110.9 3.0 %collective-permute-start.16 = (bf16[20,128,128]{2,1,0:T(8,128)(2,1)S(1)}, bf16[20,128,128]{2,1,0:T(8,128)(2,1)}, u32[]{:S(2)}, u32[]{:S(2)}) collective-permute-start(bf16[20,128,128]{2,1,0:T(8,128)(2,1)S(1)} %get-tuple-element.55), channel_id=1, source_target_pairs={{0,8},{8,0},{16,24},{24,16},{32,40},{40,32},{48,56},{56,48},{64,72... | collective-permute-start | bytes 1966088 | tf_op jit(solution)/shard_map/ppermute | solution.py:250
  114.5 1.7 %copy-done.3 = f32[40,128,128]{2,1,0:T(8,128)S(1)} copy-done((f32[40,128,128]{2,1,0:T(8,128)S(1)}, f32[40,128,128]{2,1,0:T(8,128)}, u32[]{:S(2)}) %copy-start.3) | copy-done | bytes 2621464
  116.2 1.5 attend.11
  117.8 13.5 %collective-permute-done.17.stats_other = f32[20,8,128]{2,1,0:T(8,128)S(1)} collective-permute-done((f32[20,8,128]{2,1,0:T(8,128)S(1)}, f32[20,8,128]{2,1,0:T(8,128)S(1)}, u32[]{:S(2)}, u32[]{:S(2)}) %collective-permute-start.17) | collective-permute-done | bytes 81952 | tf_op jit(solution)/shard_map/ppermute | solution.py:250
  131.3 1.6 finish.1
  133.1 1.2 collective-permute-start.18
  134.3 1.0 collective-permute-start.21
  135.3 3.1 %fusion.10 = f32[256,2560]{1,0:T(8,128)S(1)} fusion(bf16[640,2560]{1,0:T(8,128)(2,1)} %constant_dynamic-slice_fusion, bf16[64,640]{1,0:T(8,128)(2,1)S(1)} %get-tuple-element.63, bf16[64,640]{1,0:T(8,128)(2,1)S(1)} %get-tuple-element.64, bf16[64,640]{1,0:T(8,128)(2,1)S(1)} %get-tuple-element.65, bf16[64,640]{1,0:T(8,128)(2,1)S(1)} %get-tuple-element.66), kind=kOutput, calls=%fused_computation.36 | convolution fusion | flops 840171520 | bytes 6225920 | tf_op jit(solution)/shard_map/dot_general | solution.py:173
  138.4 1.2 fusion
  140.3 2.7 %convolution_add_fusion.3 = f32[128,2560]{1,0:T(8,128)S(1)} fusion(bf16[128,640]{1,0:T(8,128)(2,1)S(1)} %collective-permute-done.18, bf16[640,2560]{1,0:T(8,128)(2,1)} %collective-permute-done.19, f32[256,2560]{1,0:T(8,128)S(1)} %fusion.10), kind=kOutput, calls=%fused_computation.4 | convolution fusion | flops 419758080 | bytes 6062080 | tf_op jit(solution)/shard_map/dot_general | solution.py:176
  143.0 2.7 %convolution_add_fusion.2 = f32[128,2560]{1,0:T(8,128)S(1)} fusion(bf16[128,640]{1,0:T(8,128)(2,1)S(1)} %collective-permute-done.18, bf16[640,2560]{1,0:T(8,128)(2,1)} %collective-permute-done.20, f32[256,2560]{1,0:T(8,128)S(1)} %fusion), kind=kOutput, calls=%fused_computation.3 | convolution fusion | flops 419758080 | bytes 6062080 | tf_op jit(solution)/shard_map/dot_general | solution.py:176
  146.0 1.8 %collective-permute-start.25 = (bf16[64,2560]{1,0:T(8,128)(2,1)S(1)}, bf16[64,2560]{1,0:T(8,128)(2,1)S(1)}, u32[]{:S(2)}, u32[]{:S(2)}) collective-permute-start(bf16[64,2560]{1,0:T(8,128)(2,1)S(1)} %split.62), channel_id=1, source_target_pairs={{0,3},{1,0},{2,1},{3,2},{4,7},{5,4},{6,5},{7,6},{8,11},{9,8},{10,9... | collective-permute-start | bytes 983048 | tf_op jit(solution)/shard_map/ppermute | solution.py:184
  147.8 2.7 %convolution_add_fusion = f32[128,2560]{1,0:T(8,128)S(1)} fusion(bf16[128,640]{1,0:T(8,128)(2,1)S(1)} %collective-permute-done.21, bf16[640,2560]{1,0:T(8,128)(2,1)} %collective-permute-done.20, f32[256,2560]{1,0:T(8,128)S(1)} %fusion), kind=kOutput, calls=%fused_computation.1 | convolution fusion | flops 419758080 | bytes 6062080 | tf_op jit(solution)/shard_map/dot_general | solution.py:176
  150.5 2.7 %convolution_add_fusion.1 = f32[128,2560]{1,0:T(8,128)S(1)} fusion(bf16[128,640]{1,0:T(8,128)(2,1)S(1)} %collective-permute-done.21, bf16[640,2560]{1,0:T(8,128)(2,1)} %collective-permute-done.19, f32[256,2560]{1,0:T(8,128)S(1)} %fusion.10), kind=kOutput, calls=%fused_computation.2 | convolution fusion | flops 419758080 | bytes 6062080 | tf_op jit(solution)/shard_map/dot_general | solution.py:176
  154.0 1.6 collective-permute-start.23
  156.2 5.6 %collective-permute-done.23 = bf16[64,2560]{1,0:T(8,128)(2,1)S(1)} collective-permute-done((bf16[64,2560]{1,0:T(8,128)(2,1)S(1)}, bf16[64,2560]{1,0:T(8,128)(2,1)S(1)}, u32[]{:S(2)}, u32[]{:S(2)}) %collective-permute-start.23) | collective-permute-done | bytes 327712 | tf_op jit(solution)/shard_map/ppermute | solution.py:184
  161.8 2.3 %collective-permute-start.24 = (bf16[64,2560]{1,0:T(8,128)(2,1)S(1)}, bf16[64,2560]{1,0:T(8,128)(2,1)S(1)}, u32[]{:S(2)}, u32[]{:S(2)}) collective-permute-start(bf16[64,2560]{1,0:T(8,128)(2,1)S(1)} %fusion.6), channel_id=1, source_target_pairs={{0,1},{1,2},{2,3},{3,0},{4,5},{5,6},{6,7},{7,4},{8,9},{9,10},{10,1... | collective-permute-start | bytes 983048 | tf_op jit(solution)/shard_map/ppermute | solution.py:184
  164.3 4.7 %collective-permute-done.24 = bf16[64,2560]{1,0:T(8,128)(2,1)S(1)} collective-permute-done((bf16[64,2560]{1,0:T(8,128)(2,1)S(1)}, bf16[64,2560]{1,0:T(8,128)(2,1)S(1)}, u32[]{:S(2)}, u32[]{:S(2)}) %collective-permute-start.24) | collective-permute-done | bytes 327712 | tf_op jit(solution)/shard_map/ppermute | solution.py:184
  169.1 3.5 %collective-permute-done.27 = bf16[64,2560]{1,0:T(8,128)(2,1)S(1)} collective-permute-done((bf16[64,2560]{1,0:T(8,128)(2,1)S(1)}, bf16[64,2560]{1,0:T(8,128)(2,1)S(1)}, u32[]{:S(2)}, u32[]{:S(2)}) %collective-permute-start.27) | collective-permute-done | bytes 327712 | tf_op jit(solution)/shard_map/ppermute | solution.py:184
  172.7 1.0 maximum_select_fusion
  (75 shorter events, 9.4 us)
Async XLA Ops:
  0.0 18.6 %collective-permute-start.2 = (bf16[512,640]{1,0:T(8,128)(2,1)}, bf16[512,640]{1,0:T(8,128)(2,1)}, u32[]{:S(2)}, u32[]{:S(2)}) collective-permute-start(bf16[512,640]{1,0:T(8,128)(2,1)} %refs_0_.1), channel_id=1, source_target_pairs={{0,16},{8,24},{16,32},{24,40},{32,48},{40,56},{48,64},{56,72},{64,... | collective-permute-start | bytes 1966088 | tf_op jit(solution)/shard_map/ppermute | solution.py:233
  3.1 31.7 %collective-permute-start.4 = (bf16[512,640]{1,0:T(8,128)(2,1)}, bf16[512,640]{1,0:T(8,128)(2,1)}, u32[]{:S(2)}, u32[]{:S(2)}) collective-permute-start(bf16[512,640]{1,0:T(8,128)(2,1)} %refs_0_.1), channel_id=1, source_target_pairs={{16,0},{24,8},{32,16},{40,24},{48,32},{56,40},{64,48},{72,56},{80,... | collective-permute-start | bytes 1966088 | tf_op jit(solution)/shard_map/ppermute | solution.py:234
  4.6 5.5 %collective-permute-start = (s32[4,17]{1,0:T(4,128)S(1)}, s32[4,17]{1,0:T(4,128)S(1)}, u32[]{:S(2)}, u32[]{:S(2)}) collective-permute-start(s32[4,17]{1,0:T(4,128)S(1)} %pad_add_fusion.4), channel_id=1, source_target_pairs={{0,8},{8,0},{16,24},{24,16},{32,40},{40,32},{48,56},{56,48},{64,72... | collective-permute-start | bytes 824 | tf_op jit(solution)/shard_map/ppermute | solution.py:208
  6.8 18.1 %collective-permute-start.1 = (bf16[512,640]{1,0:T(8,128)(2,1)}, bf16[512,640]{1,0:T(8,128)(2,1)}, u32[]{:S(2)}, u32[]{:S(2)}) collective-permute-start(bf16[512,640]{1,0:T(8,128)(2,1)} %param.6), channel_id=1, source_target_pairs={{0,8},{8,0},{16,24},{24,16},{32,40},{40,32},{48,56},{56,48},{64,72... | collective-permute-start | bytes 1966088 | tf_op jit(solution)/shard_map/ppermute | solution.py:209
  8.2 26.6 %collective-permute-start.6 = (bf16[512,640]{1,0:T(8,128)(2,1)}, bf16[512,640]{1,0:T(8,128)(2,1)S(1)}, u32[]{:S(2)}, u32[]{:S(2)}) collective-permute-start(bf16[512,640]{1,0:T(8,128)(2,1)} %refs_1_.1), channel_id=1, source_target_pairs={{16,0},{24,8},{32,16},{40,24},{48,32},{56,40},{64,48},{72,56},{80,... | collective-permute-start | bytes 1966088 | tf_op jit(solution)/shard_map/ppermute | solution.py:234
  10.1 24.7 %collective-permute-start.5 = (bf16[512,640]{1,0:T(8,128)(2,1)}, bf16[512,640]{1,0:T(8,128)(2,1)}, u32[]{:S(2)}, u32[]{:S(2)}) collective-permute-start(bf16[512,640]{1,0:T(8,128)(2,1)} %refs_1_.1), channel_id=1, source_target_pairs={{0,16},{8,24},{16,32},{24,40},{32,48},{40,56},{48,64},{56,72},{64,... | collective-permute-start | bytes 1966088 | tf_op jit(solution)/shard_map/ppermute | solution.py:233
  15.1 10.9 %copy-start = (bf16[512,640]{1,0:T(8,128)(2,1)S(1)}, bf16[512,640]{1,0:T(8,128)(2,1)}, u32[]{:S(2)}) copy-start(bf16[512,640]{1,0:T(8,128)(2,1)} %refs_1_.1) | copy-start | bytes 1966084
  15.1 10.9 %copy-start.1 = (bf16[512,640]{1,0:T(8,128)(2,1)S(1)}, bf16[512,640]{1,0:T(8,128)(2,1)}, u32[]{:S(2)}) copy-start(bf16[512,640]{1,0:T(8,128)(2,1)} %refs_0_.1) | copy-start | bytes 1966084
  22.4 88.4 %collective-permute-start.19 = (bf16[640,2560]{1,0:T(8,128)(2,1)}, bf16[640,2560]{1,0:T(8,128)(2,1)}, u32[]{:S(2)}, u32[]{:S(2)}) collective-permute-start(bf16[640,2560]{1,0:T(8,128)(2,1)} %constant_dynamic-slice_fusion), channel_id=1, source_target_pairs={{0,4},{1,5},{2,6},{3,7},{4,0},{5,1},{6,2},{7,3},{8,12},{9,13},{10,... | collective-permute-start | bytes 9830408 | tf_op jit(solution)/shard_map/ppermute | solution.py:153
  34.8 17.9 %collective-permute-start.3 = (bf16[512,640]{1,0:T(8,128)(2,1)}, bf16[512,640]{1,0:T(8,128)(2,1)S(1)}, u32[]{:S(2)}, u32[]{:S(2)}) collective-permute-start(bf16[512,640]{1,0:T(8,128)(2,1)} %collective-permute-done.2.refs_0_), channel_id=1, source_target_pairs={{0,16},{8,24},{16,32},{24,40},{32,48},{40,56},{48,64},{56,72},{64,... | collective-permute-start | bytes 1966088 | tf_op jit(solution)/shard_map/ppermute | solution.py:233
  35.2 19.1 %collective-permute-start.8 = (bf16[512,640]{1,0:T(8,128)(2,1)}, bf16[512,640]{1,0:T(8,128)(2,1)S(1)}, u32[]{:S(2)}, u32[]{:S(2)}) collective-permute-start(bf16[512,640]{1,0:T(8,128)(2,1)} %collective-permute-done.4.refs_1_), channel_id=1, source_target_pairs={{16,0},{24,8},{32,16},{40,24},{48,32},{56,40},{64,48},{72,56},{80,... | collective-permute-start | bytes 1966088 | tf_op jit(solution)/shard_map/ppermute | solution.py:234
  36.8 29.9 %collective-permute-start.9 = (bf16[512,640]{1,0:T(8,128)(2,1)}, bf16[512,640]{1,0:T(8,128)(2,1)S(1)}, u32[]{:S(2)}, u32[]{:S(2)}) collective-permute-start(bf16[512,640]{1,0:T(8,128)(2,1)} %collective-permute-done.5.refs_2_), channel_id=1, source_target_pairs={{0,16},{8,24},{16,32},{24,40},{32,48},{40,56},{48,64},{56,72},{64,... | collective-permute-start | bytes 1966088 | tf_op jit(solution)/shard_map/ppermute | solution.py:233
  38.4 29.9 %collective-permute-start.10 = (bf16[512,640]{1,0:T(8,128)(2,1)S(1)}, bf16[512,640]{1,0:T(8,128)(2,1)S(1)}, u32[]{:S(2)}, u32[]{:S(2)}) collective-permute-start(bf16[512,640]{1,0:T(8,128)(2,1)S(1)} %collective-permute-done.6.refs_3_), channel_id=1, source_target_pairs={{16,0},{24,8},{32,16},{40,24},{48,32},{56,40},{64,48},{72,56},{80,... | collective-permute-start | bytes 1966088 | tf_op jit(solution)/shard_map/ppermute | solution.py:234
  52.7 28.1 %collective-permute-start.7 = (bf16[512,640]{1,0:T(8,128)(2,1)S(1)}, bf16[512,640]{1,0:T(8,128)(2,1)S(1)}, u32[]{:S(2)}, u32[]{:S(2)}) collective-permute-start(bf16[512,640]{1,0:T(8,128)(2,1)S(1)} %collective-permute-done.3.refs_0_), channel_id=1, source_target_pairs={{0,16},{8,24},{16,32},{24,40},{32,48},{40,56},{48,64},{56,72},{64,... | collective-permute-start | bytes 1966088 | tf_op jit(solution)/shard_map/ppermute | solution.py:233
  54.3 39.9 %collective-permute-start.14 = (bf16[512,640]{1,0:T(8,128)(2,1)S(1)}, bf16[512,640]{1,0:T(8,128)(2,1)S(1)}, u32[]{:S(2)}, u32[]{:S(2)}) collective-permute-start(bf16[512,640]{1,0:T(8,128)(2,1)S(1)} %collective-permute-done.8.refs_1_), channel_id=1, source_target_pairs={{16,0},{24,8},{32,16},{40,24},{48,32},{56,40},{64,48},{72,56},{80,... | collective-permute-start | bytes 1966088 | tf_op jit(solution)/shard_map/ppermute | solution.py:234
  66.7 28.1 %collective-permute-start.15 = (bf16[512,640]{1,0:T(8,128)(2,1)S(1)}, bf16[512,640]{1,0:T(8,128)(2,1)S(1)}, u32[]{:S(2)}, u32[]{:S(2)}) collective-permute-start(bf16[512,640]{1,0:T(8,128)(2,1)S(1)} %collective-permute-done.9.refs_2_), channel_id=1, source_target_pairs={{0,16},{8,24},{16,32},{24,40},{32,48},{40,56},{48,64},{56,72},{64,... | collective-permute-start | bytes 1966088 | tf_op jit(solution)/shard_map/ppermute | solution.py:233
  68.3 25.7 %collective-permute-start.12 = (bf16[512,640]{1,0:T(8,128)(2,1)S(1)}, bf16[512,640]{1,0:T(8,128)(2,1)S(1)}, u32[]{:S(2)}, u32[]{:S(2)}) collective-permute-start(bf16[512,640]{1,0:T(8,128)(2,1)S(1)} %collective-permute-done.10.refs_3_), channel_id=1, source_target_pairs={{16,0},{24,8},{32,16},{40,24},{48,32},{56,40},{64,48},{72,56},{80,... | collective-permute-start | bytes 1966088 | tf_op jit(solution)/shard_map/ppermute | solution.py:234
  80.8 25.7 %collective-permute-start.11 = (bf16[512,640]{1,0:T(8,128)(2,1)S(1)}, bf16[512,640]{1,0:T(8,128)(2,1)S(1)}, u32[]{:S(2)}, u32[]{:S(2)}) collective-permute-start(bf16[512,640]{1,0:T(8,128)(2,1)S(1)} %collective-permute-done.7.refs_0_), channel_id=1, source_target_pairs={{0,16},{8,24},{16,32},{24,40},{32,48},{40,56},{48,64},{56,72},{64,... | collective-permute-start | bytes 1966088 | tf_op jit(solution)/shard_map/ppermute | solution.py:237
  94.1 15.6 %collective-permute-start.13 = (bf16[512,640]{1,0:T(8,128)(2,1)S(1)}, bf16[512,640]{1,0:T(8,128)(2,1)S(1)}, u32[]{:S(2)}, u32[]{:S(2)}) collective-permute-start(bf16[512,640]{1,0:T(8,128)(2,1)S(1)} %collective-permute-done.12.refs_3_), channel_id=1, source_target_pairs={{16,0},{24,8},{32,16},{40,24},{48,32},{56,40},{64,48},{72,56},{80,... | collective-permute-start | bytes 1966088 | tf_op jit(solution)/shard_map/ppermute | solution.py:237
  98.0 12.8 %copy-start.2 = (f32[40,128,128]{2,1,0:T(8,128)}, f32[40,128,128]{2,1,0:T(8,128)S(1)}, u32[]{:S(2)}) copy-start(f32[40,128,128]{2,1,0:T(8,128)S(1)} %get-tuple-element.49.refs_2_) | copy-start | bytes 7864324
  110.8 32.2 %collective-permute-start.20 = (bf16[640,2560]{1,0:T(8,128)(2,1)}, bf16[640,2560]{1,0:T(8,128)(2,1)}, u32[]{:S(2)}, u32[]{:S(2)}) collective-permute-start(bf16[640,2560]{1,0:T(8,128)(2,1)} %collective-permute-done.19), channel_id=1, source_target_pairs={{0,128},{128,0},{1,129},{129,1},{2,130},{130,2},{3,131},{131,3},{4... | collective-permute-start | bytes 9830408 | tf_op jit(solution)/shard_map/ppermute | solution.py:157
  110.9 20.4 %collective-permute-start.16 = (bf16[20,128,128]{2,1,0:T(8,128)(2,1)S(1)}, bf16[20,128,128]{2,1,0:T(8,128)(2,1)}, u32[]{:S(2)}, u32[]{:S(2)}) collective-permute-start(bf16[20,128,128]{2,1,0:T(8,128)(2,1)S(1)} %get-tuple-element.55), channel_id=1, source_target_pairs={{0,8},{8,0},{16,24},{24,16},{32,40},{40,32},{48,56},{56,48},{64,72... | collective-permute-start | bytes 1966088 | tf_op jit(solution)/shard_map/ppermute | solution.py:250
  113.9 17.4 %collective-permute-start.17 = (f32[20,8,128]{2,1,0:T(8,128)S(1)}, f32[20,8,128]{2,1,0:T(8,128)S(1)}, u32[]{:S(2)}, u32[]{:S(2)}) collective-permute-start(f32[20,8,128]{2,1,0:T(8,128)S(1)} %get-tuple-element.51), channel_id=1, source_target_pairs={{0,8},{8,0},{16,24},{24,16},{32,40},{40,32},{48,56},{56,48},{64,72... | collective-permute-start | bytes 245768 | tf_op jit(solution)/shard_map/ppermute | solution.py:250
  114.5 1.7 %copy-start.3 = (f32[40,128,128]{2,1,0:T(8,128)S(1)}, f32[40,128,128]{2,1,0:T(8,128)}, u32[]{:S(2)}) copy-start(f32[40,128,128]{2,1,0:T(8,128)} %copy-done.2) | copy-start | bytes 7864324
  131.3 7.1 %slice-start = ((s8[6553600]{0:T(1024)(128)(4,1)}), s8[2359296]{0:T(1024)(128)(4,1)S(1)}, s32[]{:S(2)}) async-start(s8[6553600]{0:T(1024)(128)(4,1)} %bitcast.34), calls=%async_computation | async-start | bytes 4718592
  132.9 5.5 %slice-start.1 = ((s8[6553600]{0:T(1024)(128)(4,1)}), s8[4194304]{0:T(1024)(128)(4,1)S(1)}, s32[]{:S(2)}) async-start(s8[6553600]{0:T(1024)(128)(4,1)} %bitcast.34), calls=%async_computation.1 | async-start | bytes 8388608
  133.1 7.2 %collective-permute-start.18 = (bf16[128,640]{1,0:T(8,128)(2,1)S(1)}, bf16[128,640]{1,0:T(8,128)(2,1)S(1)}, u32[]{:S(2)}, u32[]{:S(2)}) collective-permute-start(bf16[128,640]{1,0:T(8,128)(2,1)S(1)} %pad_maximum_fusion.1), channel_id=1, source_target_pairs={{0,4},{1,5},{2,6},{3,7},{4,0},{5,1},{6,2},{7,3},{8,12},{9,13},{10,... | collective-permute-start | bytes 491528 | tf_op jit(solution)/shard_map/ppermute | solution.py:153
  134.3 11.4 %collective-permute-start.21 = (bf16[128,640]{1,0:T(8,128)(2,1)S(1)}, bf16[128,640]{1,0:T(8,128)(2,1)S(1)}, u32[]{:S(2)}, u32[]{:S(2)}) collective-permute-start(bf16[128,640]{1,0:T(8,128)(2,1)S(1)} %pad_maximum_fusion.2), channel_id=1, source_target_pairs={{0,4},{1,5},{2,6},{3,7},{4,0},{5,1},{6,2},{7,3},{8,12},{9,13},{10,... | collective-permute-start | bytes 491528 | tf_op jit(solution)/shard_map/ppermute | solution.py:153
  145.7 8.2 %collective-permute-start.22 = (bf16[64,2560]{1,0:T(8,128)(2,1)S(1)}, bf16[64,2560]{1,0:T(8,128)(2,1)S(1)}, u32[]{:S(2)}, u32[]{:S(2)}) collective-permute-start(bf16[64,2560]{1,0:T(8,128)(2,1)S(1)} %split.63), channel_id=1, source_target_pairs={{0,1},{1,2},{2,3},{3,0},{4,5},{5,6},{6,7},{7,4},{8,9},{9,10},{10,1... | collective-permute-start | bytes 983048 | tf_op jit(solution)/shard_map/ppermute | solution.py:184
  146.0 9.5 %collective-permute-start.25 = (bf16[64,2560]{1,0:T(8,128)(2,1)S(1)}, bf16[64,2560]{1,0:T(8,128)(2,1)S(1)}, u32[]{:S(2)}, u32[]{:S(2)}) collective-permute-start(bf16[64,2560]{1,0:T(8,128)(2,1)S(1)} %split.62), channel_id=1, source_target_pairs={{0,3},{1,0},{2,1},{3,2},{4,7},{5,4},{6,5},{7,6},{8,11},{9,8},{10,9... | collective-permute-start | bytes 983048 | tf_op jit(solution)/shard_map/ppermute | solution.py:184
  154.0 7.8 %collective-permute-start.23 = (bf16[64,2560]{1,0:T(8,128)(2,1)S(1)}, bf16[64,2560]{1,0:T(8,128)(2,1)S(1)}, u32[]{:S(2)}, u32[]{:S(2)}) collective-permute-start(bf16[64,2560]{1,0:T(8,128)(2,1)S(1)} %fusion.7), channel_id=1, source_target_pairs={{0,1},{1,2},{2,3},{3,0},{4,5},{5,6},{6,7},{7,4},{8,9},{9,10},{10,1... | collective-permute-start | bytes 983048 | tf_op jit(solution)/shard_map/ppermute | solution.py:184
  155.6 8.5 %collective-permute-start.26 = (bf16[64,2560]{1,0:T(8,128)(2,1)S(1)}, bf16[64,2560]{1,0:T(8,128)(2,1)S(1)}, u32[]{:S(2)}, u32[]{:S(2)}) collective-permute-start(bf16[64,2560]{1,0:T(8,128)(2,1)S(1)} %fusion.4), channel_id=1, source_target_pairs={{0,3},{1,0},{2,1},{3,2},{4,7},{5,4},{6,5},{7,6},{8,11},{9,8},{10,9... | collective-permute-start | bytes 983048 | tf_op jit(solution)/shard_map/ppermute | solution.py:184
  161.8 7.2 %collective-permute-start.24 = (bf16[64,2560]{1,0:T(8,128)(2,1)S(1)}, bf16[64,2560]{1,0:T(8,128)(2,1)S(1)}, u32[]{:S(2)}, u32[]{:S(2)}) collective-permute-start(bf16[64,2560]{1,0:T(8,128)(2,1)S(1)} %fusion.6), channel_id=1, source_target_pairs={{0,1},{1,2},{2,3},{3,0},{4,5},{5,6},{6,7},{7,4},{8,9},{9,10},{10,1... | collective-permute-start | bytes 983048 | tf_op jit(solution)/shard_map/ppermute | solution.py:184
  164.2 8.4 %collective-permute-start.27 = (bf16[64,2560]{1,0:T(8,128)(2,1)S(1)}, bf16[64,2560]{1,0:T(8,128)(2,1)S(1)}, u32[]{:S(2)}, u32[]{:S(2)}) collective-permute-start(bf16[64,2560]{1,0:T(8,128)(2,1)S(1)} %fusion.3), channel_id=1, source_target_pairs={{0,3},{1,0},{2,1},{3,2},{4,7},{5,4},{6,5},{7,6},{8,11},{9,8},{10,9... | collective-permute-start | bytes 983048 | tf_op jit(solution)/shard_map/ppermute | solution.py:184

commit v5 on v4

--- a/solution.py
+++ b/solution.py
@@ -20,7 +20,7 @@
 
 
 def attend_kernel(chunks, first, last, base, flags, q, *refs):
-    keys, values = refs[:chunks], refs[chunks : 2 * chunks]
+    keys, values = ((refs[0],), (refs[1],)) if chunks == 1 else ((refs[0], refs[3]), (refs[2], refs[1]))
     refs = refs[2 * chunks :]
     heads = q.shape[1] // HD
     per = keys[0].shape[0] // BS
@@ -112,7 +112,7 @@
             flops=tiles * chunks * 100000000, bytes_accessed=4 << 20, transcendentals=chunks << 20
         ),
         name="attend",
-    )(flags, q, *keys, *values, *state)
+    )(flags, q, keys[0], *values[::-1], *keys[1:], *state)
 
 
 def finish_kernel(mixed, stats, mixed_other, stats_other, out):
@@ -230,8 +230,9 @@
     ups, downs = (keys, values), (keys, values)
     for s in range(1, NZ // 2 + 1):
         if s < NZ // 2:
-            ups = tuple(lax.ppermute(a, "blk", up) for a in ups)
-            downs = tuple(lax.ppermute(a, "blk", down) for a in downs)
+            key_up, value_down = lax.ppermute(ups[0], "blk", up), lax.ppermute(downs[1], "blk", down)
+            ups = key_up, lax.ppermute(ups[1], "blk", up)
+            downs = lax.ppermute(downs[0], "blk", down), value_down
             coming = ((s, *ups), (NZ - s, *downs))
         else:
             coming = ((s, lax.ppermute(ups[0], "blk", up), lax.ppermute(downs[1], "blk", down)),)
@@ -242,7 +243,7 @@
             rest = lax.dynamic_slice_in_dim(held, (1 - core) * half, half, 1)
             fetched = over_x(ours)
         state = visit(stage, state)
-        if s < NZ // 2:
+        if 1 < s < NZ // 2:
             ups = tuple(after(a, state[1]) for a in ups)
             downs = tuple(after(a, state[1]) for a in downs)
         stage = coming

time: 176 us -> 173 us (0.983); the launches traced: 174 us -> 173 us
  Pallas kernels: 21.8 us -> 38.2 us
  waiting for transfers between devices: 89.8 us -> 74.3 us
  matrix products: 15 us -> 13.1 us
  starting transfers between devices: 32.9 us -> 34.7 us
    ppermute x12 -> x6, waiting for transfers between devices: 48 us -> 17.7 us  [the longest x3 16.2 us: on_device(): ups = (key_up, lax.ppermute(ups[1], 'blk', up))]
    pallas_call x6, Pallas kernels: 20.2 us -> 36.6 us  [attend(): pl.pallas_call(functools.partial(attend_kernel, chunks, first, last, tile...]
    ppermute x1 -> x4, waiting for transfers between devices: 3.2 us -> 12.1 us  [on_device(): lax.ppermute(downs[1], 'blk', down)]
    ppermute x1 -> x4, starting transfers between devices: 1.59 us -> 7.62 us  [on_device(): lax.ppermute(ups[0], 'blk', up)]
    ppermute x12 -> x6, starting transfers between devices: 14.6 us -> 8.58 us  [the longest x3 8.04 us: on_device(): ups = (key_up, lax.ppermute(ups[1], 'blk', up))]
    ppermute x1, waiting for transfers between devices: 1.52 us -> 4.87 us  [on_device(): both = jnp.concatenate([queries, lax.ppermute(queries, 'blk', cross)])]
    ppermute x1 -> x4, waiting for transfers between devices: 8.45 us -> 10.8 us  [on_device(): lax.ppermute(ups[0], 'blk', up)]
    ppermute x1 -> x4, starting transfers between devices: 0.12 us -> 2.28 us  [on_device(): lax.ppermute(downs[1], 'blk', down)]
  transfers between devices with their start and end apart: 28 -> 28, of which waited for: 16 -> 16; matrix products, arithmetic and copies ran while one was open for 15% -> 13% of each run, Pallas kernels for 13% -> 22%
where the time goes in v5:
time: 173 us
  waiting for transfers between devices  74.3 us (43%)
  Pallas kernels  38.2 us (22%)
  starting transfers between devices  34.7 us (20%)
  matrix products  13.1 us (8%)
  local copies, waits for them, and re-layouts  8.67 us (5%)
  other arithmetic  3.36 us (2%)
    pallas_call x6, Pallas kernels, attend(): pl.pallas_call(functools.partial(attend_kernel, chunks, first, last, tile...  36.6 us
    ppermute x3, waiting for transfers between devices, on_device(): ups = (key_up, lax.ppermute(ups[1], 'blk', up))  16.2 us
    ppermute x6, waiting for transfers between devices, turn(): return lax.ppermute(a, 'head', to).astype(jnp.float32)  14.4 us
    ppermute x4, waiting for transfers between devices, on_device(): lax.ppermute(downs[1], 'blk', down)  12.1 us
    ppermute x2, waiting for transfers between devices, on_device(): other = [lax.ppermute(a, 'blk', cross) for a in theirs]  11.9 us
    ppermute x4, waiting for transfers between devices, on_device(): lax.ppermute(ups[0], 'blk', up)  10.8 us
    dot_general x4, matrix products, terms(): part = jnp.dot(acts, weights[half][1], preferred_element_type=jnp.float32)  10.7 us
    ppermute x3, starting transfers between devices, on_device(): ups = (key_up, lax.ppermute(ups[1], 'blk', up))  8.04 us
  transfers between devices with their start and end apart: 28, of which 16 were waited for; matrix products, arithmetic and copies ran while one was open for 13% of the time, Pallas kernels for 22%

profile of v5, /device:TPU:122, one launch (start us, length us, event | category | flops | bytes accessed | tf_op | source)
XLA Modules:
  0.0 172.8 jit_solution(4710438045788552554)
XLA Ops:
  0.0 3.1 %collective-permute-start.2 = (bf16[512,640]{1,0:T(8,128)(2,1)}, bf16[512,640]{1,0:T(8,128)(2,1)S(1)}, u32[]{:S(2)}, u32[]{:S(2)}) collective-permute-start(bf16[512,640]{1,0:T(8,128)(2,1)} %refs_0_.1), channel_id=1, source_target_pairs={{0,16},{8,24},{16,32},{24,40},{32,48},{40,56},{48,64},{56,72},{64,... | collective-permute-start | bytes 1966088 | tf_op jit(solution)/shard_map/ppermute | solution.py:233
  4.6 2.1 %collective-permute-start = (s32[4,17]{1,0:T(4,128)S(1)}, s32[4,17]{1,0:T(4,128)S(1)}, u32[]{:S(2)}, u32[]{:S(2)}) collective-permute-start(s32[4,17]{1,0:T(4,128)S(1)} %pad_add_fusion.4), channel_id=1, source_target_pairs={{0,8},{8,0},{16,24},{24,16},{32,40},{40,32},{48,56},{56,48},{64,72... | collective-permute-start | bytes 824 | tf_op jit(solution)/shard_map/ppermute | solution.py:208
  6.8 1.4 collective-permute-start.1
  8.9 1.1 constant_dynamic-update-slice_fusion.1
  10.1 3.3 %collective-permute-start.5 = (bf16[512,640]{1,0:T(8,128)(2,1)}, bf16[512,640]{1,0:T(8,128)(2,1)}, u32[]{:S(2)}, u32[]{:S(2)}) collective-permute-start(bf16[512,640]{1,0:T(8,128)(2,1)} %refs_1_.1), channel_id=1, source_target_pairs={{0,16},{8,24},{16,32},{24,40},{32,48},{40,56},{48,64},{56,72},{64,... | collective-permute-start | bytes 1966088 | tf_op jit(solution)/shard_map/ppermute | solution.py:234
  15.4 3.1 %collective-permute-done.2.refs_0_ = bf16[512,640]{1,0:T(8,128)(2,1)S(1)} collective-permute-done((bf16[512,640]{1,0:T(8,128)(2,1)}, bf16[512,640]{1,0:T(8,128)(2,1)S(1)}, u32[]{:S(2)}, u32[]{:S(2)}) %collective-permute-start.2) | collective-permute-done | bytes 655392 | tf_op jit(solution)/shard_map/ppermute | solution.py:233
  18.6 2.1 %constant_dynamic-slice_fusion = bf16[640,2560]{1,0:T(8,128)(2,1)S(1)} fusion(bf16[640,5120]{1,0:T(8,128)(2,1)} %param.11, s32[]{:T(128)S(6)} %select_n.135), kind=kLoop, calls=%fused_computation.48 | loop fusion | bytes 6553604 | tf_op jit(solution)/shard_map/dynamic_slice | solution.py:242
  21.4 4.9 %collective-permute-done.1 = bf16[512,640]{1,0:T(8,128)(2,1)} collective-permute-done((bf16[512,640]{1,0:T(8,128)(2,1)}, bf16[512,640]{1,0:T(8,128)(2,1)}, u32[]{:S(2)}, u32[]{:S(2)}) %collective-permute-start.1) | collective-permute-done | bytes 655392 | tf_op jit(solution)/shard_map/ppermute | solution.py:209
  26.2 2.7 %collective-permute-start.3 = (bf16[512,640]{1,0:T(8,128)(2,1)S(1)}, bf16[512,640]{1,0:T(8,128)(2,1)S(1)}, u32[]{:S(2)}, u32[]{:S(2)}) collective-permute-start(bf16[512,640]{1,0:T(8,128)(2,1)S(1)} %collective-permute-done.2.refs_0_), channel_id=1, source_target_pairs={{0,16},{8,24},{16,32},{24,40},{32,48},{40,56},{48,64},{56,72},{64,... | collective-permute-start | bytes 1966088 | tf_op jit(solution)/shard_map/ppermute | solution.py:233
  29.0 7.3 %collective-permute-done.4.refs_1_ = bf16[512,640]{1,0:T(8,128)(2,1)S(1)} collective-permute-done((bf16[512,640]{1,0:T(8,128)(2,1)}, bf16[512,640]{1,0:T(8,128)(2,1)S(1)}, u32[]{:S(2)}, u32[]{:S(2)}) %collective-permute-start.4) | collective-permute-done | bytes 655392 | tf_op jit(solution)/shard_map/ppermute | solution.py:233
  36.3 3.2 %collective-permute-start.9 = (bf16[512,640]{1,0:T(8,128)(2,1)}, bf16[512,640]{1,0:T(8,128)(2,1)S(1)}, u32[]{:S(2)}, u32[]{:S(2)}) collective-permute-start(bf16[512,640]{1,0:T(8,128)(2,1)} %collective-permute-done.5.refs_2_), channel_id=1, source_target_pairs={{0,16},{8,24},{16,32},{24,40},{32,48},{40,56},{48,64},{56,72},{64,... | collective-permute-start | bytes 1966088 | tf_op jit(solution)/shard_map/ppermute | solution.py:234
  39.5 1.2 constant_dynamic-update-slice_fusion.q
  40.7 7.8 %attend.6 = (f32[40,128,128]{2,1,0:T(8,128)S(1)}, f32[40,8,128]{2,1,0:T(8,128)S(1)}) custom-call(s32[1,8,4]{2,1,0:T(8,128)S(1)} %copy.37.flags, bf16[1024,640]{1,0:T(8,128)(2,1)S(1)} %constant_dynamic-update-slice_fusion.q, bf16[512,640]{1,0:T(8,128)(2,1)S(1)} %copy-done, bf16[512,640]{1,0:T(8,128)(2,1)S(1)} %copy-done.1), custom_call_target="tpu_custom_call" | custom-call | flops 4000000000 | bytes 4194304 | tf_op jit(solution)/shard_map/attend/pallas_call | solution.py:100
  48.5 6.9 %attend.7 = (f32[40,128,128]{2,1,0:T(8,128)S(1)}, f32[40,8,128]{2,1,0:T(8,128)S(1)}) custom-call(s32[2,8,4]{2,1,0:T(8,128)S(1)} %pad_add_fusion.flags, bf16[1024,640]{1,0:T(8,128)(2,1)S(1)} %constant_dynamic-update-slice_fusion.q, bf16[512,640]{1,0:T(8,128)(2,1)S(1)} %collective-permute-done.2.refs_0_, ...), custom_call_target="tpu_custom_call", output_to_operand_aliasing={{0}: (6, {}), {1}: (7, {})} | custom-call | flops 8000000000 | bytes 4194304 | tf_op jit(solution)/shard_map/attend/pallas_call | solution.py:100
  55.4 4.2 %collective-permute-done.9.refs_2_ = bf16[512,640]{1,0:T(8,128)(2,1)S(1)} collective-permute-done((bf16[512,640]{1,0:T(8,128)(2,1)}, bf16[512,640]{1,0:T(8,128)(2,1)S(1)}, u32[]{:S(2)}, u32[]{:S(2)}) %collective-permute-start.9) | collective-permute-done | bytes 655392 | tf_op jit(solution)/shard_map/ppermute | solution.py:234
  59.6 3.3 %collective-permute-done.8.refs_1_ = bf16[512,640]{1,0:T(8,128)(2,1)S(1)} collective-permute-done((bf16[512,640]{1,0:T(8,128)(2,1)S(1)}, bf16[512,640]{1,0:T(8,128)(2,1)S(1)}, u32[]{:S(2)}, u32[]{:S(2)}) %collective-permute-start.8) | collective-permute-done | bytes 655392 | tf_op jit(solution)/shard_map/ppermute | solution.py:233
  63.2 1.7 %collective-permute-start.12 = (bf16[512,640]{1,0:T(8,128)(2,1)S(1)}, bf16[512,640]{1,0:T(8,128)(2,1)S(1)}, u32[]{:S(2)}, u32[]{:S(2)}) collective-permute-start(bf16[512,640]{1,0:T(8,128)(2,1)S(1)} %collective-permute-done.8.refs_1_), channel_id=1, source_target_pairs={{16,0},{24,8},{32,16},{40,24},{48,32},{56,40},{64,48},{72,56},{80,... | collective-permute-start | bytes 1966088 | tf_op jit(solution)/shard_map/ppermute | solution.py:233
  64.9 1.5 collective-permute-start.14
  66.9 8.5 %attend.8 = (f32[40,128,128]{2,1,0:T(8,128)S(1)}, f32[40,8,128]{2,1,0:T(8,128)S(1)}) custom-call(s32[2,8,4]{2,1,0:T(8,128)S(1)} %pad_add_fusion.1.flags, bf16[1024,640]{1,0:T(8,128)(2,1)S(1)} %constant_dynamic-update-slice_fusion.q, bf16[512,640]{1,0:T(8,128)(2,1)S(1)} %collective-permute-done.3.refs_0_, ...), custom_call_target="tpu_custom_call", output_to_operand_aliasing={{0}: (6, {}), {1}: (7, {})} | custom-call | flops 8000000000 | bytes 4194304 | tf_op jit(solution)/shard_map/attend/pallas_call | solution.py:100
  75.4 5.1 %collective-permute-done.7.refs_0_ = bf16[512,640]{1,0:T(8,128)(2,1)S(1)} collective-permute-done((bf16[512,640]{1,0:T(8,128)(2,1)S(1)}, bf16[512,640]{1,0:T(8,128)(2,1)S(1)}, u32[]{:S(2)}, u32[]{:S(2)}) %collective-permute-start.7) | collective-permute-done | bytes 655392 | tf_op jit(solution)/shard_map/ppermute | solution.py:233
  80.5 1.5 collective-permute-start.11
  82.6 12.0 %collective-permute-done.14.refs_2_ = bf16[512,640]{1,0:T(8,128)(2,1)S(1)} collective-permute-done((bf16[512,640]{1,0:T(8,128)(2,1)S(1)}, bf16[512,640]{1,0:T(8,128)(2,1)S(1)}, u32[]{:S(2)}, u32[]{:S(2)}) %collective-permute-start.14) | collective-permute-done | bytes 655392 | tf_op jit(solution)/shard_map/ppermute | solution.py:234
  94.6 1.5 collective-permute-done.15.refs_3_
  96.1 7.6 %attend.9 = (f32[40,128,128]{2,1,0:T(8,128)S(1)}, f32[40,8,128]{2,1,0:T(8,128)S(1)}) custom-call(s32[2,8,4]{2,1,0:T(8,128)S(1)} %pad_add_fusion.2.flags, bf16[1024,640]{1,0:T(8,128)(2,1)S(1)} %constant_dynamic-update-slice_fusion.q, bf16[512,640]{1,0:T(8,128)(2,1)S(1)} %collective-permute-done.7.refs_0_, ...), custom_call_target="tpu_custom_call", output_to_operand_aliasing={{0}: (6, {}), {1}: (7, {})} | custom-call | flops 8000000000 | bytes 4194304 | tf_op jit(solution)/shard_map/attend/pallas_call | solution.py:100
  103.7 2.6 %collective-permute-done.11.refs_0_ = bf16[512,640]{1,0:T(8,128)(2,1)S(1)} collective-permute-done((bf16[512,640]{1,0:T(8,128)(2,1)S(1)}, bf16[512,640]{1,0:T(8,128)(2,1)S(1)}, u32[]{:S(2)}, u32[]{:S(2)}) %collective-permute-start.11) | collective-permute-done | bytes 655392 | tf_op jit(solution)/shard_map/ppermute | solution.py:238
  106.3 1.5 collective-permute-done.13.refs_1_
  107.8 2.7 %attend.10 = (bf16[20,128,128]{2,1,0:T(8,128)(2,1)S(1)}, f32[20,8,128]{2,1,0:T(8,128)S(1)}) custom-call(s32[1,8,4]{2,1,0:T(8,128)S(1)} %copy.34.flags, bf16[1024,640]{1,0:T(8,128)(2,1)S(1)} %constant_dynamic-update-slice_fusion.q, bf16[512,640]{1,0:T(8,128)(2,1)S(1)} %collective-permute-done.11.refs_0_, ...), custom_call_target="tpu_custom_call" | custom-call | flops 2000000000 | bytes 4194304 | tf_op jit(solution)/shard_map/attend/pallas_call | solution.py:100
  110.6 1.4 collective-permute-start.16
  112.0 2.2 %collective-permute-start.17 = (f32[20,8,128]{2,1,0:T(8,128)S(1)}, f32[20,8,128]{2,1,0:T(8,128)S(1)}, u32[]{:S(2)}, u32[]{:S(2)}) collective-permute-start(f32[20,8,128]{2,1,0:T(8,128)S(1)} %get-tuple-element.43), channel_id=1, source_target_pairs={{0,8},{8,0},{16,24},{24,16},{32,40},{40,32},{48,56},{56,48},{64,72... | collective-permute-start | bytes 245768 | tf_op jit(solution)/shard_map/ppermute | solution.py:251
  114.3 1.7 %copy-done.3 = f32[40,128,128]{2,1,0:T(8,128)S(1)} copy-done((f32[40,128,128]{2,1,0:T(8,128)S(1)}, f32[40,128,128]{2,1,0:T(8,128)}, u32[]{:S(2)}) %copy-start.3) | copy-done | bytes 2621464
  116.0 3.1 %attend.11 = (f32[20,128,128]{2,1,0:T(8,128)S(1)}, f32[20,8,128]{2,1,0:T(8,128)S(1)}) custom-call(s32[1,8,4]{2,1,0:T(8,128)S(1)} %copy.34.flags, bf16[1024,640]{1,0:T(8,128)(2,1)S(1)} %constant_dynamic-update-slice_fusion.q, bf16[512,640]{1,0:T(8,128)(2,1)S(1)} %collective-permute-done.11.refs_0_, bf16[512,640]{1,0:T(8,128)(2,1)S(1)} %collective-permute-done.13.refs_1_, ...), custom_call_target="tpu_custom_call" | custom-call | flops 2000000000 | bytes 4194304 | tf_op jit(solution)/shard_map/attend/pallas_call | solution.py:100
  119.1 11.9 %collective-permute-done.17.stats_other = f32[20,8,128]{2,1,0:T(8,128)S(1)} collective-permute-done((f32[20,8,128]{2,1,0:T(8,128)S(1)}, f32[20,8,128]{2,1,0:T(8,128)S(1)}, u32[]{:S(2)}, u32[]{:S(2)}) %collective-permute-start.17) | collective-permute-done | bytes 81952 | tf_op jit(solution)/shard_map/ppermute | solution.py:251
  131.1 1.6 finish.1
  133.4 1.6 collective-permute-start.21
  135.0 1.2 fusion.10
  136.3 1.2 fusion
  137.5 2.5 %collective-permute-done.18 = bf16[128,640]{1,0:T(8,128)(2,1)S(1)} collective-permute-done((bf16[128,640]{1,0:T(8,128)(2,1)S(1)}, bf16[128,640]{1,0:T(8,128)(2,1)S(1)}, u32[]{:S(2)}, u32[]{:S(2)}) %collective-permute-start.18) | collective-permute-done | bytes 163872 | tf_op jit(solution)/shard_map/ppermute | solution.py:153
  140.0 2.7 %convolution_add_fusion.3 = f32[128,2560]{1,0:T(8,128)S(1)} fusion(bf16[128,640]{1,0:T(8,128)(2,1)S(1)} %collective-permute-done.18, bf16[640,2560]{1,0:T(8,128)(2,1)} %collective-permute-done.19, f32[256,2560]{1,0:T(8,128)S(1)} %fusion.10), kind=kOutput, calls=%fused_computation.4 | convolution fusion | flops 419758080 | bytes 6062080 | tf_op jit(solution)/shard_map/dot_general | solution.py:176
  142.7 2.7 %convolution_add_fusion.2 = f32[128,2560]{1,0:T(8,128)S(1)} fusion(bf16[128,640]{1,0:T(8,128)(2,1)S(1)} %collective-permute-done.18, bf16[640,2560]{1,0:T(8,128)(2,1)} %collective-permute-done.20, f32[256,2560]{1,0:T(8,128)S(1)} %fusion), kind=kOutput, calls=%fused_computation.3 | convolution fusion | flops 419758080 | bytes 6062080 | tf_op jit(solution)/shard_map/dot_general | solution.py:176
  145.7 1.8 %collective-permute-start.25 = (bf16[64,2560]{1,0:T(8,128)(2,1)S(1)}, bf16[64,2560]{1,0:T(8,128)(2,1)S(1)}, u32[]{:S(2)}, u32[]{:S(2)}) collective-permute-start(bf16[64,2560]{1,0:T(8,128)(2,1)S(1)} %split.62), channel_id=1, source_target_pairs={{0,3},{1,0},{2,1},{3,2},{4,7},{5,4},{6,5},{7,6},{8,11},{9,8},{10,9... | collective-permute-start | bytes 983048 | tf_op jit(solution)/shard_map/ppermute | solution.py:184
  147.5 2.7 %convolution_add_fusion = f32[128,2560]{1,0:T(8,128)S(1)} fusion(bf16[128,640]{1,0:T(8,128)(2,1)S(1)} %collective-permute-done.21, bf16[640,2560]{1,0:T(8,128)(2,1)} %collective-permute-done.20, f32[256,2560]{1,0:T(8,128)S(1)} %fusion), kind=kOutput, calls=%fused_computation.1 | convolution fusion | flops 419758080 | bytes 6062080 | tf_op jit(solution)/shard_map/dot_general | solution.py:176
  150.2 2.7 %convolution_add_fusion.1 = f32[128,2560]{1,0:T(8,128)S(1)} fusion(bf16[128,640]{1,0:T(8,128)(2,1)S(1)} %collective-permute-done.21, bf16[640,2560]{1,0:T(8,128)(2,1)} %collective-permute-done.19, f32[256,2560]{1,0:T(8,128)S(1)} %fusion.10), kind=kOutput, calls=%fused_computation.2 | convolution fusion | flops 419758080 | bytes 6062080 | tf_op jit(solution)/shard_map/dot_general | solution.py:176
  153.0 1.6 collective-permute-start.23
  155.2 6.3 %collective-permute-done.23 = bf16[64,2560]{1,0:T(8,128)(2,1)S(1)} collective-permute-done((bf16[64,2560]{1,0:T(8,128)(2,1)S(1)}, bf16[64,2560]{1,0:T(8,128)(2,1)S(1)}, u32[]{:S(2)}, u32[]{:S(2)}) %collective-permute-start.23) | collective-permute-done | bytes 327712 | tf_op jit(solution)/shard_map/ppermute | solution.py:184
  161.6 1.4 collective-permute-start.24
  163.9 4.9 %collective-permute-done.24 = bf16[64,2560]{1,0:T(8,128)(2,1)S(1)} collective-permute-done((bf16[64,2560]{1,0:T(8,128)(2,1)S(1)}, bf16[64,2560]{1,0:T(8,128)(2,1)S(1)}, u32[]{:S(2)}, u32[]{:S(2)}) %collective-permute-start.24) | collective-permute-done | bytes 327712 | tf_op jit(solution)/shard_map/ppermute | solution.py:184
  168.9 2.9 %collective-permute-done.27 = bf16[64,2560]{1,0:T(8,128)(2,1)S(1)} collective-permute-done((bf16[64,2560]{1,0:T(8,128)(2,1)S(1)}, bf16[64,2560]{1,0:T(8,128)(2,1)S(1)}, u32[]{:S(2)}, u32[]{:S(2)}) %collective-permute-start.27) | collective-permute-done | bytes 327712 | tf_op jit(solution)/shard_map/ppermute | solution.py:184
  171.8 1.0 maximum_select_fusion
  (79 shorter events, 9.2 us)
Async XLA Ops:
  0.0 18.6 %collective-permute-start.2 = (bf16[512,640]{1,0:T(8,128)(2,1)}, bf16[512,640]{1,0:T(8,128)(2,1)S(1)}, u32[]{:S(2)}, u32[]{:S(2)}) collective-permute-start(bf16[512,640]{1,0:T(8,128)(2,1)} %refs_0_.1), channel_id=1, source_target_pairs={{0,16},{8,24},{16,32},{24,40},{32,48},{40,56},{48,64},{56,72},{64,... | collective-permute-start | bytes 1966088 | tf_op jit(solution)/shard_map/ppermute | solution.py:233
  3.1 25.8 %collective-permute-start.6 = (bf16[512,640]{1,0:T(8,128)(2,1)}, bf16[512,640]{1,0:T(8,128)(2,1)S(1)}, u32[]{:S(2)}, u32[]{:S(2)}) collective-permute-start(bf16[512,640]{1,0:T(8,128)(2,1)} %refs_0_.1), channel_id=1, source_target_pairs={{16,0},{24,8},{32,16},{40,24},{48,32},{56,40},{64,48},{72,56},{80,... | collective-permute-start | bytes 1966088 | tf_op jit(solution)/shard_map/ppermute | solution.py:235
  4.6 5.5 %collective-permute-start = (s32[4,17]{1,0:T(4,128)S(1)}, s32[4,17]{1,0:T(4,128)S(1)}, u32[]{:S(2)}, u32[]{:S(2)}) collective-permute-start(s32[4,17]{1,0:T(4,128)S(1)} %pad_add_fusion.4), channel_id=1, source_target_pairs={{0,8},{8,0},{16,24},{24,16},{32,40},{40,32},{48,56},{56,48},{64,72... | collective-permute-start | bytes 824 | tf_op jit(solution)/shard_map/ppermute | solution.py:208
  6.8 19.5 %collective-permute-start.1 = (bf16[512,640]{1,0:T(8,128)(2,1)}, bf16[512,640]{1,0:T(8,128)(2,1)}, u32[]{:S(2)}, u32[]{:S(2)}) collective-permute-start(bf16[512,640]{1,0:T(8,128)(2,1)} %param.6), channel_id=1, source_target_pairs={{0,8},{8,0},{16,24},{24,16},{32,40},{40,32},{48,56},{56,48},{64,72... | collective-permute-start | bytes 1966088 | tf_op jit(solution)/shard_map/ppermute | solution.py:209
  8.2 28.1 %collective-permute-start.4 = (bf16[512,640]{1,0:T(8,128)(2,1)}, bf16[512,640]{1,0:T(8,128)(2,1)S(1)}, u32[]{:S(2)}, u32[]{:S(2)}) collective-permute-start(bf16[512,640]{1,0:T(8,128)(2,1)} %refs_1_.1), channel_id=1, source_target_pairs={{16,0},{24,8},{32,16},{40,24},{48,32},{56,40},{64,48},{72,56},{80,... | collective-permute-start | bytes 1966088 | tf_op jit(solution)/shard_map/ppermute | solution.py:233
  10.1 26.1 %collective-permute-start.5 = (bf16[512,640]{1,0:T(8,128)(2,1)}, bf16[512,640]{1,0:T(8,128)(2,1)}, u32[]{:S(2)}, u32[]{:S(2)}) collective-permute-start(bf16[512,640]{1,0:T(8,128)(2,1)} %refs_1_.1), channel_id=1, source_target_pairs={{0,16},{8,24},{16,32},{24,40},{32,48},{40,56},{48,64},{56,72},{64,... | collective-permute-start | bytes 1966088 | tf_op jit(solution)/shard_map/ppermute | solution.py:234
  15.4 25.2 %copy-start = (bf16[512,640]{1,0:T(8,128)(2,1)S(1)}, bf16[512,640]{1,0:T(8,128)(2,1)}, u32[]{:S(2)}) copy-start(bf16[512,640]{1,0:T(8,128)(2,1)} %refs_0_.1) | copy-start | bytes 1966084
  15.4 25.2 %copy-start.1 = (bf16[512,640]{1,0:T(8,128)(2,1)S(1)}, bf16[512,640]{1,0:T(8,128)(2,1)}, u32[]{:S(2)}) copy-start(bf16[512,640]{1,0:T(8,128)(2,1)} %refs_1_.1) | copy-start | bytes 1966084
  20.7 27.8 %copy-start.4 = (bf16[640,2560]{1,0:T(8,128)(2,1)}, bf16[640,2560]{1,0:T(8,128)(2,1)S(1)}, u32[]{:S(2)}) copy-start(bf16[640,2560]{1,0:T(8,128)(2,1)S(1)} %constant_dynamic-slice_fusion) | copy-start | bytes 9830404
  20.7 89.8 %collective-permute-start.19 = (bf16[640,2560]{1,0:T(8,128)(2,1)S(1)}, bf16[640,2560]{1,0:T(8,128)(2,1)}, u32[]{:S(2)}, u32[]{:S(2)}) collective-permute-start(bf16[640,2560]{1,0:T(8,128)(2,1)S(1)} %constant_dynamic-slice_fusion), channel_id=1, source_target_pairs={{0,4},{1,5},{2,6},{3,7},{4,0},{5,1},{6,2},{7,3},{8,12},{9,13},{10,... | collective-permute-start | bytes 9830408 | tf_op jit(solution)/shard_map/ppermute | solution.py:153
  26.2 36.6 %collective-permute-start.3 = (bf16[512,640]{1,0:T(8,128)(2,1)S(1)}, bf16[512,640]{1,0:T(8,128)(2,1)S(1)}, u32[]{:S(2)}, u32[]{:S(2)}) collective-permute-start(bf16[512,640]{1,0:T(8,128)(2,1)S(1)} %collective-permute-done.2.refs_0_), channel_id=1, source_target_pairs={{0,16},{8,24},{16,32},{24,40},{32,48},{40,56},{48,64},{56,72},{64,... | collective-permute-start | bytes 1966088 | tf_op jit(solution)/shard_map/ppermute | solution.py:233
  29.0 26.4 %collective-permute-start.10 = (bf16[512,640]{1,0:T(8,128)(2,1)S(1)}, bf16[512,640]{1,0:T(8,128)(2,1)S(1)}, u32[]{:S(2)}, u32[]{:S(2)}) collective-permute-start(bf16[512,640]{1,0:T(8,128)(2,1)S(1)} %collective-permute-done.6.refs_3_), channel_id=1, source_target_pairs={{16,0},{24,8},{32,16},{40,24},{48,32},{56,40},{64,48},{72,56},{80,... | collective-permute-start | bytes 1966088 | tf_op jit(solution)/shard_map/ppermute | solution.py:235
  36.3 26.6 %collective-permute-start.8 = (bf16[512,640]{1,0:T(8,128)(2,1)S(1)}, bf16[512,640]{1,0:T(8,128)(2,1)S(1)}, u32[]{:S(2)}, u32[]{:S(2)}) collective-permute-start(bf16[512,640]{1,0:T(8,128)(2,1)S(1)} %collective-permute-done.4.refs_1_), channel_id=1, source_target_pairs={{16,0},{24,8},{32,16},{40,24},{48,32},{56,40},{64,48},{72,56},{80,... | collective-permute-start | bytes 1966088 | tf_op jit(solution)/shard_map/ppermute | solution.py:233
  36.3 23.3 %collective-permute-start.9 = (bf16[512,640]{1,0:T(8,128)(2,1)}, bf16[512,640]{1,0:T(8,128)(2,1)S(1)}, u32[]{:S(2)}, u32[]{:S(2)}) collective-permute-start(bf16[512,640]{1,0:T(8,128)(2,1)} %collective-permute-done.5.refs_2_), channel_id=1, source_target_pairs={{0,16},{8,24},{16,32},{24,40},{32,48},{40,56},{48,64},{56,72},{64,... | collective-permute-start | bytes 1966088 | tf_op jit(solution)/shard_map/ppermute | solution.py:234
  62.9 17.7 %collective-permute-start.7 = (bf16[512,640]{1,0:T(8,128)(2,1)S(1)}, bf16[512,640]{1,0:T(8,128)(2,1)S(1)}, u32[]{:S(2)}, u32[]{:S(2)}) collective-permute-start(bf16[512,640]{1,0:T(8,128)(2,1)S(1)} %collective-permute-done.3.refs_0_), channel_id=1, source_target_pairs={{0,16},{8,24},{16,32},{24,40},{32,48},{40,56},{48,64},{56,72},{64,... | collective-permute-start | bytes 1966088 | tf_op jit(solution)/shard_map/ppermute | solution.py:233
  63.2 18.9 %collective-permute-start.12 = (bf16[512,640]{1,0:T(8,128)(2,1)S(1)}, bf16[512,640]{1,0:T(8,128)(2,1)S(1)}, u32[]{:S(2)}, u32[]{:S(2)}) collective-permute-start(bf16[512,640]{1,0:T(8,128)(2,1)S(1)} %collective-permute-done.8.refs_1_), channel_id=1, source_target_pairs={{16,0},{24,8},{32,16},{40,24},{48,32},{56,40},{64,48},{72,56},{80,... | collective-permute-start | bytes 1966088 | tf_op jit(solution)/shard_map/ppermute | solution.py:233
  64.9 29.7 %collective-permute-start.14 = (bf16[512,640]{1,0:T(8,128)(2,1)S(1)}, bf16[512,640]{1,0:T(8,128)(2,1)S(1)}, u32[]{:S(2)}, u32[]{:S(2)}) collective-permute-start(bf16[512,640]{1,0:T(8,128)(2,1)S(1)} %collective-permute-done.9.refs_2_), channel_id=1, source_target_pairs={{0,16},{8,24},{16,32},{24,40},{32,48},{40,56},{48,64},{56,72},{64,... | collective-permute-start | bytes 1966088 | tf_op jit(solution)/shard_map/ppermute | solution.py:234
  66.4 29.7 %collective-permute-start.15 = (bf16[512,640]{1,0:T(8,128)(2,1)S(1)}, bf16[512,640]{1,0:T(8,128)(2,1)S(1)}, u32[]{:S(2)}, u32[]{:S(2)}) collective-permute-start(bf16[512,640]{1,0:T(8,128)(2,1)S(1)} %collective-permute-done.10.refs_3_), channel_id=1, source_target_pairs={{16,0},{24,8},{32,16},{40,24},{48,32},{56,40},{64,48},{72,56},{80,... | collective-permute-start | bytes 1966088 | tf_op jit(solution)/shard_map/ppermute | solution.py:235
  80.5 25.7 %collective-permute-start.11 = (bf16[512,640]{1,0:T(8,128)(2,1)S(1)}, bf16[512,640]{1,0:T(8,128)(2,1)S(1)}, u32[]{:S(2)}, u32[]{:S(2)}) collective-permute-start(bf16[512,640]{1,0:T(8,128)(2,1)S(1)} %collective-permute-done.7.refs_0_), channel_id=1, source_target_pairs={{0,16},{8,24},{16,32},{24,40},{32,48},{40,56},{48,64},{56,72},{64,... | collective-permute-start | bytes 1966088 | tf_op jit(solution)/shard_map/ppermute | solution.py:238
  82.0 25.7 %collective-permute-start.13 = (bf16[512,640]{1,0:T(8,128)(2,1)S(1)}, bf16[512,640]{1,0:T(8,128)(2,1)S(1)}, u32[]{:S(2)}, u32[]{:S(2)}) collective-permute-start(bf16[512,640]{1,0:T(8,128)(2,1)S(1)} %collective-permute-done.12.refs_1_), channel_id=1, source_target_pairs={{16,0},{24,8},{32,16},{40,24},{48,32},{56,40},{64,48},{72,56},{80,... | collective-permute-start | bytes 1966088 | tf_op jit(solution)/shard_map/ppermute | solution.py:238
  103.7 6.8 %copy-start.2 = (f32[40,128,128]{2,1,0:T(8,128)}, f32[40,128,128]{2,1,0:T(8,128)S(1)}, u32[]{:S(2)}) copy-start(f32[40,128,128]{2,1,0:T(8,128)S(1)} %get-tuple-element.41.refs_2_) | copy-start | bytes 7864324
  110.5 32.2 %collective-permute-start.20 = (bf16[640,2560]{1,0:T(8,128)(2,1)}, bf16[640,2560]{1,0:T(8,128)(2,1)}, u32[]{:S(2)}, u32[]{:S(2)}) collective-permute-start(bf16[640,2560]{1,0:T(8,128)(2,1)} %collective-permute-done.19), channel_id=1, source_target_pairs={{0,128},{128,0},{1,129},{129,1},{2,130},{130,2},{3,131},{131,3},{4... | collective-permute-start | bytes 9830408 | tf_op jit(solution)/shard_map/ppermute | solution.py:157
  110.6 20.4 %collective-permute-start.16 = (bf16[20,128,128]{2,1,0:T(8,128)(2,1)S(1)}, bf16[20,128,128]{2,1,0:T(8,128)(2,1)}, u32[]{:S(2)}, u32[]{:S(2)}) collective-permute-start(bf16[20,128,128]{2,1,0:T(8,128)(2,1)S(1)} %get-tuple-element.47), channel_id=1, source_target_pairs={{0,8},{8,0},{16,24},{24,16},{32,40},{40,32},{48,56},{56,48},{64,72... | collective-permute-start | bytes 1966088 | tf_op jit(solution)/shard_map/ppermute | solution.py:251
  112.0 19.0 %collective-permute-start.17 = (f32[20,8,128]{2,1,0:T(8,128)S(1)}, f32[20,8,128]{2,1,0:T(8,128)S(1)}, u32[]{:S(2)}, u32[]{:S(2)}) collective-permute-start(f32[20,8,128]{2,1,0:T(8,128)S(1)} %get-tuple-element.43), channel_id=1, source_target_pairs={{0,8},{8,0},{16,24},{24,16},{32,40},{40,32},{48,56},{56,48},{64,72... | collective-permute-start | bytes 245768 | tf_op jit(solution)/shard_map/ppermute | solution.py:251
  114.2 1.7 %copy-start.3 = (f32[40,128,128]{2,1,0:T(8,128)S(1)}, f32[40,128,128]{2,1,0:T(8,128)}, u32[]{:S(2)}) copy-start(f32[40,128,128]{2,1,0:T(8,128)} %copy-done.2) | copy-start | bytes 7864324
  131.0 4.0 %copy-start.5 = (bf16[640,2560]{1,0:T(8,128)(2,1)S(1)}, bf16[640,2560]{1,0:T(8,128)(2,1)}, u32[]{:S(2)}) copy-start(bf16[640,2560]{1,0:T(8,128)(2,1)} %copy-done.4) | copy-start | bytes 9830404
  131.1 5.2 %slice-start = ((s8[6553600]{0:T(1024)(128)(4,1)}), s8[2359296]{0:T(1024)(128)(4,1)S(1)}, s32[]{:S(2)}) async-start(s8[6553600]{0:T(1024)(128)(4,1)} %bitcast.34), calls=%async_computation | async-start | bytes 4718592
  132.7 3.6 %slice-start.1 = ((s8[6553600]{0:T(1024)(128)(4,1)}), s8[4194304]{0:T(1024)(128)(4,1)S(1)}, s32[]{:S(2)}) async-start(s8[6553600]{0:T(1024)(128)(4,1)} %bitcast.34), calls=%async_computation.1 | async-start | bytes 8388608
  132.8 7.2 %collective-permute-start.18 = (bf16[128,640]{1,0:T(8,128)(2,1)S(1)}, bf16[128,640]{1,0:T(8,128)(2,1)S(1)}, u32[]{:S(2)}, u32[]{:S(2)}) collective-permute-start(bf16[128,640]{1,0:T(8,128)(2,1)S(1)} %pad_maximum_fusion.1), channel_id=1, source_target_pairs={{0,4},{1,5},{2,6},{3,7},{4,0},{5,1},{6,2},{7,3},{8,12},{9,13},{10,... | collective-permute-start | bytes 491528 | tf_op jit(solution)/shard_map/ppermute | solution.py:153
  133.4 12.0 %collective-permute-start.21 = (bf16[128,640]{1,0:T(8,128)(2,1)S(1)}, bf16[128,640]{1,0:T(8,128)(2,1)S(1)}, u32[]{:S(2)}, u32[]{:S(2)}) collective-permute-start(bf16[128,640]{1,0:T(8,128)(2,1)S(1)} %pad_maximum_fusion.2), channel_id=1, source_target_pairs={{0,4},{1,5},{2,6},{3,7},{4,0},{5,1},{6,2},{7,3},{8,12},{9,13},{10,... | collective-permute-start | bytes 491528 | tf_op jit(solution)/shard_map/ppermute | solution.py:153
  145.4 7.5 %collective-permute-start.22 = (bf16[64,2560]{1,0:T(8,128)(2,1)S(1)}, bf16[64,2560]{1,0:T(8,128)(2,1)S(1)}, u32[]{:S(2)}, u32[]{:S(2)}) collective-permute-start(bf16[64,2560]{1,0:T(8,128)(2,1)S(1)} %split.63), channel_id=1, source_target_pairs={{0,1},{1,2},{2,3},{3,0},{4,5},{5,6},{6,7},{7,4},{8,9},{9,10},{10,1... | collective-permute-start | bytes 983048 | tf_op jit(solution)/shard_map/ppermute | solution.py:184
  145.7 8.9 %collective-permute-start.25 = (bf16[64,2560]{1,0:T(8,128)(2,1)S(1)}, bf16[64,2560]{1,0:T(8,128)(2,1)S(1)}, u32[]{:S(2)}, u32[]{:S(2)}) collective-permute-start(bf16[64,2560]{1,0:T(8,128)(2,1)S(1)} %split.62), channel_id=1, source_target_pairs={{0,3},{1,0},{2,1},{3,2},{4,7},{5,4},{6,5},{7,6},{8,11},{9,8},{10,9... | collective-permute-start | bytes 983048 | tf_op jit(solution)/shard_map/ppermute | solution.py:184
  153.0 8.6 %collective-permute-start.23 = (bf16[64,2560]{1,0:T(8,128)(2,1)S(1)}, bf16[64,2560]{1,0:T(8,128)(2,1)S(1)}, u32[]{:S(2)}, u32[]{:S(2)}) collective-permute-start(bf16[64,2560]{1,0:T(8,128)(2,1)S(1)} %fusion.7), channel_id=1, source_target_pairs={{0,1},{1,2},{2,3},{3,0},{4,5},{5,6},{6,7},{7,4},{8,9},{9,10},{10,1... | collective-permute-start | bytes 983048 | tf_op jit(solution)/shard_map/ppermute | solution.py:184
  154.7 8.7 %collective-permute-start.26 = (bf16[64,2560]{1,0:T(8,128)(2,1)S(1)}, bf16[64,2560]{1,0:T(8,128)(2,1)S(1)}, u32[]{:S(2)}, u32[]{:S(2)}) collective-permute-start(bf16[64,2560]{1,0:T(8,128)(2,1)S(1)} %fusion.4), channel_id=1, source_target_pairs={{0,3},{1,0},{2,1},{3,2},{4,7},{5,4},{6,5},{7,6},{8,11},{9,8},{10,9... | collective-permute-start | bytes 983048 | tf_op jit(solution)/shard_map/ppermute | solution.py:184
  161.6 7.2 %collective-permute-start.24 = (bf16[64,2560]{1,0:T(8,128)(2,1)S(1)}, bf16[64,2560]{1,0:T(8,128)(2,1)S(1)}, u32[]{:S(2)}, u32[]{:S(2)}) collective-permute-start(bf16[64,2560]{1,0:T(8,128)(2,1)S(1)} %fusion.6), channel_id=1, source_target_pairs={{0,1},{1,2},{2,3},{3,0},{4,5},{5,6},{6,7},{7,4},{8,9},{9,10},{10,1... | collective-permute-start | bytes 983048 | tf_op jit(solution)/shard_map/ppermute | solution.py:184
  163.4 8.4 %collective-permute-start.27 = (bf16[64,2560]{1,0:T(8,128)(2,1)S(1)}, bf16[64,2560]{1,0:T(8,128)(2,1)S(1)}, u32[]{:S(2)}, u32[]{:S(2)}) collective-permute-start(bf16[64,2560]{1,0:T(8,128)(2,1)S(1)} %fusion.3), channel_id=1, source_target_pairs={{0,3},{1,0},{2,1},{3,2},{4,7},{5,4},{6,5},{7,6},{8,11},{9,8},{10,9... | collective-permute-start | bytes 983048 | tf_op jit(solution)/shard_map/ppermute | solution.py:184
